TPU v7x, 512 devices: a whole 4x4x16 slice. The times are simulated.
512 devices in a mesh: dp: 16 (over y, x), seq: 32 (over z, core).
Axes of the slice: x: 4, y: 4, z: 16, core: 2. Of those that a mesh axis runs over, the one named last changes fastest.
Arguments:
- queries: bfloat16 [65536, 32, 128], P(('dp', 'seq')), parts along dimension 0, may hold values from -6 to 6
- attn_keys: bfloat16 [65536, 32, 128], P(('dp', 'seq')), parts along dimension 0, may hold values from -6 to 6
- attn_values: bfloat16 [65536, 32, 128], P(('dp', 'seq')), parts along dimension 0, may hold values from -6 to 6
- splats: bfloat16 [16384, 32, 128], P(('dp', 'seq')), parts along dimension 0, may hold values from -6 to 6
- splat_dest: int32 [16384], P(('dp', 'seq')), parts along dimension 0, may hold values from 0 to 31, as said below
- splat_sub: int32 [16384], P(('dp', 'seq')), parts along dimension 0, may hold values from 0 to 3
- splat_weight: bfloat16 [16384], P(('dp', 'seq')), parts along dimension 0, may hold values from 0.049804688 to 0.5
- cond_weight: bfloat16 [128, 32, 128], P(None, 'seq'), may hold values from -0.5 to 0.5
Outputs:
- attn_out: bfloat16 [65536, 32, 128], P(('dp', 'seq')), parts along dimension 0
There are 16 independent parts, one for each index of `dp`. A program takes and returns all parts, laid end to end along the dimension named above; an argument that names none is the same for every part. Nothing has to cross between parts.
Inputs may be any that keep to these rules, and one draw needn't show every extreme that they name: `splat_dest`: of the splat blocks that one device holds, at most 2 name the same device; one device, drawn afresh, is named by exactly 2 splat blocks of every device.
All inputs are finite; a program needn't handle non-finite values.
Results may differ from a plain program's by a relative error of at most 0.0059.
Values may be sent and summed in bfloat16 or wider, within the bound.
No kernel may reach another device: no remote copies, remote signals or barrier semaphores. Data moves between devices by JAX's collectives and lax.ppermute only.
A program may use at most 64 MiB of HBM per device.

v0:
```python
import jax
import jax.numpy as jnp
from jax import lax
from jax.sharding import PartitionSpec as P


def normalize(block_sums, block_weights, feats):
    denom = jnp.maximum(block_weights, 1.0)
    return (block_sums / denom[:, None]).reshape(-1, feats).astype(jnp.bfloat16)


def on_device(
    queries, attn_keys, attn_values, splats, splat_dest, splat_sub, splat_weight, cond_weight
):
    tok_rows, head_count, head_size = queries.shape
    peer_count = lax.axis_size("seq")
    spl_rows, blk_rows, feats = splats.shape
    own_blocks = tok_rows // blk_rows
    seq_len = tok_rows * peer_count
    capacity = max(2, (2 * spl_rows + peer_count - 1) // peer_count)
    splat_rows = splats.reshape(spl_rows, blk_rows * feats)
    dest_onehot = (splat_dest[:, None] == jnp.arange(peer_count, dtype=jnp.int32)[None, :]).astype(
        jnp.int32
    )
    rank_within = jnp.sum(jnp.cumsum(dest_onehot, axis=0) * dest_onehot, axis=1) - 1
    slot_index = splat_dest * capacity + rank_within
    slot_ids = jnp.arange(peer_count * capacity, dtype=jnp.int32)
    placement = (slot_index[None, :] == slot_ids[:, None]).astype(jnp.bfloat16)
    sub_weights = jnp.where(
        splat_sub[:, None] == jnp.arange(own_blocks, dtype=jnp.int32)[None, :],
        splat_weight[:, None],
        jnp.zeros((), jnp.bfloat16),
    )
    slot_data = jnp.dot(placement, splat_rows, preferred_element_type=jnp.float32).astype(
        jnp.bfloat16
    )
    slot_keys = jnp.dot(placement, sub_weights, preferred_element_type=jnp.float32).astype(
        jnp.bfloat16
    )
    slot_data = slot_data.reshape(peer_count, capacity, blk_rows * feats)
    slot_keys = slot_keys.reshape(peer_count, capacity, own_blocks)
    arrived_data, arrived_keys = (
        lax.all_to_all(slot_data, "seq", split_axis=0, concat_axis=0, tiled=True),
        lax.all_to_all(slot_keys, "seq", split_axis=0, concat_axis=0, tiled=True),
    )
    arrived_data = arrived_data.reshape(peer_count * capacity, blk_rows * feats)
    arrived_keys = arrived_keys.reshape(peer_count * capacity, own_blocks)
    own_sum = lax.dot_general(
        arrived_keys, arrived_data, (((0,), (0,)), ((), ())), preferred_element_type=jnp.float32
    )
    own_weight = jnp.sum(arrived_keys.astype(jnp.float32), axis=0)
    own_cond = normalize(own_sum, own_weight, feats)
    cond_mix = jnp.einsum(
        "tc,chd->thd",
        own_cond,
        lax.all_gather(cond_weight, "seq", axis=1, tiled=True),
        preferred_element_type=jnp.float32,
    )
    carried = (attn_values.astype(jnp.float32) + cond_mix).astype(jnp.bfloat16)
    query_heads, key_heads, value_heads = (
        lax.all_to_all(queries, "seq", split_axis=1, concat_axis=0, tiled=True),
        lax.all_to_all(attn_keys, "seq", split_axis=1, concat_axis=0, tiled=True),
        lax.all_to_all(carried, "seq", split_axis=1, concat_axis=0, tiled=True),
    )
    heads_dev = query_heads.shape[1]
    score_scale = float(head_size) ** (-0.5)
    block_count = seq_len // 512
    query_blocks = query_heads.reshape(block_count, seq_len // block_count, heads_dev, head_size)

    def attend(query_block):
        scores = (
            jnp.einsum("qhd,khd->hqk", query_block, key_heads, preferred_element_type=jnp.float32)
            * score_scale
        )
        probs = jax.nn.softmax(scores, axis=-1).astype(jnp.bfloat16)
        return jnp.einsum(
            "hqk,khd->qhd", probs, value_heads, preferred_element_type=jnp.float32
        ).astype(jnp.bfloat16)

    head_output = lax.map(attend, query_blocks).reshape(seq_len, heads_dev, head_size)
    return lax.all_to_all(head_output, "seq", split_axis=0, concat_axis=1, tiled=True)


def solution(mesh):
    in_specs = (
        P(("dp", "seq"), None, None),
        P(("dp", "seq"), None, None),
        P(("dp", "seq"), None, None),
        P(("dp", "seq"), None, None),
        P(("dp", "seq")),
        P(("dp", "seq")),
        P(("dp", "seq")),
        P(None, "seq", None),
    )
    out_specs = P(("dp", "seq"), None, None)
    return jax.shard_map(
        on_device, mesh=mesh, in_specs=in_specs, out_specs=out_specs, check_vma=False
    )
```

profile of v0, /device:TPU:1, one launch (start us, length us, event | category | flops | bytes accessed | tf_op | source)
XLA Modules:
  0.0 411.8 jit_solution(839589104765940426)
XLA Ops:
  10.5 16.7 %all-to-all-start.2 = ((bf16[32,2,4]{2,1,0:T(2,128)(2,1)}), bf16[32,2,4]{2,1,0:T(2,128)(2,1)S(1)}, u32[]{:S(2)}, u32[]{:S(2)}) async-start(bf16[32,2,4]{2,1,0:T(2,128)(2,1)} %bitcast.14), calls=%async_computation.2 | async-start | bytes 32768 | tf_op jit(solution)/shard_map/all_to_all | solution.py:44
  29.7 9.3 %all-to-all-done.2 = bf16[32,2,4]{2,1,0:T(2,128)(2,1)S(1)} async-done(((bf16[32,2,4]{2,1,0:T(2,128)(2,1)}), bf16[32,2,4]{2,1,0:T(2,128)(2,1)S(1)}, u32[]{:S(2)}, u32[]{:S(2)}) %all-to-all-start.2) | async-done | bytes 544 | tf_op jit(solution)/shard_map/all_to_all | solution.py:44
  39.0 4.5 %all-to-all-start.3 = ((bf16[32,2,4096]{2,1,0:T(2,128)(2,1)}), bf16[32,2,4096]{2,1,0:T(2,128)(2,1)S(1)}, u32[]{:S(2)}, u32[]{:S(2)}) async-start(bf16[32,2,4096]{2,1,0:T(2,128)(2,1)} %reshape.60), calls=%async_computation.3 | async-start | bytes 1048576 | tf_op jit(solution)/shard_map/all_to_all | solution.py:43
  43.5 2.6 copy.31
  46.1 30.9 %all-to-all-done.3 = bf16[32,2,4096]{2,1,0:T(2,128)(2,1)S(1)} async-done(((bf16[32,2,4096]{2,1,0:T(2,128)(2,1)}), bf16[32,2,4096]{2,1,0:T(2,128)(2,1)S(1)}, u32[]{:S(2)}, u32[]{:S(2)}) %all-to-all-start.3) | async-done | bytes 524320 | tf_op jit(solution)/shard_map/all_to_all | solution.py:43
  77.8 4.4 %all-to-all-start = ((bf16[128,32,128]{2,0,1:T(8,128)(2,1)}), bf16[128,32,128]{2,0,1:T(8,128)(2,1)S(1)}, u32[]{:S(2)}, u32[]{:S(2)}) async-start(bf16[128,32,128]{2,0,1:T(8,128)(2,1)} %copy.31), calls=%async_computation | async-start | bytes 2097152 | tf_op jit(solution)/shard_map/all_to_all | solution.py:61
  82.2 2.6 copy.32
  84.8 53.2 %all-to-all-done = bf16[128,32,128]{2,0,1:T(8,128)(2,1)S(1)} async-done(((bf16[128,32,128]{2,0,1:T(8,128)(2,1)}), bf16[128,32,128]{2,0,1:T(8,128)(2,1)S(1)}, u32[]{:S(2)}, u32[]{:S(2)}) %all-to-all-start) | async-done | bytes 1048608 | tf_op jit(solution)/shard_map/all_to_all | solution.py:61
  138.0 4.6 %all-to-all-start.1 = ((bf16[128,32,128]{2,0,1:T(8,128)(2,1)}), bf16[128,32,128]{2,0,1:T(8,128)(2,1)S(1)}, u32[]{:S(2)}, u32[]{:S(2)}) async-start(bf16[128,32,128]{2,0,1:T(8,128)(2,1)} %copy.32), calls=%async_computation.1 | async-start | bytes 2097152 | tf_op jit(solution)/shard_map/all_to_all | solution.py:62
  144.9 80.9 %all-gather.2.cloned.1.call-done = bf16[128,32,128]{2,0,1:T(8,128)(2,1)} async-done(((bf16[128,1,128]{2,0,1:T(8,128)(2,1)}), bf16[128,32,128]{2,0,1:T(8,128)(2,1)}) %all-gather.2.cloned.1.call-update) | async-done | bytes 1048592 | tf_op jit(solution)/shard_map/all_gather | solution.py:56
  225.9 2.8 add_convert_fusion
  228.6 9.2 %all-to-all-start.4 = ((bf16[128,32,128]{2,0,1:T(8,128)(2,1)}), bf16[128,32,128]{2,0,1:T(8,128)(2,1)}, u32[]{:S(2)}, u32[]{:S(2)}) async-start(bf16[128,32,128]{2,0,1:T(8,128)(2,1)} %add_convert_fusion), calls=%async_computation.4 | async-start | bytes 2097152 | tf_op jit(solution)/shard_map/all_to_all | solution.py:63
  237.8 55.8 %all-to-all-done.4 = bf16[128,32,128]{2,0,1:T(8,128)(2,1)} async-done(((bf16[128,32,128]{2,0,1:T(8,128)(2,1)}), bf16[128,32,128]{2,0,1:T(8,128)(2,1)}, u32[]{:S(2)}, u32[]{:S(2)}) %all-to-all-start.4) | async-done | bytes 1048608 | tf_op jit(solution)/shard_map/all_to_all | solution.py:63
  293.6 47.3 %while.10 = (s32[]{:T(128)}, bf16[8,512,1,128]{3,1,2,0:T(8,128)(2,1)S(1)}, bf16[8,512,1,128]{3,1,2,0:T(8,128)(2,1)S(1)}, bf16[4096,1,128]{2,0,1:T(8,128)(2,1)S(1)}, bf16[4096,1,128]{2,0,1:T(8,128)(2,1)}, /*index=5*/s32[]{:T(128)}) while((s32[]{:T(128)}, bf16[8,512,1,128]{3,1,2,0:T(8,128)(2,1)S(1)}, bf16[8,512,1,128]{3,1,2,0:T(8,128)(2,1)S(1)}, ...), condition=%wide.region_6.7_spmd, body=%wide.region_3.6_spmd.sunk | while | flops 1092680704 | bytes 27535436 | solution.py:80
  294.9 1.5 fusion.33
  296.4 3.1 fusion.34
  300.8 1.5 fusion.33
  302.3 3.1 fusion.34
  306.7 1.5 fusion.33
  308.2 3.1 fusion.34
  312.6 1.5 fusion.33
  314.1 3.1 fusion.34
  318.6 1.5 fusion.33
  320.1 3.1 fusion.34
  324.5 1.5 fusion.33
  326.0 3.1 fusion.34
  330.4 1.5 fusion.33
  331.9 3.1 fusion.34
  336.3 1.5 fusion.33
  337.8 3.1 fusion.34
  343.1 59.0 %all_to_all.79 = bf16[32,2,8192]{2,1,0:T(2,128)(2,1)S(1)} all-to-all(bf16[32,2,8192]{2,1,0:T(2,128)(2,1)S(1)} %reshape.65), channel_id=1, replica_groups=mesh['dp'=16,'seq'=32] {'seq'}, dimensions={0} | all-to-all | bytes 2097152 | tf_op jit(solution)/shard_map/all_to_all | solution.py:81
  403.3 1.6 copy.39
  (33 shorter events, 23.5 us)
Async XLA Ops:
  6.5 219.3 %copy-start = (bf16[128,32,128]{2,1,0:T(8,128)(2,1)S(1)}, bf16[128,32,128]{2,1,0:T(8,128)(2,1)}, u32[]{:S(2)}) copy-start(bf16[128,32,128]{2,1,0:T(8,128)(2,1)} %param.12) | copy-start | bytes 3145732
  10.5 28.5 %all-to-all-start.2 = ((bf16[32,2,4]{2,1,0:T(2,128)(2,1)}), bf16[32,2,4]{2,1,0:T(2,128)(2,1)S(1)}, u32[]{:S(2)}, u32[]{:S(2)}) async-start(bf16[32,2,4]{2,1,0:T(2,128)(2,1)} %bitcast.14), calls=%async_computation.2 | async-start | bytes 32768 | tf_op jit(solution)/shard_map/all_to_all | solution.py:44
  39.0 38.0 %all-to-all-start.3 = ((bf16[32,2,4096]{2,1,0:T(2,128)(2,1)}), bf16[32,2,4096]{2,1,0:T(2,128)(2,1)S(1)}, u32[]{:S(2)}, u32[]{:S(2)}) async-start(bf16[32,2,4096]{2,1,0:T(2,128)(2,1)} %reshape.60), calls=%async_computation.3 | async-start | bytes 1048576 | tf_op jit(solution)/shard_map/all_to_all | solution.py:43
  77.0 0.8 copy-start.1
  77.8 60.2 %all-to-all-start = ((bf16[128,32,128]{2,0,1:T(8,128)(2,1)}), bf16[128,32,128]{2,0,1:T(8,128)(2,1)S(1)}, u32[]{:S(2)}, u32[]{:S(2)}) async-start(bf16[128,32,128]{2,0,1:T(8,128)(2,1)} %copy.31), calls=%async_computation | async-start | bytes 2097152 | tf_op jit(solution)/shard_map/all_to_all | solution.py:61
  138.0 90.6 %all-to-all-start.1 = ((bf16[128,32,128]{2,0,1:T(8,128)(2,1)}), bf16[128,32,128]{2,0,1:T(8,128)(2,1)S(1)}, u32[]{:S(2)}, u32[]{:S(2)}) async-start(bf16[128,32,128]{2,0,1:T(8,128)(2,1)} %copy.32), calls=%async_computation.1 | async-start | bytes 2097152 | tf_op jit(solution)/shard_map/all_to_all | solution.py:62
  142.7 83.2 %all-gather.2.cloned.1.call-start = ((), (), s32[]{:S(2)}) async-start(), calls=%async_computation.6 | async-start | bytes 1081344 | tf_op jit(solution)/shard_map/all_gather | solution.py:56
  228.6 64.9 %all-to-all-start.4 = ((bf16[128,32,128]{2,0,1:T(8,128)(2,1)}), bf16[128,32,128]{2,0,1:T(8,128)(2,1)}, u32[]{:S(2)}, u32[]{:S(2)}) async-start(bf16[128,32,128]{2,0,1:T(8,128)(2,1)} %add_convert_fusion), calls=%async_computation.4 | async-start | bytes 2097152 | tf_op jit(solution)/shard_map/all_to_all | solution.py:63
Sparse Core Ops, SparseCore 0:
  145.6 80.2 all-gather.1
where the time goes:
time: 413 us; the launch traced here: 412 us
  waiting for transfers between devices  231 us (56%)
  blocking collectives  59 us (14%)
  matrix products  41.5 us (10%)
  starting transfers between devices  39.4 us (10%)
  other arithmetic  15.9 us (4%)
  between operations  13.5 us (3%)
  local copies, waits for them, and re-layouts  11.5 us (3%)
    all_gather x1, waiting for transfers between devices, on_device(): lax.all_gather(cond_weight, 'seq', axis=1, tiled=True)  80.9 us
    all_to_all x1, blocking collectives, on_device(): lax.all_to_all(head_output, 'seq', split_axis=0, concat_axis=1, tiled=True)  59 us
    all_to_all x1, waiting for transfers between devices, on_device(): lax.all_to_all(carried, 'seq', split_axis=1, concat_axis=0, tiled=True)  55.8 us
    all_to_all x1, waiting for transfers between devices, on_device(): lax.all_to_all(queries, 'seq', split_axis=1, concat_axis=0, tiled=True)  53.2 us
    all_to_all x1, waiting for transfers between devices, on_device(): lax.all_to_all(slot_data, 'seq', split_axis=0, concat_axis=0, tiled=True)  30.9 us
    dot_general x8, matrix products, attend(): jnp.einsum('hqk,khd->qhd', probs, value_heads, preferred_element_type=jnp...  24.4 us
    all_to_all x1, starting transfers between devices, on_device(): lax.all_to_all(slot_keys, 'seq', split_axis=0, concat_axis=0, tiled=True)  16.7 us
    reduce_sum x8, other arithmetic, attend(): probs = jax.nn.softmax(scores, axis=-1).astype(jnp.bfloat16)  12.1 us
  transfers between devices with their start and end apart: 6, of which 5 were waited for; matrix products, arithmetic and copies ran while one was open for 3% of the time, Pallas kernels for 0%

commit v1 on v0

v1 whole, which is shorter than its diff:
```python
import math

import jax
import jax.numpy as jnp
from jax import lax
from jax.experimental import pallas as pl
from jax.experimental.pallas import tpu as pltpu
from jax.sharding import PartitionSpec as P


def attention(recv, mix, sub_rows):
    peers, _, rows, hd = recv.shape
    tokens = peers * rows
    tile = 1024
    to_exp2 = hd**-0.5 * math.log2(math.e)

    def kernel(q_ref, k_ref, v_ref, mix_ref, o_ref, v_ext):
        @pl.when(pl.program_id(0) == 0)
        def _():
            values = v_ref[...].reshape(tokens, hd).astype(jnp.float32)
            v_ext[:, :hd] = (values + mix_ref[...]).astype(jnp.bfloat16)
            v_ext[:, hd:] = jnp.ones((tokens, hd), jnp.bfloat16)

        keys = k_ref[...].reshape(tokens, hd)
        for at in range(tile // sub_rows):
            q = q_ref[(at * sub_rows) // rows, 0, pl.ds((at * sub_rows) % rows, sub_rows)]
            scores = lax.dot_general(
                q, keys, (((1,), (1,)), ((), ())), preferred_element_type=jnp.float32
            )
            top = jnp.max(scores, axis=1, keepdims=True)
            probs = jnp.exp2((scores - top) * to_exp2).astype(jnp.bfloat16)
            both = jnp.dot(probs, v_ext[...], preferred_element_type=jnp.float32)
            o_ref[pl.ds(at * sub_rows, sub_rows)] = (both[:, :hd] / both[:, hd:]).astype(
                jnp.bfloat16
            )

    def whole(part):
        return pl.BlockSpec((peers, 1, rows, hd), lambda i: (0, part, 0, 0))

    return pl.pallas_call(
        kernel,
        name="attend",
        grid=(tokens // tile,),
        in_specs=[
            pl.BlockSpec((tile // rows, 1, rows, hd), lambda i: (i, 0, 0, 0)),
            whole(1),
            whole(2),
            pl.BlockSpec((tokens, hd), lambda i: (0, 0)),
        ],
        out_specs=pl.BlockSpec((tile, hd), lambda i: (i, 0)),
        out_shape=jax.ShapeDtypeStruct((tokens, hd), jnp.bfloat16),
        scratch_shapes=[pltpu.VMEM((tokens, 2 * hd), jnp.bfloat16)],
        compiler_params=pltpu.CompilerParams(vmem_limit_bytes=48 << 20),
    )(recv, recv, recv, mix)


def gathered_condition(splats, splat_dest, splat_sub, splat_weight, own_blocks):
    peers = lax.axis_size("seq")
    chips = peers // 2
    count, blk_rows, feats = splats.shape
    blocks = peers * own_blocks
    half = blk_rows // 2
    core = lax.axis_index("seq") % 2
    target = splat_dest * own_blocks + splat_sub
    table = jnp.where(
        target[None, :] == jnp.arange(blocks, dtype=jnp.int32)[:, None],
        splat_weight[None, :],
        jnp.zeros((), jnp.bfloat16),
    )
    halves = splats.reshape(count, 2, half * feats)
    mine = lax.dynamic_index_in_dim(halves, core, 1, keepdims=False)
    other = lax.dynamic_index_in_dim(halves, 1 - core, 1, keepdims=False)
    swap = [(d, d ^ 1) for d in range(peers)]
    arrived = lax.ppermute(jnp.concatenate([other, table.T], axis=1), "seq", swap)
    rows = jnp.concatenate([mine, arrived[:, : half * feats]], axis=0)
    both_table = jnp.concatenate([table, arrived[:, half * feats :].T], axis=1)
    sums = jnp.dot(both_table, rows, preferred_element_type=jnp.float32)
    weights = jnp.sum(both_table.astype(jnp.float32), axis=1, keepdims=True)
    per_chip = 2 * own_blocks
    partial = jnp.concatenate([sums, jnp.broadcast_to(weights, (blocks, 2 * feats))], axis=1)
    same_core = [[2 * z + c for z in range(chips)] for c in range(2)]
    total = lax.psum_scatter(
        partial, "seq", scatter_dimension=0, tiled=True, axis_index_groups=same_core
    )
    denom = jnp.maximum(total[:, half * feats : half * feats + 1], 1.0)
    cond = (total[:, : half * feats] / denom).astype(jnp.bfloat16)
    cond = cond.reshape(per_chip * half, feats)
    everyone = lax.all_gather(cond, "seq", axis=0, tiled=True)
    everyone = everyone.reshape(chips, 2, per_chip, half, feats).transpose(0, 2, 1, 3, 4)
    return everyone.reshape(blocks * blk_rows, feats)


def on_device(
    queries, attn_keys, attn_values, splats, splat_dest, splat_sub, splat_weight, cond_weight
):
    tok_rows, head_count, head_size = queries.shape
    peers = lax.axis_size("seq")
    own_blocks = tok_rows // splats.shape[1]
    send = jnp.concatenate(
        [x.transpose(1, 0, 2) for x in (queries, attn_keys, attn_values)], axis=1
    )
    recv = lax.all_to_all(send, "seq", split_axis=0, concat_axis=0, tiled=True)
    cond = gathered_condition(splats, splat_dest, splat_sub, splat_weight, own_blocks)
    mix = jnp.dot(cond, cond_weight[:, 0], preferred_element_type=jnp.float32)
    head_out = attention(recv.reshape(peers, 3, tok_rows, head_size), mix, 128)
    head_out = head_out.reshape(peers, tok_rows, head_size)
    arrived = lax.all_to_all(head_out, "seq", split_axis=0, concat_axis=0, tiled=True)
    return arrived.transpose(1, 0, 2)


def solution(mesh):
    in_specs = (
        P(("dp", "seq"), None, None),
        P(("dp", "seq"), None, None),
        P(("dp", "seq"), None, None),
        P(("dp", "seq"), None, None),
        P(("dp", "seq")),
        P(("dp", "seq")),
        P(("dp", "seq")),
        P(None, "seq", None),
    )
    out_specs = P(("dp", "seq"), None, None)
    return jax.shard_map(
        on_device, mesh=mesh, in_specs=in_specs, out_specs=out_specs, check_vma=False
    )
```

time: 413 us -> 330 us (0.80)
  matrix products: 41.5 us -> 0.73 us
  waiting for transfers between devices: 231 us -> 194 us
  Pallas kernels: 0 us -> 24.3 us
  starting transfers between devices: 39.4 us -> 19.2 us
  other arithmetic: 15.9 us -> 4.85 us
  blocking collectives: 59 us -> 63.9 us
    all_to_all x5 -> x1, waiting for transfers between devices: 149 us -> 0.01 us  [on_device(): recv = lax.all_to_all(send, 'seq', split_axis=0, concat_axis=0, tiled=True)]
    reduce_scatter x0 -> x1, waiting for transfers between devices: none -> 112 us  [gathered_condition(): lax.psum_scatter(partial, 'seq', scatter_dimension=0, tiled=True, axis_in...]
    dot_general x20 -> x2, matrix products: 41.5 us -> 0.73 us  [the longest x1 0.41 us: on_device(): mix = jnp.dot(cond, cond_weight[:, 0], preferred_element_type=jnp.float32)]
    pallas_call x0 -> x1, Pallas kernels: none -> 24.3 us  [attention(): pl.pallas_call(kernel, name='attend', grid=(tokens // tile,), in_specs=[p...]
    all_to_all x5 -> x1, starting transfers between devices: 39.4 us -> 16.9 us  [on_device(): recv = lax.all_to_all(send, 'seq', split_axis=0, concat_axis=0, tiled=True)]
    reduce_sum x10 -> x1, other arithmetic: 13 us -> 0.03 us  [gathered_condition(): weights = jnp.sum(both_table.astype(jnp.float32), axis=1, keepdims=True)]
    unnamed x9 -> x13, local copies, waits for them, and re-layouts: 7.48 us -> 1.82 us
    transpose x0 -> x4, local copies, waits for them, and re-layouts: none -> 5.44 us  [the longest x1 2.36 us: on_device(): x.transpose(1, 0, 2)]
  transfers between devices with their start and end apart: 6 -> 4, of which waited for: 5 -> 3; matrix products, arithmetic and copies ran while one was open for 3% -> 2% of each run, Pallas kernels for 0% -> 0%
where the time goes in v1:
time: 330 us
  waiting for transfers between devices  194 us (59%)
  blocking collectives  63.9 us (19%)
  Pallas kernels  24.3 us (7%)
  starting transfers between devices  19.2 us (6%)
  between operations  13.6 us (4%)
  local copies, waits for them, and re-layouts  8.6 us (3%)
  other arithmetic  4.85 us (1%)
    reduce_scatter x1, waiting for transfers between devices, gathered_condition(): lax.psum_scatter(partial, 'seq', scatter_dimension=0, tiled=True, axis_in...  112 us
    all_gather x1, waiting for transfers between devices, gathered_condition(): everyone = lax.all_gather(cond, 'seq', axis=0, tiled=True)  81.4 us
    all_to_all x1, blocking collectives, on_device(): lax.all_to_all(head_out, 'seq', split_axis=0, concat_axis=0, tiled=True)  63.9 us
    pallas_call x1, Pallas kernels, attention(): pl.pallas_call(kernel, name='attend', grid=(tokens // tile,), in_specs=[p...  24.3 us
    all_to_all x1, starting transfers between devices, on_device(): recv = lax.all_to_all(send, 'seq', split_axis=0, concat_axis=0, tiled=True)  16.9 us
  transfers between devices with their start and end apart: 4, of which 3 were waited for; matrix products, arithmetic and copies ran while one was open for 2% of the time, Pallas kernels for 0%

profile of v1, /device:TPU:1, one launch (start us, length us, event | category | flops | bytes accessed | tf_op | source)
XLA Modules:
  0.0 329.7 jit_solution(7825218284841648900)
XLA Ops:
  6.5 1.6 copy.28
  8.2 2.4 copy_bitcast_fusion
  10.5 1.8 pad_maximum_fusion
  12.4 16.9 %all-to-all-start = ((bf16[32,384,128]{2,1,0:T(8,128)(2,1)}), bf16[32,384,128]{2,1,0:T(8,128)(2,1)}, u32[]{:S(2)}, u32[]{:S(2)}) async-start(bf16[32,384,128]{2,1,0:T(8,128)(2,1)} %pad_maximum_fusion), calls=%async_computation | async-start | bytes 6291456 | tf_op jit(solution)/shard_map/all_to_all | solution.py:102
  29.3 0.0 reduce-scatter.2.cloned.1.call-start
  29.4 0.0 copy-done.1
  29.4 0.1 reshape.22
  29.5 0.5 constant_dynamic-slice_fusion
  30.0 0.1 copy.30
  30.1 0.0 copy-done.3
  30.2 0.1 fusion.8
  30.3 2.2 collective-permute-start
  32.5 0.1 copy.29
  32.6 0.1 fusion.7
  32.6 0.9 collective-permute-done
  33.6 0.3 fusion
  33.9 0.1 broadcast_in_dim.29
  34.0 1.1 pad_maximum_fusion.1
  35.1 0.0 reduce-scatter.2.cloned.1.call-update
  35.1 0.0 all-gather.2.cloned.1.call-start
  35.2 112.2 %reduce-scatter.2.cloned.1.call-done = f32[8,2304]{1,0:T(8,128)} async-done(((f32[128,2304]{1,0:T(8,128)}), f32[8,2304]{1,0:T(8,128)}) %reduce-scatter.2.cloned.1.call-update) | async-done | bytes 73744 | tf_op jit(solution)/shard_map/reduce_scatter | solution.py:82
  147.4 0.8 fusion.9
  148.2 0.9 fusion.4
  149.1 0.6 reshape.23
  149.7 0.0 all-gather.2.cloned.1.call-update
  149.8 81.4 %all-gather.2.cloned.1.call-done = bf16[4096,128]{1,0:T(8,128)(2,1)} async-done(((bf16[128,128]{1,0:T(8,128)(2,1)}), bf16[4096,128]{1,0:T(8,128)(2,1)}) %all-gather.2.cloned.1.call-update) | async-done | bytes 1048592 | tf_op jit(solution)/shard_map/all_gather | solution.py:88
  231.1 1.4 copy.19
  232.6 0.4 fusion.5.mix_ref
  233.0 0.0 all-to-all-done
  233.0 24.3 %attend.1 = bf16[4096,128]{1,0:T(8,128)(2,1)S(1)} custom-call(bf16[32,3,128,128]{3,2,1,0:T(8,128)(2,1)} %bitcast.3.q_ref.k_ref.v_ref, bf16[32,3,128,128]{3,2,1,0:T(8,128)(2,1)} %bitcast.3.q_ref.k_ref.v_ref, bf16[32,3,128,128]{3,2,1,0:T(8,128)(2,1)} %bitcast.3.q_ref.k_ref.v_ref, f32[4096,128]{1,0:T(8,128)S(1)} %fusion.5.mix_ref), custom_call_target="tpu_custom_call" | custom-call | tf_op jit(solution)/shard_map/attend/pallas_call | solution.py:40
  257.3 63.9 %all_to_all.10 = bf16[32,128,128]{2,1,0:T(8,128)(2,1)S(1)} all-to-all(bf16[32,128,128]{2,1,0:T(8,128)(2,1)S(1)} %bitcast.26), channel_id=1, replica_groups=mesh['dp'=16,'seq'=32] {'seq'}, dimensions={0} | all-to-all | bytes 2097152 | tf_op jit(solution)/shard_map/all_to_all | solution.py:107
  321.2 1.6 copy.20
  (13 shorter events, 0.1 us)
Async XLA Ops:
  6.5 226.0 %copy-start = (bf16[128,1,128]{2,0,1:T(8,128)(2,1)S(1)}, bf16[128,1,128]{2,0,1:T(8,128)(2,1)}, u32[]{:S(2)}) copy-start(bf16[128,1,128]{2,0,1:T(8,128)(2,1)} %param.15) | copy-start | bytes 98308
  12.4 17.0 %copy-start.1 = (bf16[32,32,128]{2,1,0:T(8,128)(2,1)S(1)}, bf16[32,32,128]{2,1,0:T(8,128)(2,1)}, u32[]{:S(2)}) copy-start(bf16[32,32,128]{2,1,0:T(8,128)(2,1)} %param.11) | copy-start | bytes 786436
  12.4 17.8 %copy-start.3 = (s32[32]{0:T(128)S(1)}, s32[32]{0:T(128)}, u32[]{:S(2)}) copy-start(s32[32]{0:T(128)} %param.13) | copy-start | bytes 388
  12.4 17.8 %copy-start.4 = (s32[32]{0:T(128)S(1)}, s32[32]{0:T(128)}, u32[]{:S(2)}) copy-start(s32[32]{0:T(128)} %param.12) | copy-start | bytes 388
  12.4 17.8 %copy-start.2 = (bf16[32]{0:T(256)(128)(2,1)S(1)}, bf16[32]{0:T(256)(128)(2,1)}, u32[]{:S(2)}) copy-start(bf16[32]{0:T(256)(128)(2,1)} %param.14) | copy-start | bytes 196
  12.4 220.6 %all-to-all-start = ((bf16[32,384,128]{2,1,0:T(8,128)(2,1)}), bf16[32,384,128]{2,1,0:T(8,128)(2,1)}, u32[]{:S(2)}, u32[]{:S(2)}) async-start(bf16[32,384,128]{2,1,0:T(8,128)(2,1)} %pad_maximum_fusion), calls=%async_computation | async-start | bytes 6291456 | tf_op jit(solution)/shard_map/all_to_all | solution.py:102
  29.3 118.1 %reduce-scatter.2.cloned.1.call-start = ((), (), s32[]{:S(2)}) async-start(), calls=%async_computation.3 | async-start | bytes 1253376 | tf_op jit(solution)/shard_map/reduce_scatter | solution.py:82
  30.3 3.3 collective-permute-start
  35.1 196.0 %all-gather.2.cloned.1.call-start = ((), (), s32[]{:S(2)}) async-start(), calls=%async_computation.4 | async-start | bytes 1081344 | tf_op jit(solution)/shard_map/all_gather | solution.py:88
Sparse Core Ops, SparseCore 0:
  35.2 112.1 reduce-scatter.1
  149.9 81.1 all-gather.1

commit v2 on v1

v2 whole, which is shorter than its diff:
```python
import math

import jax
import jax.numpy as jnp
from jax import lax
from jax.experimental import pallas as pl
from jax.experimental.pallas import tpu as pltpu
from jax.sharding import PartitionSpec as P


def attention_probs(recv, tile, sub_rows):
    peers, _, rows, hd = recv.shape
    tokens = peers * rows
    to_exp2 = hd**-0.5 * math.log2(math.e)

    def kernel(q_ref, k_ref, p_ref):
        keys = k_ref[...].reshape(tokens, hd)
        for at in range(tile // sub_rows):
            q = q_ref[(at * sub_rows) // rows, 0, pl.ds((at * sub_rows) % rows, sub_rows)]
            scores = lax.dot_general(
                q, keys, (((1,), (1,)), ((), ())), preferred_element_type=jnp.float32
            )
            top = jnp.max(scores, axis=1, keepdims=True)
            probs = jnp.exp2((scores - top) * to_exp2)
            total = jnp.sum(probs, axis=1, keepdims=True)
            p_ref[pl.ds(at * sub_rows, sub_rows)] = (probs * (1.0 / total)).astype(jnp.bfloat16)

    return pl.pallas_call(
        kernel,
        name="probs",
        grid=(tokens // tile,),
        in_specs=[
            pl.BlockSpec((tile // rows, 1, rows, hd), lambda i: (i, 0, 0, 0)),
            pl.BlockSpec((peers, 1, rows, hd), lambda i: (0, 1, 0, 0)),
        ],
        out_specs=pl.BlockSpec((tile, tokens), lambda i: (i, 0)),
        out_shape=jax.ShapeDtypeStruct((tokens, tokens), jnp.bfloat16),
        cost_estimate=pl.CostEstimate(
            flops=2 * tokens * tokens * hd,
            transcendentals=tokens * tokens,
            bytes_accessed=2 * tokens * tokens,
        ),
        compiler_params=pltpu.CompilerParams(vmem_limit_bytes=48 << 20),
    )(recv, recv)


def weigh_values(probs, recv, mix, tile):
    peers, rows, hd = recv.shape
    tokens = peers * rows

    def kernel(p_ref, v_ref, mix_ref, o_ref, mixed):
        @pl.when(pl.program_id(0) == 0)
        def _():
            values = v_ref[...].reshape(tokens, hd).astype(jnp.float32)
            mixed[...] = (values + mix_ref[...]).astype(jnp.bfloat16)

        o_ref[...] = jnp.dot(
            p_ref[...], mixed[...], preferred_element_type=jnp.float32
        ).astype(jnp.bfloat16)

    return pl.pallas_call(
        kernel,
        name="weigh",
        grid=(tokens // tile,),
        in_specs=[
            pl.BlockSpec((tile, tokens), lambda i: (i, 0)),
            pl.BlockSpec((peers, rows, hd), lambda i: (0, 0, 0)),
            pl.BlockSpec((tokens, hd), lambda i: (0, 0)),
        ],
        out_specs=pl.BlockSpec((tile, hd), lambda i: (i, 0)),
        out_shape=jax.ShapeDtypeStruct((tokens, hd), jnp.bfloat16),
        scratch_shapes=[pltpu.VMEM((tokens, hd), jnp.bfloat16)],
        compiler_params=pltpu.CompilerParams(vmem_limit_bytes=48 << 20),
    )(probs, recv, mix)


def gathered_condition(splats, splat_dest, splat_sub, splat_weight, own_blocks):
    peers = lax.axis_size("seq")
    chips = peers // 2
    count, blk_rows, feats = splats.shape
    blocks = peers * own_blocks
    per_chip = 2 * own_blocks
    half = blk_rows // 2
    first_core = lax.axis_index("seq") % 2 == 0
    swap = [(d, d ^ 1) for d in range(peers)]
    same_core = [[2 * z + c for z in range(chips)] for c in range(2)]
    target = splat_dest * own_blocks + splat_sub
    table = jnp.where(
        target[None, :] == jnp.arange(blocks, dtype=jnp.int32)[:, None],
        splat_weight[None, :],
        jnp.zeros((), jnp.bfloat16),
    )
    low = splats[:, :half].reshape(count, half * feats)
    high = splats[:, half:].reshape(count, half * feats)
    mine = jnp.where(first_core, low, high)
    other = jnp.where(first_core, high, low)
    arrived = lax.ppermute(jnp.concatenate([other, table.T], axis=1), "seq", swap)
    rows = jnp.concatenate([mine, arrived[:, : half * feats]], axis=0)
    both_table = jnp.concatenate([table, arrived[:, half * feats :].T], axis=1)
    sums = jnp.dot(both_table, rows, preferred_element_type=jnp.float32)
    weights = jnp.sum(both_table.astype(jnp.float32), axis=1, keepdims=True)
    partial = jnp.concatenate([sums, jnp.broadcast_to(weights, (blocks, 2 * feats))], axis=1)
    total = lax.psum_scatter(
        partial, "seq", scatter_dimension=0, tiled=True, axis_index_groups=same_core
    )
    denom = jnp.maximum(total[:, half * feats : half * feats + 1], 1.0)
    cond = (total[:, : half * feats] / denom).astype(jnp.bfloat16)
    cond = cond.reshape(per_chip, half, feats)
    theirs = lax.ppermute(cond, "seq", swap)
    on_chip = jnp.concatenate(
        [jnp.where(first_core, cond, theirs), jnp.where(first_core, theirs, cond)], axis=1
    )
    on_chip = on_chip.reshape(per_chip * blk_rows, feats)
    return lax.all_gather(on_chip, "seq", axis=0, tiled=True, axis_index_groups=same_core)


def on_device(
    queries, attn_keys, attn_values, splats, splat_dest, splat_sub, splat_weight, cond_weight
):
    tok_rows, head_count, head_size = queries.shape
    peers = lax.axis_size("seq")
    own_blocks = tok_rows // splats.shape[1]
    send = jnp.concatenate([queries.transpose(1, 0, 2), attn_keys.transpose(1, 0, 2)], axis=1)
    recv = lax.all_to_all(send, "seq", split_axis=0, concat_axis=0, tiled=True)
    cond = gathered_condition(splats, splat_dest, splat_sub, splat_weight, own_blocks)
    values, recv = lax.optimization_barrier((attn_values.transpose(1, 0, 2), recv))
    values = lax.all_to_all(values, "seq", split_axis=0, concat_axis=0, tiled=True)
    probs = attention_probs(recv.reshape(peers, 2, tok_rows, head_size), 512, 128)
    cond, probs = lax.optimization_barrier((cond, probs))
    mix = jnp.dot(cond, cond_weight[:, 0], preferred_element_type=jnp.float32)
    head_out = weigh_values(probs, values, mix, 512)
    head_out = head_out.reshape(peers, tok_rows, head_size)
    arrived = lax.all_to_all(head_out, "seq", split_axis=0, concat_axis=0, tiled=True)
    return arrived.transpose(1, 0, 2)


def solution(mesh):
    in_specs = (
        P(("dp", "seq"), None, None),
        P(("dp", "seq"), None, None),
        P(("dp", "seq"), None, None),
        P(("dp", "seq"), None, None),
        P(("dp", "seq")),
        P(("dp", "seq")),
        P(("dp", "seq")),
        P(None, "seq", None),
    )
    out_specs = P(("dp", "seq"), None, None)
    return jax.shard_map(
        on_device, mesh=mesh, in_specs=in_specs, out_specs=out_specs, check_vma=False
    )
```

time: 330 us -> 319 us (0.967)
  waiting for transfers between devices: 194 us -> 156 us
  Pallas kernels: 24.3 us -> 38.4 us
  starting transfers between devices: 19.2 us -> 26.9 us
  blocking collectives: 63.9 us -> 70.2 us
    reduce_scatter x1, waiting for transfers between devices: 112 us -> 0.02 us  [gathered_condition(): lax.psum_scatter(partial, 'seq', scatter_dimension=0, tiled=True, axis_in...]
    all_to_all x1, waiting for transfers between devices: 0.01 us -> 102 us  [on_device(): recv = lax.all_to_all(send, 'seq', split_axis=0, concat_axis=0, tiled=True)]
    all_gather x1, waiting for transfers between devices: 81.4 us -> 52.1 us  [gathered_condition(): lax.all_gather(on_chip, 'seq', axis=0, tiled=True, axis_index_groups=same...]
    pallas_call x1 -> x2, Pallas kernels: 24.3 us -> 38.4 us  [the longest x1 22.6 us: attention_probs(): pl.pallas_call(kernel, name='probs', grid=(tokens // tile,), in_specs=[pl...]
    all_to_all x1, blocking collectives: 63.9 us -> 70.2 us  [on_device(): lax.all_to_all(head_out, 'seq', split_axis=0, concat_axis=0, tiled=True)]
    all_to_all x0 -> x1, starting transfers between devices: none -> 5.67 us  [on_device(): lax.all_to_all(values, 'seq', split_axis=0, concat_axis=0, tiled=True)]
  transfers between devices with their start and end apart: 4 -> 6, of which waited for: 3 -> 4; matrix products, arithmetic and copies ran while one was open for 2% -> 2% of each run, Pallas kernels for 0% -> 7%
where the time goes in v2:
time: 319 us; the launch traced here: 318 us
  waiting for transfers between devices  156 us (49%)
  blocking collectives  70.2 us (22%)
  Pallas kernels  38.4 us (12%)
  starting transfers between devices  26.9 us (8%)
  between operations  13.6 us (4%)
  local copies, waits for them, and re-layouts  5.89 us (2%)
  other arithmetic  5.22 us (2%)
    all_to_all x1, waiting for transfers between devices, on_device(): recv = lax.all_to_all(send, 'seq', split_axis=0, concat_axis=0, tiled=True)  102 us
    all_to_all x1, blocking collectives, on_device(): lax.all_to_all(head_out, 'seq', split_axis=0, concat_axis=0, tiled=True)  70.2 us
    all_gather x1, waiting for transfers between devices, gathered_condition(): lax.all_gather(on_chip, 'seq', axis=0, tiled=True, axis_index_groups=same...  52.1 us
    pallas_call x1, Pallas kernels, attention_probs(): pl.pallas_call(kernel, name='probs', grid=(tokens // tile,), in_specs=[pl...  22.6 us
    all_to_all x1, starting transfers between devices, on_device(): recv = lax.all_to_all(send, 'seq', split_axis=0, concat_axis=0, tiled=True)  16.9 us
    pallas_call x1, Pallas kernels, weigh_values(): pl.pallas_call(kernel, name='weigh', grid=(tokens // tile,), in_specs=[pl...  15.8 us
  transfers between devices with their start and end apart: 6, of which 4 were waited for; matrix products, arithmetic and copies ran while one was open for 2% of the time, Pallas kernels for 7%

profile of v2, /device:TPU:1, one launch (start us, length us, event | category | flops | bytes accessed | tf_op | source)
XLA Modules:
  0.0 317.9 jit_solution(3392237601414447798)
XLA Ops:
  6.5 2.4 copy_bitcast_fusion
  8.9 1.6 pad_maximum_fusion
  10.5 16.9 %all-to-all-start = ((bf16[32,256,128]{2,1,0:T(8,128)(2,1)}), bf16[32,256,128]{2,1,0:T(8,128)(2,1)S(1)}, u32[]{:S(2)}, u32[]{:S(2)}) async-start(bf16[32,256,128]{2,1,0:T(8,128)(2,1)} %pad_maximum_fusion), calls=%async_computation.1 | async-start | bytes 4194304 | tf_op jit(solution)/shard_map/all_to_all | solution.py:124
  27.4 0.0 reduce-scatter.2.cloned.1.call-start
  27.6 0.1 fusion.9
  27.7 2.1 collective-permute-start
  29.9 0.1 fusion.8
  29.9 1.0 collective-permute-done
  31.0 0.3 fusion
  31.3 0.0 copy-start.1
  31.3 0.1 broadcast_in_dim.29
  31.4 1.1 pad_maximum_fusion.1
  32.5 0.0 reduce-scatter.2.cloned.1.call-update
  32.5 0.3 copy-done.1
  32.8 1.4 copy.34
  34.2 101.6 %all-to-all-done = bf16[32,256,128]{2,1,0:T(8,128)(2,1)S(1)} async-done(((bf16[32,256,128]{2,1,0:T(8,128)(2,1)}), bf16[32,256,128]{2,1,0:T(8,128)(2,1)S(1)}, u32[]{:S(2)}, u32[]{:S(2)}) %all-to-all-start) | async-done | bytes 2097184 | tf_op jit(solution)/shard_map/all_to_all | solution.py:124
  135.8 5.7 %all-to-all-start.1 = ((bf16[32,128,128]{2,1,0:T(8,128)(2,1)}), bf16[32,128,128]{2,1,0:T(8,128)(2,1)S(1)}, u32[]{:S(2)}, u32[]{:S(2)}) async-start(bf16[32,128,128]{2,1,0:T(8,128)(2,1)} %bitcast.30), calls=%async_computation.2 | async-start | bytes 2097152 | tf_op jit(solution)/shard_map/all_to_all | solution.py:127
  141.5 0.0 all-gather.2.cloned.1.call-start
  141.5 0.0 reduce-scatter.2.cloned.1.call-done
  141.5 0.8 fusion.10
  142.3 0.9 fusion.7
  143.3 2.1 collective-permute-start.1
  145.4 0.9 collective-permute-done.1
  146.4 0.6 pad_maximum_fusion.3
  147.0 0.0 all-gather.2.cloned.1.call-update
  147.0 22.6 %probs.1.p_ref = bf16[4096,4096]{1,0:T(8,128)(2,1)} custom-call(bf16[32,2,128,128]{3,2,1,0:T(8,128)(2,1)S(1)} %bitcast.27, bf16[32,2,128,128]{3,2,1,0:T(8,128)(2,1)S(1)} %bitcast.28), custom_call_target="tpu_custom_call" | custom-call | flops 4294967296 | bytes 33554432 | tf_op jit(solution)/shard_map/probs/pallas_call | solution.py:28
  169.6 52.1 %all-gather.2.cloned.1.call-done = bf16[4096,128]{1,0:T(8,128)(2,1)} async-done(((bf16[256,128]{1,0:T(8,128)(2,1)}), bf16[4096,128]{1,0:T(8,128)(2,1)}) %all-gather.2.cloned.1.call-update) | async-done | bytes 1048592 | tf_op jit(solution)/shard_map/all_gather | solution.py:114
  221.7 1.6 fusion.5.mix_ref
  223.3 0.0 all-to-all-done.1.v_ref
  223.3 15.8 %weigh.1 = bf16[4096,128]{1,0:T(8,128)(2,1)S(1)} custom-call(bf16[4096,4096]{1,0:T(8,128)(2,1)} %probs.1.p_ref, bf16[32,128,128]{2,1,0:T(8,128)(2,1)S(1)} %all-to-all-done.1.v_ref, f32[4096,128]{1,0:T(8,128)S(1)} %fusion.5.mix_ref), custom_call_target="tpu_custom_call" | custom-call | tf_op jit(solution)/shard_map/weigh/pallas_call | solution.py:61
  239.2 70.2 %all_to_all.15 = bf16[32,128,128]{2,1,0:T(8,128)(2,1)S(1)} all-to-all(bf16[32,128,128]{2,1,0:T(8,128)(2,1)S(1)} %bitcast.29), channel_id=1, replica_groups=mesh['dp'=16,'seq'=32] {'seq'}, dimensions={0} | all-to-all | bytes 2097152 | tf_op jit(solution)/shard_map/all_to_all | solution.py:133
  309.4 1.6 copy.24
  (20 shorter events, 0.2 us)
Async XLA Ops:
  6.5 215.1 %copy-start = (bf16[128,1,128]{2,0,1:T(8,128)(2,1)S(1)}, bf16[128,1,128]{2,0,1:T(8,128)(2,1)}, u32[]{:S(2)}) copy-start(bf16[128,1,128]{2,0,1:T(8,128)(2,1)} %param.15) | copy-start | bytes 98308
  10.5 17.0 %copy-start.2 = (bf16[32,32,128]{2,1,0:T(8,128)(2,1)S(1)}, bf16[32,32,128]{2,1,0:T(8,128)(2,1)}, u32[]{:S(2)}) copy-start(bf16[32,32,128]{2,1,0:T(8,128)(2,1)} %param.11) | copy-start | bytes 786436
  10.5 17.1 %copy-start.4 = (s32[32]{0:T(128)S(1)}, s32[32]{0:T(128)}, u32[]{:S(2)}) copy-start(s32[32]{0:T(128)} %param.13) | copy-start | bytes 388
  10.5 17.1 %copy-start.5 = (s32[32]{0:T(128)S(1)}, s32[32]{0:T(128)}, u32[]{:S(2)}) copy-start(s32[32]{0:T(128)} %param.12) | copy-start | bytes 388
  10.5 17.1 %copy-start.3 = (bf16[32]{0:T(256)(128)(2,1)S(1)}, bf16[32]{0:T(256)(128)(2,1)}, u32[]{:S(2)}) copy-start(bf16[32]{0:T(256)(128)(2,1)} %param.14) | copy-start | bytes 196
  10.5 125.3 %all-to-all-start = ((bf16[32,256,128]{2,1,0:T(8,128)(2,1)}), bf16[32,256,128]{2,1,0:T(8,128)(2,1)S(1)}, u32[]{:S(2)}, u32[]{:S(2)}) async-start(bf16[32,256,128]{2,1,0:T(8,128)(2,1)} %pad_maximum_fusion), calls=%async_computation.1 | async-start | bytes 4194304 | tf_op jit(solution)/shard_map/all_to_all | solution.py:124
  27.4 114.2 %reduce-scatter.2.cloned.1.call-start = ((), (), s32[]{:S(2)}) async-start(), calls=%async_computation.4 | async-start | bytes 1253376 | tf_op jit(solution)/shard_map/reduce_scatter | solution.py:103
  27.7 3.3 %collective-permute-start = (bf16[32,2176]{1,0:T(8,128)(2,1)S(1)}, bf16[32,2176]{1,0:T(8,128)(2,1)S(1)}, u32[]{:S(2)}, u32[]{:S(2)}) collective-permute-start(bf16[32,2176]{1,0:T(8,128)(2,1)S(1)} %pad_maximum_fusion.2), channel_id=1, source_target_pairs={{0,1},{1,0},{2,3},{3,2},{4,5},{5,4},{6,7},{7,6},{8,9},{9,8},{10,11... | collective-permute-start | bytes 417800 | tf_op jit(solution)/shard_map/ppermute | solution.py:97
  31.3 1.5 copy-start.1
  135.8 87.5 %all-to-all-start.1 = ((bf16[32,128,128]{2,1,0:T(8,128)(2,1)}), bf16[32,128,128]{2,1,0:T(8,128)(2,1)S(1)}, u32[]{:S(2)}, u32[]{:S(2)}) async-start(bf16[32,128,128]{2,1,0:T(8,128)(2,1)} %bitcast.30), calls=%async_computation.2 | async-start | bytes 2097152 | tf_op jit(solution)/shard_map/all_to_all | solution.py:127
  141.5 80.2 %all-gather.2.cloned.1.call-start = ((), (), s32[]{:S(2)}) async-start(), calls=%async_computation.5 | async-start | bytes 1114112 | tf_op jit(solution)/shard_map/all_gather | solution.py:114
  143.3 3.1 collective-permute-start.1
Sparse Core Ops, SparseCore 0:
  32.6 103.3 reduce-scatter.1
  147.2 74.4 all-gather.1

commit v3 on v2

v3 whole, which is shorter than its diff:
```python
import math

import jax
import jax.numpy as jnp
from jax import lax
from jax.experimental import pallas as pl
from jax.experimental.pallas import tpu as pltpu
from jax.sharding import PartitionSpec as P


def attention_probs(recv, tile, sub_rows):
    peers, _, rows, hd = recv.shape
    tokens = peers * rows
    to_exp2 = hd**-0.5 * math.log2(math.e)

    def kernel(q_ref, k_ref, p_ref):
        keys = k_ref[...].reshape(tokens, hd)
        for at in range(tile // sub_rows):
            q = q_ref[(at * sub_rows) // rows, 0, pl.ds((at * sub_rows) % rows, sub_rows)]
            scores = lax.dot_general(
                q, keys, (((1,), (1,)), ((), ())), preferred_element_type=jnp.float32
            )
            top = jnp.max(scores, axis=1, keepdims=True)
            probs = jnp.exp2((scores - top) * to_exp2)
            total = jnp.sum(probs, axis=1, keepdims=True)
            p_ref[pl.ds(at * sub_rows, sub_rows)] = (probs * (1.0 / total)).astype(jnp.bfloat16)

    return pl.pallas_call(
        kernel,
        name="probs",
        grid=(tokens // tile,),
        in_specs=[
            pl.BlockSpec((tile // rows, 1, rows, hd), lambda i: (i, 0, 0, 0)),
            pl.BlockSpec((peers, 1, rows, hd), lambda i: (0, 1, 0, 0)),
        ],
        out_specs=pl.BlockSpec((tile, tokens), lambda i: (i, 0)),
        out_shape=jax.ShapeDtypeStruct((tokens, tokens), jnp.bfloat16),
        cost_estimate=pl.CostEstimate(
            flops=2 * tokens * tokens * hd,
            transcendentals=tokens * tokens,
            bytes_accessed=2 * tokens * tokens,
        ),
        compiler_params=pltpu.CompilerParams(vmem_limit_bytes=24 << 20),
    )(recv, recv)


def weigh_values(probs, values, tile):
    peers, rows, hd = values.shape
    tokens = peers * rows

    def kernel(p_ref, v_ref, o_ref):
        v = v_ref[...].reshape(tokens, hd)
        o_ref[...] = jnp.dot(p_ref[...], v, preferred_element_type=jnp.float32).astype(
            jnp.bfloat16
        )

    return pl.pallas_call(
        kernel,
        name="weigh",
        grid=(tokens // tile,),
        in_specs=[
            pl.BlockSpec((tile, tokens), lambda i: (i, 0)),
            pl.BlockSpec((peers, rows, hd), lambda i: (0, 0, 0)),
        ],
        out_specs=pl.BlockSpec((tile, hd), lambda i: (i, 0)),
        out_shape=jax.ShapeDtypeStruct((tokens, hd), jnp.bfloat16),
        compiler_params=pltpu.CompilerParams(vmem_limit_bytes=24 << 20),
    )(probs, values)


def block_table(dest_ref, sub_ref, weight_ref, own_blocks, blocks):
    target = dest_ref[...] * own_blocks + sub_ref[...]
    count = target.shape[1]
    rows = lax.broadcasted_iota(jnp.int32, (blocks, count), 0)
    weight = jnp.broadcast_to(weight_ref[...].astype(jnp.float32), (blocks, count))
    return jnp.where(rows == target, weight, 0.0)


def block_sums(splats, splat_dest, splat_sub, splat_weight, own_blocks):
    peers = lax.axis_size("seq")
    count, blk_rows, feats = splats.shape
    blocks = peers * own_blocks
    half = blk_rows // 2
    core = (lax.axis_index("seq") % 2).astype(jnp.int32)[None]
    ids = [splat_dest[None], splat_sub[None], splat_weight[None]]
    id_specs = [pl.BlockSpec((1, count), lambda i, c: (0, 0)) for _ in ids]

    def pack(core_ref, dest_ref, sub_ref, weight_ref, rows_ref, out_ref):
        out_ref[: count * half] = rows_ref[...].reshape(count * half, feats)
        table = block_table(dest_ref, sub_ref, weight_ref, own_blocks, blocks)
        out_ref[count * half :] = table.T.astype(jnp.bfloat16)

    packed = pl.pallas_call(
        pack,
        name="pack_splats",
        grid_spec=pltpu.PrefetchScalarGridSpec(
            num_scalar_prefetch=1,
            grid=(1,),
            in_specs=[
                *id_specs,
                pl.BlockSpec((count, half, feats), lambda i, c: (0, 1 - c[0], 0)),
            ],
            out_specs=pl.BlockSpec((count * (half + 1), blocks), lambda i, c: (0, 0)),
        ),
        out_shape=jax.ShapeDtypeStruct((count * (half + 1), blocks), jnp.bfloat16),
    )(core, *ids, splats)
    arrived = lax.ppermute(packed, "seq", [(d, d ^ 1) for d in range(peers)])

    def sums(core_ref, dest_ref, sub_ref, weight_ref, rows_ref, other_ref, out_ref):
        table = block_table(dest_ref, sub_ref, weight_ref, own_blocks, blocks)
        other = other_ref[count * half :].astype(jnp.float32).T
        both = jnp.concatenate([table, other], axis=1)
        weight = jnp.sum(both, axis=1, keepdims=True)
        both = both.astype(jnp.bfloat16)
        mine = rows_ref[...].reshape(count, half * feats)
        theirs = other_ref[: count * half].reshape(count, half * feats)
        rows = jnp.concatenate([mine, theirs], axis=0)
        out_ref[:, : half * feats] = jnp.dot(both, rows, preferred_element_type=jnp.float32)
        out_ref[:, half * feats :] = jnp.broadcast_to(weight, (blocks, 2 * feats))

    width = (half + 2) * feats
    return pl.pallas_call(
        sums,
        name="block_sums",
        grid_spec=pltpu.PrefetchScalarGridSpec(
            num_scalar_prefetch=1,
            grid=(1,),
            in_specs=[
                *id_specs,
                pl.BlockSpec((count, half, feats), lambda i, c: (0, c[0], 0)),
                pl.BlockSpec((count * (half + 1), blocks), lambda i, c: (0, 0)),
            ],
            out_specs=pl.BlockSpec((blocks, width), lambda i, c: (0, 0)),
        ),
        out_shape=jax.ShapeDtypeStruct((blocks, width), jnp.float32),
    )(core, *ids, splats, arrived)


def own_condition(total, half, feats, own_blocks, swap):
    first_core = lax.axis_index("seq") % 2 == 0
    denom = jnp.maximum(total[:, half * feats : half * feats + 1], 1.0)
    cond = (total[:, : half * feats] / denom).astype(jnp.bfloat16)
    cond = cond.reshape(2, own_blocks, half, feats)
    mine = jnp.where(first_core, cond[0], cond[1])
    theirs = lax.ppermute(jnp.where(first_core, cond[1], cond[0]), "seq", swap)
    low = jnp.where(first_core, mine, theirs)
    high = jnp.where(first_core, theirs, mine)
    return jnp.concatenate([low, high], axis=1).reshape(own_blocks * 2 * half, feats)


def mix_values(cond, weights, values):
    heads, rows, hd = values.shape
    feats = cond.shape[1]
    group = 8

    def kernel(c_ref, w_ref, v_ref, o_ref):
        for h in range(group):
            mix = jnp.dot(c_ref[...], w_ref[h], preferred_element_type=jnp.float32)
            o_ref[h] = (v_ref[h].astype(jnp.float32) + mix).astype(jnp.bfloat16)

    return pl.pallas_call(
        kernel,
        name="mix",
        grid=(heads // group,),
        in_specs=[
            pl.BlockSpec((rows, feats), lambda i: (0, 0)),
            pl.BlockSpec((group, feats, hd), lambda i: (i, 0, 0)),
            pl.BlockSpec((group, rows, hd), lambda i: (i, 0, 0)),
        ],
        out_specs=pl.BlockSpec((group, rows, hd), lambda i: (i, 0, 0)),
        out_shape=jax.ShapeDtypeStruct((heads, rows, hd), jnp.bfloat16),
    )(cond, weights, values)


def on_device(
    queries, attn_keys, attn_values, splats, splat_dest, splat_sub, splat_weight, cond_weight
):
    tok_rows, head_count, head_size = queries.shape
    peers = lax.axis_size("seq")
    _, blk_rows, feats = splats.shape
    own_blocks = tok_rows // blk_rows
    swap = [(d, d ^ 1) for d in range(peers)]
    same_core = [[d for d in range(c, peers, 2)] for c in range(2)]
    first_core = lax.axis_index("seq") % 2 == 0

    partial = block_sums(splats, splat_dest, splat_sub, splat_weight, own_blocks)
    send = jnp.concatenate([queries.transpose(1, 0, 2), attn_keys.transpose(1, 0, 2)], axis=1)
    total = lax.psum_scatter(
        partial, "seq", scatter_dimension=0, tiled=True, axis_index_groups=same_core
    )
    recv = lax.all_to_all(send, "seq", split_axis=0, concat_axis=0, tiled=True)

    weights, _ = lax.optimization_barrier((cond_weight[:, 0], partial))
    weights = lax.all_gather(weights, "seq", axis=0, axis_index_groups=same_core)
    others = lax.ppermute(weights, "seq", swap)
    even = jnp.where(first_core, weights, others)
    odd = jnp.where(first_core, others, weights)
    weights = jnp.stack([even, odd], axis=1).reshape(head_count, feats, head_size)

    cond = own_condition(total, blk_rows // 2, feats, own_blocks, swap)
    mixed = mix_values(cond, weights, attn_values.transpose(1, 0, 2))
    mixed, recv = lax.optimization_barrier((mixed, recv))
    values = lax.all_to_all(mixed, "seq", split_axis=0, concat_axis=0, tiled=True)
    probs = attention_probs(recv.reshape(peers, 2, tok_rows, head_size), 512, 128)
    head_out = weigh_values(probs, values, 512)
    head_out = head_out.reshape(peers, tok_rows, head_size)
    arrived = lax.all_to_all(head_out, "seq", split_axis=0, concat_axis=0, tiled=True)
    return arrived.transpose(1, 0, 2)


def solution(mesh):
    in_specs = (
        P(("dp", "seq"), None, None),
        P(("dp", "seq"), None, None),
        P(("dp", "seq"), None, None),
        P(("dp", "seq"), None, None),
        P(("dp", "seq")),
        P(("dp", "seq")),
        P(("dp", "seq")),
        P(None, "seq", None),
    )
    out_specs = P(("dp", "seq"), None, None)
    return jax.shard_map(
        on_device, mesh=mesh, in_specs=in_specs, out_specs=out_specs, check_vma=False
    )
```

time: 319 us -> 323 us (1.013)
  waiting for transfers between devices: 156 us -> 34.5 us
  blocking collectives: 70.2 us -> 175 us
  starting transfers between devices: 26.9 us -> 37.4 us
  Pallas kernels: 38.4 us -> 46.3 us
    all_gather x0 -> x1, blocking collectives: none -> 116 us  [on_device(): lax.all_gather(weights, 'seq', axis=0, axis_index_groups=same_core)]
    all_to_all x1, waiting for transfers between devices: 102 us -> 0.01 us  [on_device(): recv = lax.all_to_all(send, 'seq', split_axis=0, concat_axis=0, tiled=True)]
    all_gather x1 -> x0, waiting for transfers between devices: 52.1 us -> none  [gathered_condition(): lax.all_gather(on_chip, 'seq', axis=0, tiled=True, axis_index_groups=same...]
    all_to_all x1, waiting for transfers between devices: 0.01 us -> 33.1 us  [on_device(): lax.all_to_all(mixed, 'seq', split_axis=0, concat_axis=0, tiled=True)]
    all_to_all x1, blocking collectives: 70.2 us -> 59 us  [on_device(): lax.all_to_all(head_out, 'seq', split_axis=0, concat_axis=0, tiled=True)]
    pallas_call x0 -> x3, Pallas kernels: none -> 8.09 us  [the longest x1 3.96 us: mix_values(): pl.pallas_call(kernel, name='mix', grid=(heads // group,), in_specs=[pl.B...]
    ppermute x2 -> x3, starting transfers between devices: 4.29 us -> 10.8 us  [the longest x1 6.8 us: on_device(): others = lax.ppermute(weights, 'seq', swap)]
    all_to_all x1, starting transfers between devices: 5.67 us -> 9.74 us  [on_device(): lax.all_to_all(mixed, 'seq', split_axis=0, concat_axis=0, tiled=True)]
  transfers between devices with their start and end apart: 6 -> 6, of which waited for: 4 -> 2; matrix products, arithmetic and copies ran while one was open for 2% -> 3% of each run, Pallas kernels for 7% -> 10%
where the time goes in v3:
time: 323 us; the launch traced here: 322 us
  blocking collectives  175 us (54%)
  Pallas kernels  46.3 us (14%)
  starting transfers between devices  37.4 us (12%)
  waiting for transfers between devices  34.5 us (11%)
  between operations  13.5 us (4%)
  other arithmetic  7.95 us (2%)
  local copies, waits for them, and re-layouts  7.3 us (2%)
    all_gather x1, blocking collectives, on_device(): lax.all_gather(weights, 'seq', axis=0, axis_index_groups=same_core)  116 us
    all_to_all x1, blocking collectives, on_device(): lax.all_to_all(head_out, 'seq', split_axis=0, concat_axis=0, tiled=True)  59 us
    all_to_all x1, waiting for transfers between devices, on_device(): lax.all_to_all(mixed, 'seq', split_axis=0, concat_axis=0, tiled=True)  33.1 us
    pallas_call x1, Pallas kernels, attention_probs(): pl.pallas_call(kernel, name='probs', grid=(tokens // tile,), in_specs=[pl...  22.6 us
    all_to_all x1, starting transfers between devices, on_device(): recv = lax.all_to_all(send, 'seq', split_axis=0, concat_axis=0, tiled=True)  16.8 us
    pallas_call x1, Pallas kernels, weigh_values(): pl.pallas_call(kernel, name='weigh', grid=(tokens // tile,), in_specs=[pl...  15.6 us
    all_to_all x1, starting transfers between devices, on_device(): lax.all_to_all(mixed, 'seq', split_axis=0, concat_axis=0, tiled=True)  9.74 us
    ppermute x1, starting transfers between devices, on_device(): others = lax.ppermute(weights, 'seq', swap)  6.8 us
  transfers between devices with their start and end apart: 6, of which 2 were waited for; matrix products, arithmetic and copies ran while one was open for 3% of the time, Pallas kernels for 10%

profile of v3, /device:TPU:1, one launch (start us, length us, event | category | flops | bytes accessed | tf_op | source)
XLA Modules:
  0.0 321.9 jit_solution(18328833465179080879)
XLA Ops:
  6.5 2.4 copy_bitcast_fusion
  8.9 1.6 pad_maximum_fusion
  10.5 16.8 %all-to-all-start = ((bf16[32,256,128]{2,1,0:T(8,128)(2,1)}), bf16[32,256,128]{2,1,0:T(8,128)(2,1)S(1)}, u32[]{:S(2)}, u32[]{:S(2)}) async-start(bf16[32,256,128]{2,1,0:T(8,128)(2,1)} %pad_maximum_fusion), calls=%async_computation.1 | async-start | bytes 4194304 | tf_op jit(solution)/shard_map/all_to_all | solution.py:191
  27.2 0.0 copy-start.1
  27.2 0.0 reduce-scatter.2.cloned.1.call-start
  27.3 1.7 pack_splats.1
  29.0 2.1 collective-permute-start
  31.1 1.3 collective-permute-done.other_ref
  32.4 0.0 copy-start
  32.4 0.7 copy-done
  33.1 2.4 block_sums.1
  35.5 0.0 reduce-scatter.2.cloned.1.call-update
  35.6 0.0 copy-done.1
  35.6 116.0 %all-gather = bf16[2048,128]{1,0:T(8,128)(2,1)S(1)} all-gather(bf16[128,128]{1,0:T(8,128)(2,1)S(1)} %bitcast.43), channel_id=2, replica_groups={{0,2,4,6,8,10,12,14,16,18,20,22,24,26,28,30},{1,3,5,7,9,11,13,15,17,19,..., dimensions={0}, use_global_device_ids=true | all-gather | bytes 557056 | tf_op jit(solution)/shard_map/all_gather | solution.py:194
  151.6 6.8 %collective-permute-start.2 = (bf16[16,128,128]{2,1,0:T(8,128)(2,1)S(1)}, bf16[16,128,128]{2,1,0:T(8,128)(2,1)}, u32[]{:S(2)}, u32[]{:S(2)}) collective-permute-start(bf16[16,128,128]{2,1,0:T(8,128)(2,1)S(1)} %bitcast.40), channel_id=1, source_target_pairs={{0,1},{1,0},{2,3},{3,2},{4,5},{5,4},{6,7},{7,6},{8,9},{9,8},{10,11... | collective-permute-start | bytes 1572872 | tf_op jit(solution)/shard_map/ppermute | solution.py:195
  158.4 2.6 copy.30
  161.0 0.0 collective-permute-done.2
  161.0 1.9 select_bitcast_fusion.1
  162.9 0.8 fusion.1
  163.7 0.9 fusion
  164.7 1.9 collective-permute-start.1
  166.6 2.1 pad_maximum_fusion.1
  168.7 0.0 collective-permute-done.1
  168.7 0.6 pad_maximum_fusion.2
  169.4 4.0 %mix.1 = bf16[32,128,128]{2,1,0:T(8,128)(2,1)} custom-call(bf16[128,128]{1,0:T(8,128)(2,1)} %bitcast.42, bf16[32,128,128]{2,1,0:T(8,128)(2,1)} %bitcast.38, bf16[32,128,128]{2,1,0:T(8,128)(2,1)} %bitcast.37), custom_call_target="tpu_custom_call" | custom-call | tf_op jit(solution)/shard_map/mix/pallas_call | solution.py:161
  173.3 0.0 all-to-all-done
  173.3 9.7 %all-to-all-start.1 = ((bf16[32,128,128]{2,1,0:T(8,128)(2,1)}), bf16[32,128,128]{2,1,0:T(8,128)(2,1)S(1)}, u32[]{:S(2)}, u32[]{:S(2)}) async-start(bf16[32,128,128]{2,1,0:T(8,128)(2,1)} %mix.1), calls=%async_computation.2 | async-start | bytes 2097152 | tf_op jit(solution)/shard_map/all_to_all | solution.py:203
  183.1 22.6 %probs.1.p_ref = bf16[4096,4096]{1,0:T(8,128)(2,1)} custom-call(bf16[32,2,128,128]{3,2,1,0:T(8,128)(2,1)S(1)} %bitcast.34, bf16[32,2,128,128]{3,2,1,0:T(8,128)(2,1)S(1)} %bitcast.35), custom_call_target="tpu_custom_call" | custom-call | flops 4294967296 | bytes 33554432 | tf_op jit(solution)/shard_map/probs/pallas_call | solution.py:28
  205.7 33.1 %all-to-all-done.1.v_ref = bf16[32,128,128]{2,1,0:T(8,128)(2,1)S(1)} async-done(((bf16[32,128,128]{2,1,0:T(8,128)(2,1)}), bf16[32,128,128]{2,1,0:T(8,128)(2,1)S(1)}, u32[]{:S(2)}, u32[]{:S(2)}) %all-to-all-start.1) | async-done | bytes 1048608 | tf_op jit(solution)/shard_map/all_to_all | solution.py:203
  238.8 15.6 %weigh.1 = bf16[4096,128]{1,0:T(8,128)(2,1)S(1)} custom-call(bf16[4096,4096]{1,0:T(8,128)(2,1)} %probs.1.p_ref, bf16[32,128,128]{2,1,0:T(8,128)(2,1)S(1)} %all-to-all-done.1.v_ref), custom_call_target="tpu_custom_call" | custom-call | tf_op jit(solution)/shard_map/weigh/pallas_call | solution.py:57
  254.4 59.0 %all_to_all.15 = bf16[32,128,128]{2,1,0:T(8,128)(2,1)S(1)} all-to-all(bf16[32,128,128]{2,1,0:T(8,128)(2,1)S(1)} %bitcast.36), channel_id=1, replica_groups=mesh['dp'=16,'seq'=32] {'seq'}, dimensions={0} | all-to-all | bytes 2097152 | tf_op jit(solution)/shard_map/all_to_all | solution.py:207
  313.4 1.6 copy.21
  (4 shorter events, 0.0 us)
Async XLA Ops:
  10.5 162.9 %all-to-all-start = ((bf16[32,256,128]{2,1,0:T(8,128)(2,1)}), bf16[32,256,128]{2,1,0:T(8,128)(2,1)S(1)}, u32[]{:S(2)}, u32[]{:S(2)}) async-start(bf16[32,256,128]{2,1,0:T(8,128)(2,1)} %pad_maximum_fusion), calls=%async_computation.1 | async-start | bytes 4194304 | tf_op jit(solution)/shard_map/all_to_all | solution.py:191
  27.2 8.3 %copy-start.1 = (bf16[128,1,128]{2,0,1:T(8,128)(2,1)S(1)}, bf16[128,1,128]{2,0,1:T(8,128)(2,1)}, u32[]{:S(2)}) copy-start(bf16[128,1,128]{2,0,1:T(8,128)(2,1)} %param.15) | copy-start | bytes 98308
  27.2 135.7 %reduce-scatter.2.cloned.1.call-start = ((), (), s32[]{:S(2)}) async-start(), calls=%async_computation.4 | async-start | bytes 1253376 | tf_op jit(solution)/shard_map/reduce_scatter | solution.py:188
  29.0 3.5 %collective-permute-start = (bf16[544,128]{1,0:T(8,128)(2,1)}, bf16[544,128]{1,0:T(8,128)(2,1)S(1)}, u32[]{:S(2)}, u32[]{:S(2)}) collective-permute-start(bf16[544,128]{1,0:T(8,128)(2,1)} %pack_splats.1), channel_id=1, source_target_pairs={{0,1},{1,0},{2,3},{3,2},{4,5},{5,4},{6,7},{7,6},{8,9},{9,8},{10,11... | collective-permute-start | bytes 417800 | tf_op jit(solution)/shard_map/ppermute | solution.py:107
  32.4 0.7 copy-start
  151.6 9.4 %collective-permute-start.2 = (bf16[16,128,128]{2,1,0:T(8,128)(2,1)S(1)}, bf16[16,128,128]{2,1,0:T(8,128)(2,1)}, u32[]{:S(2)}, u32[]{:S(2)}) collective-permute-start(bf16[16,128,128]{2,1,0:T(8,128)(2,1)S(1)} %bitcast.40), channel_id=1, source_target_pairs={{0,1},{1,0},{2,3},{3,2},{4,5},{5,4},{6,7},{7,6},{8,9},{9,8},{10,11... | collective-permute-start | bytes 1572872 | tf_op jit(solution)/shard_map/ppermute | solution.py:195
  164.7 4.0 %collective-permute-start.1 = (bf16[4,16,128]{2,1,0:T(8,128)(2,1)S(1)}, bf16[4,16,128]{2,1,0:T(8,128)(2,1)S(1)}, u32[]{:S(2)}, u32[]{:S(2)}) collective-permute-start(bf16[4,16,128]{2,1,0:T(8,128)(2,1)S(1)} %bitcast.44), channel_id=1, source_target_pairs={{0,1},{1,0},{2,3},{3,2},{4,5},{5,4},{6,7},{7,6},{8,9},{9,8},{10,11... | collective-permute-start | bytes 49160 | tf_op jit(solution)/shard_map/ppermute | solution.py:145
  173.3 65.5 %all-to-all-start.1 = ((bf16[32,128,128]{2,1,0:T(8,128)(2,1)}), bf16[32,128,128]{2,1,0:T(8,128)(2,1)S(1)}, u32[]{:S(2)}, u32[]{:S(2)}) async-start(bf16[32,128,128]{2,1,0:T(8,128)(2,1)} %mix.1), calls=%async_computation.2 | async-start | bytes 2097152 | tf_op jit(solution)/shard_map/all_to_all | solution.py:203
Sparse Core Ops, SparseCore 0:
  35.7 103.9 reduce-scatter.1

commit v4 on v3

--- a/solution.py
+++ b/solution.py
@@ -148,28 +148,52 @@
     return jnp.concatenate([low, high], axis=1).reshape(own_blocks * 2 * half, feats)
 
 
-def mix_values(cond, weights, values):
+def ring_gather(block, chips):
+    ahead = [(2 * z + c, 2 * ((z + 1) % chips) + c) for z in range(chips) for c in range(2)]
+    back = [(dst, src) for src, dst in ahead]
+    found = {0: block}
+    up = down = block
+    for step in range(1, chips // 2 + 1):
+        up = lax.ppermute(up, "seq", ahead)
+        found[step] = up
+        if step < chips // 2:
+            down = lax.ppermute(down, "seq", back)
+            found[chips - step] = down
+    return jnp.stack([found[s] for s in range(chips)])
+
+
+def mix_values(cond, weights, others, values):
     heads, rows, hd = values.shape
-    feats = cond.shape[1]
+    chips, feats, _ = weights.shape
     group = 8
-
-    def kernel(c_ref, w_ref, v_ref, o_ref):
+    place = lax.axis_index("seq").astype(jnp.int32)[None]
+
+    def kernel(place_ref, c_ref, w_ref, w2_ref, v_ref, o_ref):
+        chip, core = place_ref[0] // 2, place_ref[0] % 2
         for h in range(group):
-            mix = jnp.dot(c_ref[...], w_ref[h], preferred_element_type=jnp.float32)
+            at = pl.program_id(0) * (group // 2) + h // 2
+            at = (chip - at + chips) % chips
+            w = jnp.where(core == h % 2, w_ref[at], w2_ref[at])
+            mix = jnp.dot(c_ref[...], w, preferred_element_type=jnp.float32)
             o_ref[h] = (v_ref[h].astype(jnp.float32) + mix).astype(jnp.bfloat16)
 
+    whole = pl.BlockSpec((chips, feats, hd), lambda i, p: (0, 0, 0))
     return pl.pallas_call(
         kernel,
         name="mix",
-        grid=(heads // group,),
-        in_specs=[
-            pl.BlockSpec((rows, feats), lambda i: (0, 0)),
-            pl.BlockSpec((group, feats, hd), lambda i: (i, 0, 0)),
-            pl.BlockSpec((group, rows, hd), lambda i: (i, 0, 0)),
-        ],
-        out_specs=pl.BlockSpec((group, rows, hd), lambda i: (i, 0, 0)),
+        grid_spec=pltpu.PrefetchScalarGridSpec(
+            num_scalar_prefetch=1,
+            grid=(heads // group,),
+            in_specs=[
+                pl.BlockSpec((rows, feats), lambda i, p: (0, 0)),
+                whole,
+                whole,
+                pl.BlockSpec((group, rows, hd), lambda i, p: (i, 0, 0)),
+            ],
+            out_specs=pl.BlockSpec((group, rows, hd), lambda i, p: (i, 0, 0)),
+        ),
         out_shape=jax.ShapeDtypeStruct((heads, rows, hd), jnp.bfloat16),
-    )(cond, weights, values)
+    )(place, cond, weights, others, values)
 
 
 def on_device(
@@ -181,7 +205,6 @@
     own_blocks = tok_rows // blk_rows
     swap = [(d, d ^ 1) for d in range(peers)]
     same_core = [[d for d in range(c, peers, 2)] for c in range(2)]
-    first_core = lax.axis_index("seq") % 2 == 0
 
     partial = block_sums(splats, splat_dest, splat_sub, splat_weight, own_blocks)
     send = jnp.concatenate([queries.transpose(1, 0, 2), attn_keys.transpose(1, 0, 2)], axis=1)
@@ -190,19 +213,15 @@
     )
     recv = lax.all_to_all(send, "seq", split_axis=0, concat_axis=0, tiled=True)
 
-    weights, _ = lax.optimization_barrier((cond_weight[:, 0], partial))
-    weights = lax.all_gather(weights, "seq", axis=0, axis_index_groups=same_core)
+    own_weights, _ = lax.optimization_barrier((cond_weight[:, 0], partial))
+    weights = ring_gather(own_weights, peers // 2)
     others = lax.ppermute(weights, "seq", swap)
-    even = jnp.where(first_core, weights, others)
-    odd = jnp.where(first_core, others, weights)
-    weights = jnp.stack([even, odd], axis=1).reshape(head_count, feats, head_size)
-
     cond = own_condition(total, blk_rows // 2, feats, own_blocks, swap)
-    mixed = mix_values(cond, weights, attn_values.transpose(1, 0, 2))
+    mixed = mix_values(cond, weights, others, attn_values.transpose(1, 0, 2))
     mixed, recv = lax.optimization_barrier((mixed, recv))
     values = lax.all_to_all(mixed, "seq", split_axis=0, concat_axis=0, tiled=True)
     probs = attention_probs(recv.reshape(peers, 2, tok_rows, head_size), 512, 128)
-    head_out = weigh_values(probs, values, 512)
+    head_out = weigh_values(probs, values, 1024)
     head_out = head_out.reshape(peers, tok_rows, head_size)
     arrived = lax.all_to_all(head_out, "seq", split_axis=0, concat_axis=0, tiled=True)
     return arrived.transpose(1, 0, 2)

time: 323 us -> 351 us (1.087)
  blocking collectives: 175 us -> 59 us
  waiting for transfers between devices: 34.5 us -> 127 us
  starting transfers between devices: 37.4 us -> 85.9 us
  local copies, waits for them, and re-layouts: 7.3 us -> 15.7 us
  other arithmetic: 7.95 us -> 3.91 us
    all_gather x1 -> x0, blocking collectives: 116 us -> none  [on_device(): lax.all_gather(weights, 'seq', axis=0, axis_index_groups=same_core)]
    ppermute x0 -> x15, waiting for transfers between devices: none -> 92.3 us  [the longest x7 85.6 us: ring_gather(): down = lax.ppermute(down, 'seq', back)]
    ppermute x0 -> x15, starting transfers between devices: none -> 45.4 us  [the longest x7 29.2 us: ring_gather(): down = lax.ppermute(down, 'seq', back)]
    unnamed x6 -> x23, local copies, waits for them, and re-layouts: 3.3 us -> 11.1 us
    another operation x2 -> x0, other arithmetic: 4.04 us -> none  [on_device(): jnp.stack([even, odd], axis=1).reshape(head_count, feats, head_size)]
  transfers between devices with their start and end apart: 6 -> 21, of which waited for: 2 -> 5; matrix products, arithmetic and copies ran while one was open for 3% -> 4% of each run, Pallas kernels for 10% -> 9%
where the time goes in v4:
time: 351 us; the launch traced here: 350 us
  waiting for transfers between devices  127 us (36%)
  starting transfers between devices  85.9 us (24%)
  blocking collectives  59 us (17%)
  Pallas kernels  45 us (13%)
  local copies, waits for them, and re-layouts  15.7 us (4%)
  between operations  13.7 us (4%)
  other arithmetic  3.91 us (1%)
    ppermute x7, waiting for transfers between devices, ring_gather(): down = lax.ppermute(down, 'seq', back)  85.6 us
    all_to_all x1, blocking collectives, on_device(): lax.all_to_all(head_out, 'seq', split_axis=0, concat_axis=0, tiled=True)  59 us
    all_to_all x1, waiting for transfers between devices, on_device(): lax.all_to_all(mixed, 'seq', split_axis=0, concat_axis=0, tiled=True)  33.1 us
    ppermute x7, starting transfers between devices, ring_gather(): down = lax.ppermute(down, 'seq', back)  29.2 us
    pallas_call x1, Pallas kernels, attention_probs(): pl.pallas_call(kernel, name='probs', grid=(tokens // tile,), in_specs=[pl...  22.6 us
    all_to_all x1, starting transfers between devices, on_device(): recv = lax.all_to_all(send, 'seq', split_axis=0, concat_axis=0, tiled=True)  16.8 us
    ppermute x8, starting transfers between devices, ring_gather(): up = lax.ppermute(up, 'seq', ahead)  16.2 us
    pallas_call x1, Pallas kernels, weigh_values(): pl.pallas_call(kernel, name='weigh', grid=(tokens // tile,), in_specs=[pl...  14.1 us
  transfers between devices with their start and end apart: 21, of which 5 were waited for; matrix products, arithmetic and copies ran while one was open for 4% of the time, Pallas kernels for 9%

profile of v4, /device:TPU:1, one launch (start us, length us, event | category | flops | bytes accessed | tf_op | source)
XLA Modules:
  0.0 349.9 jit_solution(4722958516086870782)
XLA Ops:
  6.5 2.4 copy_bitcast_fusion
  10.5 16.8 %all-to-all-start = ((bf16[32,256,128]{2,1,0:T(8,128)(2,1)}), bf16[32,256,128]{2,1,0:T(8,128)(2,1)S(1)}, u32[]{:S(2)}, u32[]{:S(2)}) async-start(bf16[32,256,128]{2,1,0:T(8,128)(2,1)} %pad_maximum_fusion), calls=%async_computation.1 | async-start | bytes 4194304 | tf_op jit(solution)/shard_map/all_to_all | solution.py:214
  27.3 1.7 pack_splats.1
  29.0 2.3 collective-permute-start
  33.2 2.5 block_sums.1
  35.7 4.6 %collective-permute-start.10 = (bf16[128,128]{1,0:T(8,128)(2,1)S(1)}, bf16[128,128]{1,0:T(8,128)(2,1)S(1)}, u32[]{:S(2)}, u32[]{:S(2)}) collective-permute-start(bf16[128,128]{1,0:T(8,128)(2,1)S(1)} %bitcast.65), channel_id=1, source_target_pairs={{2,0},{3,1},{4,2},{5,3},{6,4},{7,5},{8,6},{9,7},{10,8},{11,9},{12,... | collective-permute-start | bytes 98312 | tf_op jit(solution)/shard_map/ppermute | solution.py:160
  40.3 1.9 collective-permute-start.2
  42.9 85.6 %collective-permute-done.10 = bf16[128,128]{1,0:T(8,128)(2,1)S(1)} collective-permute-done((bf16[128,128]{1,0:T(8,128)(2,1)S(1)}, bf16[128,128]{1,0:T(8,128)(2,1)S(1)}, u32[]{:S(2)}, u32[]{:S(2)}) %collective-permute-start.10) | collective-permute-done | bytes 32800 | tf_op jit(solution)/shard_map/ppermute | solution.py:160
  128.4 2.5 collective-permute-start.11
  131.0 2.8 collective-permute-start.3
  134.3 3.9 %collective-permute-start.12 = (bf16[128,128]{1,0:T(8,128)(2,1)S(1)}, bf16[128,128]{1,0:T(8,128)(2,1)S(1)}, u32[]{:S(2)}, u32[]{:S(2)}) collective-permute-start(bf16[128,128]{1,0:T(8,128)(2,1)S(1)} %collective-permute-done.11), channel_id=1, source_target_pairs={{2,0},{3,1},{4,2},{5,3},{6,4},{7,5},{8,6},{9,7},{10,8},{11,9},{12,... | collective-permute-start | bytes 98312 | tf_op jit(solution)/shard_map/ppermute | solution.py:160
  138.3 1.9 collective-permute-start.4
  140.8 4.6 %collective-permute-start.13 = (bf16[128,128]{1,0:T(8,128)(2,1)S(1)}, bf16[128,128]{1,0:T(8,128)(2,1)S(1)}, u32[]{:S(2)}, u32[]{:S(2)}) collective-permute-start(bf16[128,128]{1,0:T(8,128)(2,1)S(1)} %collective-permute-done.12), channel_id=1, source_target_pairs={{2,0},{3,1},{4,2},{5,3},{6,4},{7,5},{8,6},{9,7},{10,8},{11,9},{12,... | collective-permute-start | bytes 98312 | tf_op jit(solution)/shard_map/ppermute | solution.py:160
  145.4 1.9 collective-permute-start.5
  147.9 4.6 %collective-permute-start.14 = (bf16[128,128]{1,0:T(8,128)(2,1)S(1)}, bf16[128,128]{1,0:T(8,128)(2,1)S(1)}, u32[]{:S(2)}, u32[]{:S(2)}) collective-permute-start(bf16[128,128]{1,0:T(8,128)(2,1)S(1)} %collective-permute-done.13), channel_id=1, source_target_pairs={{2,0},{3,1},{4,2},{5,3},{6,4},{7,5},{8,6},{9,7},{10,8},{11,9},{12,... | collective-permute-start | bytes 98312 | tf_op jit(solution)/shard_map/ppermute | solution.py:160
  152.5 1.9 collective-permute-start.6
  155.0 4.6 %collective-permute-start.15 = (bf16[128,128]{1,0:T(8,128)(2,1)S(1)}, bf16[128,128]{1,0:T(8,128)(2,1)S(1)}, u32[]{:S(2)}, u32[]{:S(2)}) collective-permute-start(bf16[128,128]{1,0:T(8,128)(2,1)S(1)} %collective-permute-done.14), channel_id=1, source_target_pairs={{2,0},{3,1},{4,2},{5,3},{6,4},{7,5},{8,6},{9,7},{10,8},{11,9},{12,... | collective-permute-start | bytes 98312 | tf_op jit(solution)/shard_map/ppermute | solution.py:160
  159.6 1.9 collective-permute-start.7
  162.1 4.6 %collective-permute-start.16 = (bf16[128,128]{1,0:T(8,128)(2,1)S(1)}, bf16[128,128]{1,0:T(8,128)(2,1)S(1)}, u32[]{:S(2)}, u32[]{:S(2)}) collective-permute-start(bf16[128,128]{1,0:T(8,128)(2,1)S(1)} %collective-permute-done.15), channel_id=1, source_target_pairs={{2,0},{3,1},{4,2},{5,3},{6,4},{7,5},{8,6},{9,7},{10,8},{11,9},{12,... | collective-permute-start | bytes 98312 | tf_op jit(solution)/shard_map/ppermute | solution.py:160
  166.7 1.9 collective-permute-start.8
  169.2 3.3 collective-permute-done.8
  172.6 1.9 collective-permute-start.9
  175.1 3.3 collective-permute-done.9
  183.3 8.8 %collective-permute-start.17 = (bf16[16,128,128]{2,1,0:T(8,128)(2,1)}, bf16[16,128,128]{2,1,0:T(8,128)(2,1)}, u32[]{:S(2)}, u32[]{:S(2)}) collective-permute-start(bf16[16,128,128]{2,1,0:T(8,128)(2,1)} %constant_dynamic-update-slice_fusion.w_ref), channel_id=1, source_target_pairs={{0,1},{1,0},{2,3},{3,2},{4,5},{5,4},{6,7},{7,6},{8,9},{9,8},{10,11... | collective-permute-start | bytes 1572872 | tf_op jit(solution)/shard_map/ppermute | solution.py:218
  193.8 1.9 collective-permute-start.1
  197.8 4.1 %mix.1 = bf16[32,128,128]{2,1,0:T(8,128)(2,1)} custom-call(s32[1]{0:T(128)} %bitcast.place_ref, bf16[128,128]{1,0:T(8,128)(2,1)} %bitcast.64, bf16[16,128,128]{2,1,0:T(8,128)(2,1)} %constant_dynamic-update-slice_fusion.w_ref, bf16[16,128,128]{2,1,0:T(8,128)(2,1)} %collective-permute-done.17.w2_ref, bf16[32,128,128]{2,1,0:T(8,128)(2,1)} %bitcast.62), custom_call_target="tpu_custom_call" | custom-call | tf_op jit(solution)/shard_map/mix/pallas_call | solution.py:181
  201.9 10.7 %all-to-all-start.1 = ((bf16[32,128,128]{2,1,0:T(8,128)(2,1)}), bf16[32,128,128]{2,1,0:T(8,128)(2,1)S(1)}, u32[]{:S(2)}, u32[]{:S(2)}) async-start(bf16[32,128,128]{2,1,0:T(8,128)(2,1)} %mix.1), calls=%async_computation.2 | async-start | bytes 2097152 | tf_op jit(solution)/shard_map/all_to_all | solution.py:222
  212.6 22.6 %probs.1.p_ref = bf16[4096,4096]{1,0:T(8,128)(2,1)} custom-call(bf16[32,2,128,128]{3,2,1,0:T(8,128)(2,1)S(1)} %bitcast.59, bf16[32,2,128,128]{3,2,1,0:T(8,128)(2,1)S(1)} %bitcast.60), custom_call_target="tpu_custom_call" | custom-call | flops 4294967296 | bytes 33554432 | tf_op jit(solution)/shard_map/probs/pallas_call | solution.py:28
  235.3 33.1 %all-to-all-done.1.v_ref = bf16[32,128,128]{2,1,0:T(8,128)(2,1)S(1)} async-done(((bf16[32,128,128]{2,1,0:T(8,128)(2,1)}), bf16[32,128,128]{2,1,0:T(8,128)(2,1)S(1)}, u32[]{:S(2)}, u32[]{:S(2)}) %all-to-all-start.1) | async-done | bytes 1048608 | tf_op jit(solution)/shard_map/all_to_all | solution.py:222
  268.3 14.1 %weigh.1 = bf16[4096,128]{1,0:T(8,128)(2,1)S(1)} custom-call(bf16[4096,4096]{1,0:T(8,128)(2,1)} %probs.1.p_ref, bf16[32,128,128]{2,1,0:T(8,128)(2,1)S(1)} %all-to-all-done.1.v_ref), custom_call_target="tpu_custom_call" | custom-call | tf_op jit(solution)/shard_map/weigh/pallas_call | solution.py:57
  282.4 59.0 %all_to_all.15 = bf16[32,128,128]{2,1,0:T(8,128)(2,1)S(1)} all-to-all(bf16[32,128,128]{2,1,0:T(8,128)(2,1)S(1)} %bitcast.61), channel_id=1, replica_groups=mesh['dp'=16,'seq'=32] {'seq'}, dimensions={0} | all-to-all | bytes 2097152 | tf_op jit(solution)/shard_map/all_to_all | solution.py:226
  341.4 1.6 copy.18
  (49 shorter events, 17.1 us)
Async XLA Ops:
  10.5 191.4 %all-to-all-start = ((bf16[32,256,128]{2,1,0:T(8,128)(2,1)}), bf16[32,256,128]{2,1,0:T(8,128)(2,1)S(1)}, u32[]{:S(2)}, u32[]{:S(2)}) async-start(bf16[32,256,128]{2,1,0:T(8,128)(2,1)} %pad_maximum_fusion), calls=%async_computation.1 | async-start | bytes 4194304 | tf_op jit(solution)/shard_map/all_to_all | solution.py:214
  27.2 8.5 %copy-start.2 = (bf16[128,1,128]{2,0,1:T(8,128)(2,1)S(1)}, bf16[128,1,128]{2,0,1:T(8,128)(2,1)}, u32[]{:S(2)}) copy-start(bf16[128,1,128]{2,0,1:T(8,128)(2,1)} %param.15) | copy-start | bytes 98308
  27.2 164.9 %reduce-scatter.2.cloned.1.call-start = ((), (), s32[]{:S(2)}) async-start(), calls=%async_computation.4 | async-start | bytes 1253376 | tf_op jit(solution)/shard_map/reduce_scatter | solution.py:211
  29.0 166.8 %copy-start = (bf16[128,32,128]{2,1,0:T(8,128)(2,1)S(1)}, bf16[128,32,128]{2,1,0:T(8,128)(2,1)}, u32[]{:S(2)}) copy-start(bf16[128,32,128]{2,1,0:T(8,128)(2,1)} %param.10) | copy-start | bytes 3145732
  29.0 3.6 %collective-permute-start = (bf16[544,128]{1,0:T(8,128)(2,1)}, bf16[544,128]{1,0:T(8,128)(2,1)S(1)}, u32[]{:S(2)}, u32[]{:S(2)}) collective-permute-start(bf16[544,128]{1,0:T(8,128)(2,1)} %pack_splats.1), channel_id=1, source_target_pairs={{0,1},{1,0},{2,3},{3,2},{4,5},{5,4},{6,7},{7,6},{8,9},{9,8},{10,11... | collective-permute-start | bytes 417800 | tf_op jit(solution)/shard_map/ppermute | solution.py:107
  32.6 0.7 copy-start.1
  35.7 92.7 %collective-permute-start.10 = (bf16[128,128]{1,0:T(8,128)(2,1)S(1)}, bf16[128,128]{1,0:T(8,128)(2,1)S(1)}, u32[]{:S(2)}, u32[]{:S(2)}) collective-permute-start(bf16[128,128]{1,0:T(8,128)(2,1)S(1)} %bitcast.65), channel_id=1, source_target_pairs={{2,0},{3,1},{4,2},{5,3},{6,4},{7,5},{8,6},{9,7},{10,8},{11,9},{12,... | collective-permute-start | bytes 98312 | tf_op jit(solution)/shard_map/ppermute | solution.py:160
  40.3 90.7 %collective-permute-start.2 = (bf16[128,128]{1,0:T(8,128)(2,1)S(1)}, bf16[128,128]{1,0:T(8,128)(2,1)S(1)}, u32[]{:S(2)}, u32[]{:S(2)}) collective-permute-start(bf16[128,128]{1,0:T(8,128)(2,1)S(1)} %bitcast.66), channel_id=1, source_target_pairs={{0,2},{1,3},{2,4},{3,5},{4,6},{5,7},{6,8},{7,9},{8,10},{9,11},{10,... | collective-permute-start | bytes 98312 | tf_op jit(solution)/shard_map/ppermute | solution.py:157
  128.4 5.9 %collective-permute-start.11 = (bf16[128,128]{1,0:T(8,128)(2,1)S(1)}, bf16[128,128]{1,0:T(8,128)(2,1)S(1)}, u32[]{:S(2)}, u32[]{:S(2)}) collective-permute-start(bf16[128,128]{1,0:T(8,128)(2,1)S(1)} %collective-permute-done.10), channel_id=1, source_target_pairs={{2,0},{3,1},{4,2},{5,3},{6,4},{7,5},{8,6},{9,7},{10,8},{11,9},{12,... | collective-permute-start | bytes 98312 | tf_op jit(solution)/shard_map/ppermute | solution.py:160
  131.0 7.3 %collective-permute-start.3 = (bf16[128,128]{1,0:T(8,128)(2,1)S(1)}, bf16[128,128]{1,0:T(8,128)(2,1)S(1)}, u32[]{:S(2)}, u32[]{:S(2)}) collective-permute-start(bf16[128,128]{1,0:T(8,128)(2,1)S(1)} %collective-permute-done.2), channel_id=1, source_target_pairs={{0,2},{1,3},{2,4},{3,5},{4,6},{5,7},{6,8},{7,9},{8,10},{9,11},{10,... | collective-permute-start | bytes 98312 | tf_op jit(solution)/shard_map/ppermute | solution.py:157
  134.3 6.4 %collective-permute-start.12 = (bf16[128,128]{1,0:T(8,128)(2,1)S(1)}, bf16[128,128]{1,0:T(8,128)(2,1)S(1)}, u32[]{:S(2)}, u32[]{:S(2)}) collective-permute-start(bf16[128,128]{1,0:T(8,128)(2,1)S(1)} %collective-permute-done.11), channel_id=1, source_target_pairs={{2,0},{3,1},{4,2},{5,3},{6,4},{7,5},{8,6},{9,7},{10,8},{11,9},{12,... | collective-permute-start | bytes 98312 | tf_op jit(solution)/shard_map/ppermute | solution.py:160
  138.3 7.1 %collective-permute-start.4 = (bf16[128,128]{1,0:T(8,128)(2,1)S(1)}, bf16[128,128]{1,0:T(8,128)(2,1)S(1)}, u32[]{:S(2)}, u32[]{:S(2)}) collective-permute-start(bf16[128,128]{1,0:T(8,128)(2,1)S(1)} %collective-permute-done.3), channel_id=1, source_target_pairs={{0,2},{1,3},{2,4},{3,5},{4,6},{5,7},{6,8},{7,9},{8,10},{9,11},{10,... | collective-permute-start | bytes 98312 | tf_op jit(solution)/shard_map/ppermute | solution.py:157
  140.8 7.1 %collective-permute-start.13 = (bf16[128,128]{1,0:T(8,128)(2,1)S(1)}, bf16[128,128]{1,0:T(8,128)(2,1)S(1)}, u32[]{:S(2)}, u32[]{:S(2)}) collective-permute-start(bf16[128,128]{1,0:T(8,128)(2,1)S(1)} %collective-permute-done.12), channel_id=1, source_target_pairs={{2,0},{3,1},{4,2},{5,3},{6,4},{7,5},{8,6},{9,7},{10,8},{11,9},{12,... | collective-permute-start | bytes 98312 | tf_op jit(solution)/shard_map/ppermute | solution.py:160
  145.4 7.1 %collective-permute-start.5 = (bf16[128,128]{1,0:T(8,128)(2,1)S(1)}, bf16[128,128]{1,0:T(8,128)(2,1)S(1)}, u32[]{:S(2)}, u32[]{:S(2)}) collective-permute-start(bf16[128,128]{1,0:T(8,128)(2,1)S(1)} %collective-permute-done.4), channel_id=1, source_target_pairs={{0,2},{1,3},{2,4},{3,5},{4,6},{5,7},{6,8},{7,9},{8,10},{9,11},{10,... | collective-permute-start | bytes 98312 | tf_op jit(solution)/shard_map/ppermute | solution.py:157
  147.9 7.1 %collective-permute-start.14 = (bf16[128,128]{1,0:T(8,128)(2,1)S(1)}, bf16[128,128]{1,0:T(8,128)(2,1)S(1)}, u32[]{:S(2)}, u32[]{:S(2)}) collective-permute-start(bf16[128,128]{1,0:T(8,128)(2,1)S(1)} %collective-permute-done.13), channel_id=1, source_target_pairs={{2,0},{3,1},{4,2},{5,3},{6,4},{7,5},{8,6},{9,7},{10,8},{11,9},{12,... | collective-permute-start | bytes 98312 | tf_op jit(solution)/shard_map/ppermute | solution.py:160
  152.5 7.1 %collective-permute-start.6 = (bf16[128,128]{1,0:T(8,128)(2,1)S(1)}, bf16[128,128]{1,0:T(8,128)(2,1)S(1)}, u32[]{:S(2)}, u32[]{:S(2)}) collective-permute-start(bf16[128,128]{1,0:T(8,128)(2,1)S(1)} %collective-permute-done.5), channel_id=1, source_target_pairs={{0,2},{1,3},{2,4},{3,5},{4,6},{5,7},{6,8},{7,9},{8,10},{9,11},{10,... | collective-permute-start | bytes 98312 | tf_op jit(solution)/shard_map/ppermute | solution.py:157
  155.0 7.1 %collective-permute-start.15 = (bf16[128,128]{1,0:T(8,128)(2,1)S(1)}, bf16[128,128]{1,0:T(8,128)(2,1)S(1)}, u32[]{:S(2)}, u32[]{:S(2)}) collective-permute-start(bf16[128,128]{1,0:T(8,128)(2,1)S(1)} %collective-permute-done.14), channel_id=1, source_target_pairs={{2,0},{3,1},{4,2},{5,3},{6,4},{7,5},{8,6},{9,7},{10,8},{11,9},{12,... | collective-permute-start | bytes 98312 | tf_op jit(solution)/shard_map/ppermute | solution.py:160
  159.6 7.1 %collective-permute-start.7 = (bf16[128,128]{1,0:T(8,128)(2,1)S(1)}, bf16[128,128]{1,0:T(8,128)(2,1)S(1)}, u32[]{:S(2)}, u32[]{:S(2)}) collective-permute-start(bf16[128,128]{1,0:T(8,128)(2,1)S(1)} %collective-permute-done.6), channel_id=1, source_target_pairs={{0,2},{1,3},{2,4},{3,5},{4,6},{5,7},{6,8},{7,9},{8,10},{9,11},{10,... | collective-permute-start | bytes 98312 | tf_op jit(solution)/shard_map/ppermute | solution.py:157
  162.1 16.9 %collective-permute-start.16 = (bf16[128,128]{1,0:T(8,128)(2,1)S(1)}, bf16[128,128]{1,0:T(8,128)(2,1)S(1)}, u32[]{:S(2)}, u32[]{:S(2)}) collective-permute-start(bf16[128,128]{1,0:T(8,128)(2,1)S(1)} %collective-permute-done.15), channel_id=1, source_target_pairs={{2,0},{3,1},{4,2},{5,3},{6,4},{7,5},{8,6},{9,7},{10,8},{11,9},{12,... | collective-permute-start | bytes 98312 | tf_op jit(solution)/shard_map/ppermute | solution.py:160
  166.7 5.9 %collective-permute-start.8 = (bf16[128,128]{1,0:T(8,128)(2,1)S(1)}, bf16[128,128]{1,0:T(8,128)(2,1)S(1)}, u32[]{:S(2)}, u32[]{:S(2)}) collective-permute-start(bf16[128,128]{1,0:T(8,128)(2,1)S(1)} %collective-permute-done.7), channel_id=1, source_target_pairs={{0,2},{1,3},{2,4},{3,5},{4,6},{5,7},{6,8},{7,9},{8,10},{9,11},{10,... | collective-permute-start | bytes 98312 | tf_op jit(solution)/shard_map/ppermute | solution.py:157
  172.6 5.9 %collective-permute-start.9 = (bf16[128,128]{1,0:T(8,128)(2,1)S(1)}, bf16[128,128]{1,0:T(8,128)(2,1)S(1)}, u32[]{:S(2)}, u32[]{:S(2)}) collective-permute-start(bf16[128,128]{1,0:T(8,128)(2,1)S(1)} %collective-permute-done.8), channel_id=1, source_target_pairs={{0,2},{1,3},{2,4},{3,5},{4,6},{5,7},{6,8},{7,9},{8,10},{9,11},{10,... | collective-permute-start | bytes 98312 | tf_op jit(solution)/shard_map/ppermute | solution.py:157
  183.3 14.5 %collective-permute-start.17 = (bf16[16,128,128]{2,1,0:T(8,128)(2,1)}, bf16[16,128,128]{2,1,0:T(8,128)(2,1)}, u32[]{:S(2)}, u32[]{:S(2)}) collective-permute-start(bf16[16,128,128]{2,1,0:T(8,128)(2,1)} %constant_dynamic-update-slice_fusion.w_ref), channel_id=1, source_target_pairs={{0,1},{1,0},{2,3},{3,2},{4,5},{5,4},{6,7},{7,6},{8,9},{9,8},{10,11... | collective-permute-start | bytes 1572872 | tf_op jit(solution)/shard_map/ppermute | solution.py:218
  193.8 3.3 collective-permute-start.1
  201.9 66.5 %all-to-all-start.1 = ((bf16[32,128,128]{2,1,0:T(8,128)(2,1)}), bf16[32,128,128]{2,1,0:T(8,128)(2,1)S(1)}, u32[]{:S(2)}, u32[]{:S(2)}) async-start(bf16[32,128,128]{2,1,0:T(8,128)(2,1)} %mix.1), calls=%async_computation.2 | async-start | bytes 2097152 | tf_op jit(solution)/shard_map/all_to_all | solution.py:222
Sparse Core Ops, SparseCore 0:
  35.8 101.9 reduce-scatter.1

commit v5 on v2

v5 whole, which is shorter than its diff:
```python
import math

import jax
import jax.numpy as jnp
from jax import lax
from jax.experimental import pallas as pl
from jax.experimental.pallas import tpu as pltpu
from jax.sharding import PartitionSpec as P


def attention_probs(recv, rows, tile, sub_rows):
    peers, _, hd = recv.shape
    tokens = peers * rows
    to_exp2 = hd**-0.5 * math.log2(math.e)

    def kernel(q_ref, k_ref, p_ref):
        keys = k_ref[...].reshape(tokens, hd)
        for at in range(tile // sub_rows):
            q = q_ref[(at * sub_rows) // rows, pl.ds((at * sub_rows) % rows, sub_rows)]
            scores = lax.dot_general(
                q, keys, (((1,), (1,)), ((), ())), preferred_element_type=jnp.float32
            )
            top = jnp.max(scores, axis=1, keepdims=True)
            probs = jnp.exp2((scores - top) * to_exp2)
            total = jnp.sum(probs, axis=1, keepdims=True)
            p_ref[pl.ds(at * sub_rows, sub_rows)] = (probs * (1.0 / total)).astype(jnp.bfloat16)

    return pl.pallas_call(
        kernel,
        name="probs",
        grid=(tokens // tile,),
        in_specs=[
            pl.BlockSpec((tile // rows, rows, hd), lambda i: (i, 0, 0)),
            pl.BlockSpec((peers, rows, hd), lambda i: (0, 1, 0)),
        ],
        out_specs=pl.BlockSpec((tile, tokens), lambda i: (i, 0)),
        out_shape=jax.ShapeDtypeStruct((tokens, tokens), jnp.bfloat16),
        cost_estimate=pl.CostEstimate(
            flops=2 * tokens * tokens * hd,
            transcendentals=tokens * tokens,
            bytes_accessed=2 * tokens * tokens,
        ),
        compiler_params=pltpu.CompilerParams(vmem_limit_bytes=24 << 20),
    )(recv, recv)


def weigh_values(probs, values, tile):
    peers, rows, hd = values.shape
    tokens = peers * rows

    def kernel(p_ref, v_ref, o_ref):
        v = v_ref[...].reshape(tokens, hd)
        o_ref[...] = jnp.dot(p_ref[...], v, preferred_element_type=jnp.float32).astype(
            jnp.bfloat16
        )

    return pl.pallas_call(
        kernel,
        name="weigh",
        grid=(tokens // tile,),
        in_specs=[
            pl.BlockSpec((tile, tokens), lambda i: (i, 0)),
            pl.BlockSpec((peers, rows, hd), lambda i: (0, 0, 0)),
        ],
        out_specs=pl.BlockSpec((tile, hd), lambda i: (i, 0)),
        out_shape=jax.ShapeDtypeStruct((tokens, hd), jnp.bfloat16),
        compiler_params=pltpu.CompilerParams(vmem_limit_bytes=24 << 20),
    )(probs, values)


SLOTS = 2
KEY_ROWS = 16


def pack_slots(splats, splat_dest, splat_sub, splat_weight, peers):
    count, blk_rows, feats = splats.shape
    out_rows = SLOTS * blk_rows + KEY_ROWS

    def kernel(dest_ref, sub_ref, weight_ref, splat_ref, out_ref, which):
        for at in range(peers * SLOTS):
            which[at] = -1
        for i in range(count):
            first = dest_ref[i] * SLOTS
            which[first + (which[first] >= 0).astype(jnp.int32)] = i
        row = lax.broadcasted_iota(jnp.int32, (KEY_ROWS, feats), 0)
        lane = lax.broadcasted_iota(jnp.int32, (KEY_ROWS, feats), 1)
        for dest in range(peers):
            keys = jnp.zeros((KEY_ROWS, feats), jnp.float32)
            for slot in range(SLOTS):
                found = which[dest * SLOTS + slot]
                at = jnp.maximum(found, 0)
                out_ref[dest, slot * blk_rows : (slot + 1) * blk_rows] = splat_ref[at]
                sub = jnp.where(found >= 0, sub_ref[at], -1)
                keys = jnp.where((row == slot) & (lane == sub), weight_ref[at], keys)
            out_ref[dest, SLOTS * blk_rows :] = keys.astype(jnp.bfloat16)

    scalars = pl.BlockSpec(memory_space=pltpu.SMEM)
    return pl.pallas_call(
        kernel,
        name="pack_slots",
        in_specs=[scalars, scalars, scalars, pl.BlockSpec(memory_space=pltpu.VMEM)],
        out_specs=pl.BlockSpec(memory_space=pltpu.VMEM),
        out_shape=jax.ShapeDtypeStruct((peers, out_rows, feats), jnp.bfloat16),
        scratch_shapes=[pltpu.SMEM((peers * SLOTS,), jnp.int32)],
    )(splat_dest, splat_sub, splat_weight.astype(jnp.float32), splats)


def mix_values(recv, first_row, weights, values, own_blocks, blk_rows):
    heads, rows, hd = values.shape
    peers, _, feats = recv.shape
    group = 8
    part = KEY_ROWS
    parts = SLOTS * blk_rows // part

    def kernel(*refs):
        data_refs, key_ref = refs[:parts], refs[parts]
        w_ref, v_ref, o_ref, cond_ref = refs[parts + 1 :]

        @pl.when(pl.program_id(0) == 0)
        def _():
            sums = [[jnp.zeros((part, feats), jnp.float32)] * (blk_rows // part) for _ in range(own_blocks)]
            total = jnp.zeros((KEY_ROWS, feats), jnp.float32)
            for src in range(peers):
                keys = key_ref[src].astype(jnp.float32)
                total = total + keys
                for at in range(parts):
                    slot, piece = divmod(at * part, blk_rows)
                    data = data_refs[at][src].astype(jnp.float32)
                    for b in range(own_blocks):
                        sums[b][piece // part] += keys[slot : slot + 1, b : b + 1] * data
            weight = jnp.sum(total, axis=0, keepdims=True)
            denom = jnp.maximum(weight, 1.0)
            for b in range(own_blocks):
                for piece in range(blk_rows // part):
                    cond_ref[pl.ds(b * blk_rows + piece * part, part)] = (
                        sums[b][piece] / denom[:, b : b + 1]
                    ).astype(jnp.bfloat16)

        for h in range(group):
            mix = jnp.dot(cond_ref[...], w_ref[h], preferred_element_type=jnp.float32)
            o_ref[h] = (v_ref[h].astype(jnp.float32) + mix).astype(jnp.bfloat16)

    def piece_spec(at):
        return pl.BlockSpec((peers, part, feats), lambda i: (0, first_row // part + at, 0))

    return pl.pallas_call(
        kernel,
        name="mix",
        grid=(heads // group,),
        in_specs=[
            *[piece_spec(at) for at in range(parts + 1)],
            pl.BlockSpec((group, feats, hd), lambda i: (i, 0, 0)),
            pl.BlockSpec((group, rows, hd), lambda i: (i, 0, 0)),
        ],
        out_specs=pl.BlockSpec((group, rows, hd), lambda i: (i, 0, 0)),
        out_shape=jax.ShapeDtypeStruct((heads, rows, hd), jnp.bfloat16),
        scratch_shapes=[pltpu.VMEM((rows, feats), jnp.bfloat16)],
        compiler_params=pltpu.CompilerParams(vmem_limit_bytes=12 << 20),
    )(*[recv] * (parts + 1), weights, values)


def on_device(
    queries, attn_keys, attn_values, splats, splat_dest, splat_sub, splat_weight, cond_weight
):
    tok_rows, head_count, head_size = queries.shape
    peers = lax.axis_size("seq")
    _, blk_rows, feats = splats.shape
    own_blocks = tok_rows // blk_rows

    weights = lax.all_gather(cond_weight[:, 0], "seq", axis=0)
    slots = pack_slots(splats, splat_dest, splat_sub, splat_weight, peers)
    send = jnp.concatenate(
        [queries.transpose(1, 0, 2), attn_keys.transpose(1, 0, 2), slots], axis=1
    )
    values = attn_values.transpose(1, 0, 2)
    recv = lax.all_to_all(send, "seq", split_axis=0, concat_axis=0, tiled=True)
    values = mix_values(recv, 2 * tok_rows, weights, values, own_blocks, blk_rows)
    values = lax.all_to_all(values, "seq", split_axis=0, concat_axis=0, tiled=True)
    probs = attention_probs(recv, tok_rows, 512, 128)
    head_out = weigh_values(probs, values, 1024)
    head_out = head_out.reshape(peers, tok_rows, head_size)
    arrived = lax.all_to_all(head_out, "seq", split_axis=0, concat_axis=0, tiled=True)
    return arrived.transpose(1, 0, 2)


def solution(mesh):
    in_specs = (
        P(("dp", "seq"), None, None),
        P(("dp", "seq"), None, None),
        P(("dp", "seq"), None, None),
        P(("dp", "seq"), None, None),
        P(("dp", "seq")),
        P(("dp", "seq")),
        P(("dp", "seq")),
        P(None, "seq", None),
    )
    out_specs = P(("dp", "seq"), None, None)
    return jax.shard_map(
        on_device, mesh=mesh, in_specs=in_specs, out_specs=out_specs, check_vma=False
    )
```

time: 319 us -> 312 us (0.978)
  blocking collectives: 70.2 us -> 59 us
  waiting for transfers between devices: 156 us -> 161 us
  local copies, waits for them, and re-layouts: 5.89 us -> 10 us
  starting transfers between devices: 26.9 us -> 23.7 us
    all_to_all x1, waiting for transfers between devices: 102 us -> 24.2 us  [on_device(): recv = lax.all_to_all(send, 'seq', split_axis=0, concat_axis=0, tiled=True)]
    all_gather x1, waiting for transfers between devices: 52.1 us -> 103 us  [on_device(): weights = lax.all_gather(cond_weight[:, 0], 'seq', axis=0)]
    all_to_all x1, waiting for transfers between devices: 0.01 us -> 33.2 us  [on_device(): lax.all_to_all(values, 'seq', split_axis=0, concat_axis=0, tiled=True)]
    all_to_all x1, blocking collectives: 70.2 us -> 59 us  [on_device(): lax.all_to_all(head_out, 'seq', split_axis=0, concat_axis=0, tiled=True)]
    ppermute x2 -> x0, starting transfers between devices: 4.29 us -> none  [the longest x1 2.14 us: gathered_condition(): lax.ppermute(jnp.concatenate([other, table.T], axis=1), 'seq', swap)]
    unnamed x15 -> x7, local copies, waits for them, and re-layouts: 1.78 us -> 6.02 us
    pallas_call x0 -> x2, Pallas kernels: none -> 3.72 us  [the longest x1 2.21 us: pack_slots(): pl.pallas_call(kernel, name='pack_slots', in_specs=[scalars, scalars, sca...]
  transfers between devices with their start and end apart: 6 -> 3, of which waited for: 4 -> 3; matrix products, arithmetic and copies ran while one was open for 2% -> 1% of each run, Pallas kernels for 7% -> 7%
where the time goes in v5:
time: 312 us
  waiting for transfers between devices  161 us (52%)
  blocking collectives  59 us (19%)
  Pallas kernels  40.7 us (13%)
  starting transfers between devices  23.7 us (8%)
  between operations  13.4 us (4%)
  local copies, waits for them, and re-layouts  10 us (3%)
  other arithmetic  4.02 us (1%)
    all_gather x1, waiting for transfers between devices, on_device(): weights = lax.all_gather(cond_weight[:, 0], 'seq', axis=0)  103 us
    all_to_all x1, blocking collectives, on_device(): lax.all_to_all(head_out, 'seq', split_axis=0, concat_axis=0, tiled=True)  59 us
    all_to_all x1, waiting for transfers between devices, on_device(): lax.all_to_all(values, 'seq', split_axis=0, concat_axis=0, tiled=True)  33.2 us
    all_to_all x1, waiting for transfers between devices, on_device(): recv = lax.all_to_all(send, 'seq', split_axis=0, concat_axis=0, tiled=True)  24.2 us
    pallas_call x1, Pallas kernels, attention_probs(): pl.pallas_call(kernel, name='probs', grid=(tokens // tile,), in_specs=[pl...  22.6 us
    all_to_all x1, starting transfers between devices, on_device(): recv = lax.all_to_all(send, 'seq', split_axis=0, concat_axis=0, tiled=True)  16.7 us
    pallas_call x1, Pallas kernels, weigh_values(): pl.pallas_call(kernel, name='weigh', grid=(tokens // tile,), in_specs=[pl...  14.4 us
    all_to_all x1, starting transfers between devices, on_device(): lax.all_to_all(values, 'seq', split_axis=0, concat_axis=0, tiled=True)  6.94 us
  transfers between devices with their start and end apart: 3, of which 3 were waited for; matrix products, arithmetic and copies ran while one was open for 1% of the time, Pallas kernels for 7%

profile of v5, /device:TPU:1, one launch (start us, length us, event | category | flops | bytes accessed | tf_op | source)
XLA Modules:
  0.0 311.6 jit_solution(11123716533631604859)
XLA Ops:
  6.5 1.2 convert_element_type.3.weight_ref
  7.7 2.4 copy_bitcast_fusion.1
  10.1 2.2 pack_slots.1
  12.3 2.8 pad_maximum_fusion
  15.1 16.7 %all-to-all-start = ((bf16[32,336,128]{2,1,0:T(8,128)(2,1)}), bf16[32,336,128]{2,1,0:T(8,128)(2,1)S(1)}, u32[]{:S(2)}, u32[]{:S(2)}) async-start(bf16[32,336,128]{2,1,0:T(8,128)(2,1)} %pad_maximum_fusion), calls=%async_computation | async-start | bytes 5505024 | tf_op jit(solution)/shard_map/all_to_all | solution.py:176
  31.9 0.0 all-gather.3.cloned.1.call-start
  31.9 0.7 all-gather.3.cloned.1.call-update
  32.6 2.6 copy.20
  35.2 102.7 %all-gather.3.cloned.1.call-done = bf16[4096,1,128]{2,0,1:T(8,128)(2,1)} async-done(((bf16[128,1,128]{2,0,1:T(8,128)(2,1)}), bf16[4096,1,128]{2,0,1:T(8,128)(2,1)}) %all-gather.3.cloned.1.call-update) | async-done | bytes 1048592 | tf_op jit(solution)/shard_map/all_gather | solution.py:170
  137.9 24.2 %all-to-all-done.q_ref.k_ref.refs_0_.refs_1_.refs_2_.refs_3_.refs_4_ = bf16[32,336,128]{2,1,0:T(8,128)(2,1)S(1)} async-done(((bf16[32,336,128]{2,1,0:T(8,128)(2,1)}), bf16[32,336,128]{2,1,0:T(8,128)(2,1)S(1)}, u32[]{:S(2)}, u32[]{:S(2)}) %all-to-all-start) | async-done | bytes 2752544 | tf_op jit(solution)/shard_map/all_to_all | solution.py:176
  162.1 0.0 copy-start
  162.1 1.2 copy-done
  163.3 0.0 copy-start.2
  163.3 1.2 copy-done.2
  164.5 1.5 mix.1
  166.0 0.0 copy-start.1
  166.0 1.0 copy-done.1
  167.0 6.9 %all-to-all-start.1 = ((bf16[32,128,128]{2,1,0:T(8,128)(2,1)}), bf16[32,128,128]{2,1,0:T(8,128)(2,1)}, u32[]{:S(2)}, u32[]{:S(2)}) async-start(bf16[32,128,128]{2,1,0:T(8,128)(2,1)} %copy-done.1), calls=%async_computation.1 | async-start | bytes 2097152 | tf_op jit(solution)/shard_map/all_to_all | solution.py:178
  173.9 22.6 %probs.1.p_ref = bf16[4096,4096]{1,0:T(8,128)(2,1)} custom-call(bf16[32,336,128]{2,1,0:T(8,128)(2,1)S(1)} %all-to-all-done.q_ref.k_ref.refs_0_.refs_1_.refs_2_.refs_3_.refs_4_, bf16[32,336,128]{2,1,0:T(8,128)(2,1)S(1)} %all-to-all-done.q_ref.k_ref.refs_0_.refs_1_.refs_2_.refs_3_.refs_4_), custom_call_target="tpu_custom_call" | custom-call | flops 4294967296 | bytes 33554432 | tf_op jit(solution)/shard_map/probs/pallas_call | solution.py:28
  196.6 33.2 %all-to-all-done.1.v_ref = bf16[32,128,128]{2,1,0:T(8,128)(2,1)} async-done(((bf16[32,128,128]{2,1,0:T(8,128)(2,1)}), bf16[32,128,128]{2,1,0:T(8,128)(2,1)}, u32[]{:S(2)}, u32[]{:S(2)}) %all-to-all-start.1) | async-done | bytes 1048608 | tf_op jit(solution)/shard_map/all_to_all | solution.py:178
  229.7 14.4 %weigh.1 = bf16[4096,128]{1,0:T(8,128)(2,1)S(1)} custom-call(bf16[4096,4096]{1,0:T(8,128)(2,1)} %probs.1.p_ref, bf16[32,128,128]{2,1,0:T(8,128)(2,1)} %all-to-all-done.1.v_ref), custom_call_target="tpu_custom_call" | custom-call | tf_op jit(solution)/shard_map/weigh/pallas_call | solution.py:57
  244.1 59.0 %all_to_all.15 = bf16[32,128,128]{2,1,0:T(8,128)(2,1)S(1)} all-to-all(bf16[32,128,128]{2,1,0:T(8,128)(2,1)S(1)} %bitcast.11), channel_id=1, replica_groups=mesh['dp'=16,'seq'=32] {'seq'}, dimensions={0} | all-to-all | bytes 2097152 | tf_op jit(solution)/shard_map/all_to_all | solution.py:182
  303.1 1.6 copy.16
Async XLA Ops:
  15.1 146.9 %all-to-all-start = ((bf16[32,336,128]{2,1,0:T(8,128)(2,1)}), bf16[32,336,128]{2,1,0:T(8,128)(2,1)S(1)}, u32[]{:S(2)}, u32[]{:S(2)}) async-start(bf16[32,336,128]{2,1,0:T(8,128)(2,1)} %pad_maximum_fusion), calls=%async_computation | async-start | bytes 5505024 | tf_op jit(solution)/shard_map/all_to_all | solution.py:176
  31.9 106.0 %all-gather.3.cloned.1.call-start = ((), (), s32[]{:S(2)}) async-start(), calls=%async_computation.3 | async-start | bytes 1081344 | tf_op jit(solution)/shard_map/all_gather | solution.py:170
  162.1 1.2 copy-start
  163.3 1.2 copy-start.2
  166.0 1.0 copy-start.1
  167.0 62.7 %all-to-all-start.1 = ((bf16[32,128,128]{2,1,0:T(8,128)(2,1)}), bf16[32,128,128]{2,1,0:T(8,128)(2,1)}, u32[]{:S(2)}, u32[]{:S(2)}) async-start(bf16[32,128,128]{2,1,0:T(8,128)(2,1)} %copy-done.1), calls=%async_computation.1 | async-start | bytes 2097152 | tf_op jit(solution)/shard_map/all_to_all | solution.py:178
Sparse Core Ops, SparseCore 0:
  34.8 103.0 all-gather.2

commit v6 on v5

--- a/solution.py
+++ b/solution.py
@@ -48,61 +48,100 @@
     peers, rows, hd = values.shape
     tokens = peers * rows
 
-    def kernel(p_ref, v_ref, o_ref):
-        v = v_ref[...].reshape(tokens, hd)
-        o_ref[...] = jnp.dot(p_ref[...], v, preferred_element_type=jnp.float32).astype(
-            jnp.bfloat16
-        )
+    def kernel(p_ref, v_ref, o_ref, acc_ref):
+        step = pl.program_id(0)
+        v = v_ref[...].reshape(tile, hd)
+        part = jnp.dot(p_ref[...], v, preferred_element_type=jnp.float32)
+
+        @pl.when(step == 0)
+        def _():
+            acc_ref[...] = part
+
+        @pl.when((step > 0) & (step < pl.num_programs(0) - 1))
+        def _():
+            acc_ref[...] += part
+
+        @pl.when(step == pl.num_programs(0) - 1)
+        def _():
+            o_ref[...] = (acc_ref[...] + part).astype(jnp.bfloat16)
 
     return pl.pallas_call(
         kernel,
         name="weigh",
         grid=(tokens // tile,),
         in_specs=[
-            pl.BlockSpec((tile, tokens), lambda i: (i, 0)),
-            pl.BlockSpec((peers, rows, hd), lambda i: (0, 0, 0)),
-        ],
-        out_specs=pl.BlockSpec((tile, hd), lambda i: (i, 0)),
+            pl.BlockSpec((tokens, tile), lambda i: (0, i)),
+            pl.BlockSpec((tile // rows, rows, hd), lambda i: (i, 0, 0)),
+        ],
+        out_specs=pl.BlockSpec((tokens, hd), lambda i: (0, 0)),
         out_shape=jax.ShapeDtypeStruct((tokens, hd), jnp.bfloat16),
+        scratch_shapes=[pltpu.VMEM((tokens, hd), jnp.float32)],
         compiler_params=pltpu.CompilerParams(vmem_limit_bytes=24 << 20),
     )(probs, values)
 
 
+def in_hbm(array):
+    return pltpu.with_memory_space_constraint(array, pltpu.HBM)
+
+
 SLOTS = 2
 KEY_ROWS = 16
 
 
-def pack_slots(splats, splat_dest, splat_sub, splat_weight, peers):
+def pack(queries, keys, splats, splat_dest, splat_sub, splat_weight):
+    rows, heads, hd = queries.shape
     count, blk_rows, feats = splats.shape
-    out_rows = SLOTS * blk_rows + KEY_ROWS
-
-    def kernel(dest_ref, sub_ref, weight_ref, splat_ref, out_ref, which):
-        for at in range(peers * SLOTS):
-            which[at] = -1
-        for i in range(count):
-            first = dest_ref[i] * SLOTS
-            which[first + (which[first] >= 0).astype(jnp.int32)] = i
+    head_rows = 2 * rows + SLOTS * blk_rows
+    group = 8
+
+    def kernel(dest_ref, sub_ref, weight_ref, q_ref, k_ref, splat_ref, out_ref, which, table):
+        @pl.when(pl.program_id(0) == 0)
+        def _():
+            for at in range(heads * SLOTS):
+                which[at] = -1
+            for i in range(count):
+                first = dest_ref[i] * SLOTS
+                which[first + (which[first] >= 0).astype(jnp.int32)] = i
+            lane = lax.broadcasted_iota(jnp.int32, (count, feats), 1)
+            sub = jnp.broadcast_to(sub_ref[...], (8, count)).astype(jnp.float32).T[:, :1]
+            weight = jnp.broadcast_to(weight_ref[...].astype(jnp.float32), (8, count)).T[:, :1]
+            table[...] = jnp.where(lane == sub.astype(jnp.int32), weight, 0.0)
+
+        out_ref[:, :rows] = jnp.swapaxes(q_ref[...], 0, 1)
+        out_ref[:, rows : 2 * rows] = jnp.swapaxes(k_ref[...], 0, 1)
         row = lax.broadcasted_iota(jnp.int32, (KEY_ROWS, feats), 0)
-        lane = lax.broadcasted_iota(jnp.int32, (KEY_ROWS, feats), 1)
-        for dest in range(peers):
-            keys = jnp.zeros((KEY_ROWS, feats), jnp.float32)
+        for h in range(group):
+            marks = jnp.zeros((KEY_ROWS, feats), jnp.float32)
             for slot in range(SLOTS):
-                found = which[dest * SLOTS + slot]
+                found = which[(pl.program_id(0) * group + h) * SLOTS + slot]
                 at = jnp.maximum(found, 0)
-                out_ref[dest, slot * blk_rows : (slot + 1) * blk_rows] = splat_ref[at]
-                sub = jnp.where(found >= 0, sub_ref[at], -1)
-                keys = jnp.where((row == slot) & (lane == sub), weight_ref[at], keys)
-            out_ref[dest, SLOTS * blk_rows :] = keys.astype(jnp.bfloat16)
-
-    scalars = pl.BlockSpec(memory_space=pltpu.SMEM)
-    return pl.pallas_call(
-        kernel,
-        name="pack_slots",
-        in_specs=[scalars, scalars, scalars, pl.BlockSpec(memory_space=pltpu.VMEM)],
-        out_specs=pl.BlockSpec(memory_space=pltpu.VMEM),
-        out_shape=jax.ShapeDtypeStruct((peers, out_rows, feats), jnp.bfloat16),
-        scratch_shapes=[pltpu.SMEM((peers * SLOTS,), jnp.int32)],
-    )(splat_dest, splat_sub, splat_weight.astype(jnp.float32), splats)
+                to = 2 * rows + slot * blk_rows
+                out_ref[h, to : to + blk_rows] = splat_ref[at]
+                mark = jnp.broadcast_to(table[pl.ds(at, 1)], (KEY_ROWS, feats))
+                marks = jnp.where((row == slot) & (found >= 0), mark, marks)
+            out_ref[h, head_rows:] = marks.astype(jnp.bfloat16)
+
+    by_head = pl.BlockSpec((rows, group, hd), lambda i: (0, i, 0))
+    return pl.pallas_call(
+        kernel,
+        name="pack",
+        grid=(heads // group,),
+        in_specs=[
+            pl.BlockSpec(memory_space=pltpu.SMEM),
+            pl.BlockSpec((1, count), lambda i: (0, 0)),
+            pl.BlockSpec((1, count), lambda i: (0, 0)),
+            by_head,
+            by_head,
+            pl.BlockSpec((count, blk_rows, feats), lambda i: (0, 0, 0)),
+        ],
+        out_specs=pl.BlockSpec((group, head_rows + KEY_ROWS, hd), lambda i: (i, 0, 0)),
+        out_shape=pltpu.HBM((heads, head_rows + KEY_ROWS, hd), jnp.bfloat16),
+        scratch_shapes=[
+            pltpu.SMEM((heads * SLOTS,), jnp.int32),
+            pltpu.VMEM((count, feats), jnp.float32),
+        ],
+        compiler_params=pltpu.CompilerParams(vmem_limit_bytes=24 << 20),
+    )(splat_dest, *map(in_hbm, (splat_sub[None], splat_weight[None], queries, keys, splats)))
 
 
 def mix_values(recv, first_row, weights, values, own_blocks, blk_rows):
@@ -153,10 +192,10 @@
             pl.BlockSpec((group, rows, hd), lambda i: (i, 0, 0)),
         ],
         out_specs=pl.BlockSpec((group, rows, hd), lambda i: (i, 0, 0)),
-        out_shape=jax.ShapeDtypeStruct((heads, rows, hd), jnp.bfloat16),
+        out_shape=pltpu.HBM((heads, rows, hd), jnp.bfloat16),
         scratch_shapes=[pltpu.VMEM((rows, feats), jnp.bfloat16)],
         compiler_params=pltpu.CompilerParams(vmem_limit_bytes=12 << 20),
-    )(*[recv] * (parts + 1), weights, values)
+    )(*[recv] * (parts + 1), in_hbm(weights), in_hbm(values))
 
 
 def on_device(
@@ -168,16 +207,13 @@
     own_blocks = tok_rows // blk_rows
 
     weights = lax.all_gather(cond_weight[:, 0], "seq", axis=0)
-    slots = pack_slots(splats, splat_dest, splat_sub, splat_weight, peers)
-    send = jnp.concatenate(
-        [queries.transpose(1, 0, 2), attn_keys.transpose(1, 0, 2), slots], axis=1
-    )
+    send = pack(queries, attn_keys, splats, splat_dest, splat_sub, splat_weight)
     values = attn_values.transpose(1, 0, 2)
     recv = lax.all_to_all(send, "seq", split_axis=0, concat_axis=0, tiled=True)
     values = mix_values(recv, 2 * tok_rows, weights, values, own_blocks, blk_rows)
     values = lax.all_to_all(values, "seq", split_axis=0, concat_axis=0, tiled=True)
     probs = attention_probs(recv, tok_rows, 512, 128)
-    head_out = weigh_values(probs, values, 1024)
+    head_out = weigh_values(probs, values, 512)
     head_out = head_out.reshape(peers, tok_rows, head_size)
     arrived = lax.all_to_all(head_out, "seq", split_axis=0, concat_axis=0, tiled=True)
     return arrived.transpose(1, 0, 2)

time: 312 us -> 310 us (level)
  Pallas kernels: 40.7 us -> 47.9 us
  local copies, waits for them, and re-layouts: 10 us -> 4.91 us
  other arithmetic: 4.02 us -> 0 us
where the time goes in v6:
time: 310 us
  waiting for transfers between devices  161 us (52%)
  blocking collectives  59 us (19%)
  Pallas kernels  47.9 us (15%)
  starting transfers between devices  23.7 us (8%)
  between operations  13.4 us (4%)
  local copies, waits for them, and re-layouts  4.91 us (2%)
    all_gather x1, waiting for transfers between devices, on_device(): weights = lax.all_gather(cond_weight[:, 0], 'seq', axis=0)  103 us
    all_to_all x1, blocking collectives, on_device(): lax.all_to_all(head_out, 'seq', split_axis=0, concat_axis=0, tiled=True)  59 us
    all_to_all x1, waiting for transfers between devices, on_device(): lax.all_to_all(values, 'seq', split_axis=0, concat_axis=0, tiled=True)  33.2 us
    all_to_all x1, waiting for transfers between devices, on_device(): recv = lax.all_to_all(send, 'seq', split_axis=0, concat_axis=0, tiled=True)  24.2 us
    pallas_call x1, Pallas kernels, attention_probs(): pl.pallas_call(kernel, name='probs', grid=(tokens // tile,), in_specs=[pl...  22.6 us
    all_to_all x1, starting transfers between devices, on_device(): recv = lax.all_to_all(send, 'seq', split_axis=0, concat_axis=0, tiled=True)  16.7 us
    pallas_call x1, Pallas kernels, weigh_values(): pl.pallas_call(kernel, name='weigh', grid=(tokens // tile,), in_specs=[pl...  16.5 us
    all_to_all x1, starting transfers between devices, on_device(): lax.all_to_all(values, 'seq', split_axis=0, concat_axis=0, tiled=True)  6.94 us
  transfers between devices with their start and end apart: 3, of which 3 were waited for; matrix products, arithmetic and copies ran while one was open for 1% of the time, Pallas kernels for 7%

profile of v6, /device:TPU:1, one launch (start us, length us, event | category | flops | bytes accessed | tf_op | source)
XLA Modules:
  0.0 309.6 jit_solution(9044029660757833255)
XLA Ops:
  6.5 0.0 copy-start
  6.5 0.7 copy-done
  7.2 4.4 %pack.1 = bf16[32,336,128]{2,1,0:T(8,128)(2,1)} custom-call(s32[32]{0:T(128)S(1)} %copy-done, s32[1,32]{1,0:T(1,128)} %bitcast.12, bf16[1,32]{1,0:T(2,128)(2,1)} %bitcast.13, bf16[128,32,128]{2,1,0:T(8,128)(2,1)} %q_ref.1, bf16[128,32,128]{2,1,0:T(8,128)(2,1)} %k_ref.1, bf16[32,32,128]{2,1,0:T(8,128)(2,1)} %splat_ref.1), custom_call_target="tpu_custom_call" | custom-call | tf_op jit(solution)/shard_map/pack/pallas_call | solution.py:125
  11.6 16.7 %all-to-all-start = ((bf16[32,336,128]{2,1,0:T(8,128)(2,1)}), bf16[32,336,128]{2,1,0:T(8,128)(2,1)S(1)}, u32[]{:S(2)}, u32[]{:S(2)}) async-start(bf16[32,336,128]{2,1,0:T(8,128)(2,1)} %pack.1), calls=%async_computation | async-start | bytes 5505024 | tf_op jit(solution)/shard_map/all_to_all | solution.py:212
  28.4 0.0 all-gather.3.cloned.1.call-start
  28.4 0.7 all-gather.3.cloned.1.call-update
  29.1 2.6 copy.14
  31.7 102.7 %all-gather.3.cloned.1.call-done = bf16[4096,1,128]{2,0,1:T(8,128)(2,1)} async-done(((bf16[128,1,128]{2,0,1:T(8,128)(2,1)}), bf16[4096,1,128]{2,0,1:T(8,128)(2,1)}) %all-gather.3.cloned.1.call-update) | async-done | bytes 1048592 | tf_op jit(solution)/shard_map/all_gather | solution.py:209
  134.4 24.2 %all-to-all-done.q_ref.k_ref.refs_0_.refs_1_.refs_2_.refs_3_.refs_4_ = bf16[32,336,128]{2,1,0:T(8,128)(2,1)S(1)} async-done(((bf16[32,336,128]{2,1,0:T(8,128)(2,1)}), bf16[32,336,128]{2,1,0:T(8,128)(2,1)S(1)}, u32[]{:S(2)}, u32[]{:S(2)}) %all-to-all-start) | async-done | bytes 2752544 | tf_op jit(solution)/shard_map/all_to_all | solution.py:212
  158.6 4.4 %mix.1 = bf16[32,128,128]{2,1,0:T(8,128)(2,1)} custom-call(bf16[32,336,128]{2,1,0:T(8,128)(2,1)S(1)} %all-to-all-done.q_ref.k_ref.refs_0_.refs_1_.refs_2_.refs_3_.refs_4_, bf16[32,336,128]{2,1,0:T(8,128)(2,1)S(1)} %all-to-all-done.q_ref.k_ref.refs_0_.refs_1_.refs_2_.refs_3_.refs_4_, ...), custom_call_target="tpu_custom_call" | custom-call | tf_op jit(solution)/shard_map/mix/pallas_call | solution.py:185
  163.0 6.9 %all-to-all-start.1 = ((bf16[32,128,128]{2,1,0:T(8,128)(2,1)}), bf16[32,128,128]{2,1,0:T(8,128)(2,1)}, u32[]{:S(2)}, u32[]{:S(2)}) async-start(bf16[32,128,128]{2,1,0:T(8,128)(2,1)} %mix.1), calls=%async_computation.1 | async-start | bytes 2097152 | tf_op jit(solution)/shard_map/all_to_all | solution.py:214
  169.9 22.6 %probs.1.p_ref = bf16[4096,4096]{1,0:T(8,128)(2,1)} custom-call(bf16[32,336,128]{2,1,0:T(8,128)(2,1)S(1)} %all-to-all-done.q_ref.k_ref.refs_0_.refs_1_.refs_2_.refs_3_.refs_4_, bf16[32,336,128]{2,1,0:T(8,128)(2,1)S(1)} %all-to-all-done.q_ref.k_ref.refs_0_.refs_1_.refs_2_.refs_3_.refs_4_), custom_call_target="tpu_custom_call" | custom-call | flops 4294967296 | bytes 33554432 | tf_op jit(solution)/shard_map/probs/pallas_call | solution.py:28
  192.5 33.2 %all-to-all-done.1.v_ref = bf16[32,128,128]{2,1,0:T(8,128)(2,1)} async-done(((bf16[32,128,128]{2,1,0:T(8,128)(2,1)}), bf16[32,128,128]{2,1,0:T(8,128)(2,1)}, u32[]{:S(2)}, u32[]{:S(2)}) %all-to-all-start.1) | async-done | bytes 1048608 | tf_op jit(solution)/shard_map/all_to_all | solution.py:214
  225.7 16.5 %weigh.1 = bf16[4096,128]{1,0:T(8,128)(2,1)S(1)} custom-call(bf16[4096,4096]{1,0:T(8,128)(2,1)} %probs.1.p_ref, bf16[32,128,128]{2,1,0:T(8,128)(2,1)} %all-to-all-done.1.v_ref), custom_call_target="tpu_custom_call" | custom-call | tf_op jit(solution)/shard_map/weigh/pallas_call | solution.py:68
  242.2 59.0 %all_to_all.15 = bf16[32,128,128]{2,1,0:T(8,128)(2,1)S(1)} all-to-all(bf16[32,128,128]{2,1,0:T(8,128)(2,1)S(1)} %bitcast.8), channel_id=1, replica_groups=mesh['dp'=16,'seq'=32] {'seq'}, dimensions={0} | all-to-all | bytes 2097152 | tf_op jit(solution)/shard_map/all_to_all | solution.py:218
  301.1 1.6 copy.12
Async XLA Ops:
  6.5 0.7 copy-start
  11.6 146.9 %all-to-all-start = ((bf16[32,336,128]{2,1,0:T(8,128)(2,1)}), bf16[32,336,128]{2,1,0:T(8,128)(2,1)S(1)}, u32[]{:S(2)}, u32[]{:S(2)}) async-start(bf16[32,336,128]{2,1,0:T(8,128)(2,1)} %pack.1), calls=%async_computation | async-start | bytes 5505024 | tf_op jit(solution)/shard_map/all_to_all | solution.py:212
  28.4 106.0 %all-gather.3.cloned.1.call-start = ((), (), s32[]{:S(2)}) async-start(), calls=%async_computation.3 | async-start | bytes 1081344 | tf_op jit(solution)/shard_map/all_gather | solution.py:209
  163.0 62.7 %all-to-all-start.1 = ((bf16[32,128,128]{2,1,0:T(8,128)(2,1)}), bf16[32,128,128]{2,1,0:T(8,128)(2,1)}, u32[]{:S(2)}, u32[]{:S(2)}) async-start(bf16[32,128,128]{2,1,0:T(8,128)(2,1)} %mix.1), calls=%async_computation.1 | async-start | bytes 2097152 | tf_op jit(solution)/shard_map/all_to_all | solution.py:214
Sparse Core Ops, SparseCore 0:
  31.3 103.0 all-gather.2

commit v7 on v6

v7 whole, which is shorter than its diff:
```python
import math

import jax
import jax.numpy as jnp
from jax import lax
from jax.experimental import pallas as pl
from jax.experimental.pallas import tpu as pltpu
from jax.sharding import PartitionSpec as P


def attention_probs(recv, rows, tile, sub_rows):
    peers, _, hd = recv.shape
    tokens = peers * rows
    to_exp2 = hd**-0.5 * math.log2(math.e)

    def kernel(q_ref, k_ref, p_ref):
        keys = k_ref[...].reshape(tokens, hd)
        for at in range(tile // sub_rows):
            q = q_ref[(at * sub_rows) // rows, pl.ds((at * sub_rows) % rows, sub_rows)]
            scores = lax.dot_general(
                q, keys, (((1,), (1,)), ((), ())), preferred_element_type=jnp.float32
            )
            top = jnp.max(scores, axis=1, keepdims=True)
            probs = jnp.exp2((scores - top) * to_exp2)
            total = jnp.sum(probs, axis=1, keepdims=True)
            p_ref[pl.ds(at * sub_rows, sub_rows)] = (probs * (1.0 / total)).astype(jnp.bfloat16)

    return pl.pallas_call(
        kernel,
        name="probs",
        grid=(tokens // tile,),
        in_specs=[
            pl.BlockSpec((tile // rows, rows, hd), lambda i: (i, 0, 0)),
            pl.BlockSpec((peers, rows, hd), lambda i: (0, 1, 0)),
        ],
        out_specs=pl.BlockSpec((tile, tokens), lambda i: (i, 0)),
        out_shape=jax.ShapeDtypeStruct((tokens, tokens), jnp.bfloat16),
        cost_estimate=pl.CostEstimate(
            flops=2 * tokens * tokens * hd,
            transcendentals=tokens * tokens,
            bytes_accessed=2 * tokens * tokens,
        ),
        compiler_params=pltpu.CompilerParams(vmem_limit_bytes=24 << 20),
    )(recv, recv)


def weigh_values(probs, values, tile):
    peers, rows, hd = values.shape
    tokens = peers * rows

    def kernel(p_ref, v_ref, o_ref):
        v = v_ref[...].reshape(tokens, hd)
        o_ref[...] = jnp.dot(p_ref[...], v, preferred_element_type=jnp.float32).astype(
            jnp.bfloat16
        )

    return pl.pallas_call(
        kernel,
        name="weigh",
        grid=(tokens // tile,),
        in_specs=[
            pl.BlockSpec((tile, tokens), lambda i: (i, 0)),
            pl.BlockSpec((peers, rows, hd), lambda i: (0, 0, 0)),
        ],
        out_specs=pl.BlockSpec((tile, hd), lambda i: (i, 0)),
        out_shape=jax.ShapeDtypeStruct((tokens, hd), jnp.bfloat16),
        compiler_params=pltpu.CompilerParams(vmem_limit_bytes=24 << 20),
    )(probs, values)


def in_hbm(array):
    return pltpu.with_memory_space_constraint(array, pltpu.HBM)


SLOTS = 2
INFO_ROWS = 8


def splat_info(splat_dest, splat_sub, splat_weight, lanes):
    rows = jnp.stack([splat_dest.astype(jnp.bfloat16), splat_sub.astype(jnp.bfloat16), splat_weight])
    rows = jnp.pad(rows, ((0, INFO_ROWS - 3), (0, 0)))
    return jnp.pad(rows, ((0, 0), (0, lanes - splat_dest.shape[0])), constant_values=-1)


def pack(queries, keys, splats, splat_dest):
    rows, heads, hd = queries.shape
    count, blk_rows, feats = splats.shape
    out_rows = 2 * rows + SLOTS * blk_rows
    group = 8

    def kernel(dest_ref, q_ref, k_ref, splat_ref, out_ref, which):
        @pl.when(pl.program_id(0) == 0)
        def _():
            for at in range(heads * SLOTS):
                which[at] = -1
            for i in range(count):
                first = dest_ref[i] * SLOTS
                which[first + (which[first] >= 0).astype(jnp.int32)] = i

        out_ref[:, :rows] = jnp.swapaxes(q_ref[...], 0, 1)
        out_ref[:, rows : 2 * rows] = jnp.swapaxes(k_ref[...], 0, 1)
        for h in range(group):
            for slot in range(SLOTS):
                at = which[(pl.program_id(0) * group + h) * SLOTS + slot]
                to = 2 * rows + slot * blk_rows
                out_ref[h, to : to + blk_rows] = splat_ref[jnp.maximum(at, 0)]

    by_head = pl.BlockSpec((rows, group, hd), lambda i: (0, i, 0))
    return pl.pallas_call(
        kernel,
        name="pack",
        grid=(heads // group,),
        in_specs=[
            pl.BlockSpec(memory_space=pltpu.SMEM),
            by_head,
            by_head,
            pl.BlockSpec((count, blk_rows, feats), lambda i: (0, 0, 0)),
        ],
        out_specs=pl.BlockSpec((group, out_rows, hd), lambda i: (i, 0, 0)),
        out_shape=pltpu.HBM((heads, out_rows, hd), jnp.bfloat16),
        scratch_shapes=[pltpu.SMEM((heads * SLOTS,), jnp.int32)],
        compiler_params=pltpu.CompilerParams(vmem_limit_bytes=24 << 20),
    )(splat_dest, *map(in_hbm, (queries, keys, splats)))


def mix_values(recv, first_row, gathered, values, own_blocks, blk_rows):
    heads, rows, hd = values.shape
    peers, _, feats = recv.shape
    group = 8
    part = 16
    parts = SLOTS * blk_rows // part
    place = lax.axis_index("seq").astype(jnp.int32)[None]

    def slot_weights(info, own):
        dest, sub, weight = info[:, 0], info[:, 1], info[:, 2]
        mine = (dest == own).astype(jnp.float32)
        lanes = dest.shape[1]
        before = lax.broadcasted_iota(jnp.int32, (lanes, lanes), 0)
        before = (before < lax.broadcasted_iota(jnp.int32, (lanes, lanes), 1)).astype(jnp.float32)
        rank = jnp.dot(mine, before, preferred_element_type=jnp.float32)
        columns = []
        for slot in range(SLOTS):
            chosen = jnp.where((mine > 0) & (rank == slot), weight, 0.0)
            columns.append(
                [
                    jnp.sum(jnp.where(sub == b, chosen, 0.0), axis=1, keepdims=True)
                    for b in range(own_blocks)
                ]
            )
        return columns

    def kernel(place_ref, *refs):
        data_refs, info_ref = refs[:parts], refs[parts]
        w_ref, v_ref, o_ref, cond_ref = refs[parts + 1 :]

        @pl.when(pl.program_id(0) == 0)
        def _():
            own = place_ref[0].astype(jnp.float32)
            columns = slot_weights(info_ref[...].astype(jnp.float32), own)
            for b in range(own_blocks):
                weight = sum(jnp.sum(columns[slot][b], axis=0, keepdims=True) for slot in range(SLOTS))
                denom = jnp.maximum(weight, 1.0)
                for piece in range(0, blk_rows, part):
                    total = jnp.zeros((part, feats), jnp.float32)
                    for slot in range(SLOTS):
                        data_ref = data_refs[(slot * blk_rows + piece) // part]
                        scale = jnp.broadcast_to(columns[slot][b], (peers, feats))
                        data = data_ref[...].astype(jnp.float32) * scale[:, None]
                        total += jnp.sum(data, axis=0)
                    cond_ref[pl.ds(b * blk_rows + piece, part)] = (total / denom).astype(
                        jnp.bfloat16
                    )

        for h in range(group):
            mix = jnp.dot(cond_ref[...], w_ref[h], preferred_element_type=jnp.float32)
            o_ref[h] = (v_ref[h].astype(jnp.float32) + mix).astype(jnp.bfloat16)

    def piece_spec(at):
        return pl.BlockSpec((peers, part, feats), lambda i, p: (0, first_row // part + at, 0))

    return pl.pallas_call(
        kernel,
        name="mix",
        grid_spec=pltpu.PrefetchScalarGridSpec(
            num_scalar_prefetch=1,
            grid=(heads // group,),
            in_specs=[
                *[piece_spec(at) for at in range(parts)],
                pl.BlockSpec((peers, INFO_ROWS, feats), lambda i, p: (0, feats // INFO_ROWS, 0)),
                pl.BlockSpec((group, feats, hd), lambda i, p: (i, 0, 0)),
                pl.BlockSpec((group, rows, hd), lambda i, p: (i, 0, 0)),
            ],
            out_specs=pl.BlockSpec((group, rows, hd), lambda i, p: (i, 0, 0)),
            scratch_shapes=[pltpu.VMEM((rows, feats), jnp.bfloat16)],
        ),
        out_shape=pltpu.HBM((heads, rows, hd), jnp.bfloat16),
        compiler_params=pltpu.CompilerParams(vmem_limit_bytes=24 << 20),
    )(place, *[recv] * parts, *[in_hbm(gathered)] * 2, in_hbm(values))


def on_device(
    queries, attn_keys, attn_values, splats, splat_dest, splat_sub, splat_weight, cond_weight
):
    tok_rows, head_count, head_size = queries.shape
    peers = lax.axis_size("seq")
    _, blk_rows, feats = splats.shape
    own_blocks = tok_rows // blk_rows

    info = splat_info(splat_dest, splat_sub, splat_weight, feats)
    gathered = lax.all_gather(jnp.concatenate([cond_weight[:, 0], info]), "seq", axis=0)
    send = pack(queries, attn_keys, splats, splat_dest)
    values = attn_values.transpose(1, 0, 2)
    recv = lax.all_to_all(send, "seq", split_axis=0, concat_axis=0, tiled=True)
    values = mix_values(
        recv, 2 * tok_rows, gathered, values, own_blocks, blk_rows
    )
    values = lax.all_to_all(values, "seq", split_axis=0, concat_axis=0, tiled=True)
    probs = attention_probs(recv, tok_rows, 512, 128)
    head_out = weigh_values(probs, values, 1024)
    head_out = head_out.reshape(peers, tok_rows, head_size)
    arrived = lax.all_to_all(head_out, "seq", split_axis=0, concat_axis=0, tiled=True)
    return arrived.transpose(1, 0, 2)


def solution(mesh):
    in_specs = (
        P(("dp", "seq"), None, None),
        P(("dp", "seq"), None, None),
        P(("dp", "seq"), None, None),
        P(("dp", "seq"), None, None),
        P(("dp", "seq")),
        P(("dp", "seq")),
        P(("dp", "seq")),
        P(None, "seq", None),
    )
    out_specs = P(("dp", "seq"), None, None)
    return jax.shard_map(
        on_device, mesh=mesh, in_specs=in_specs, out_specs=out_specs, check_vma=False
    )
```

time: 310 us -> 303 us (0.977)
  waiting for transfers between devices: 161 us -> 155 us
    all_to_all x1, waiting for transfers between devices: 24.2 us -> 17.8 us  [on_device(): recv = lax.all_to_all(send, 'seq', split_axis=0, concat_axis=0, tiled=True)]
where the time goes in v7:
time: 303 us; the launch traced here: 302 us
  waiting for transfers between devices  155 us (51%)
  blocking collectives  59 us (19%)
  Pallas kernels  45.8 us (15%)
  starting transfers between devices  23.6 us (8%)
  between operations  13.5 us (4%)
  local copies, waits for them, and re-layouts  4.92 us (2%)
    all_gather x1, waiting for transfers between devices, on_device(): lax.all_gather(jnp.concatenate([cond_weight[:, 0], info]), 'seq', axis=0)  104 us
    all_to_all x1, blocking collectives, on_device(): lax.all_to_all(head_out, 'seq', split_axis=0, concat_axis=0, tiled=True)  59 us
    all_to_all x1, waiting for transfers between devices, on_device(): lax.all_to_all(values, 'seq', split_axis=0, concat_axis=0, tiled=True)  33.2 us
    pallas_call x1, Pallas kernels, attention_probs(): pl.pallas_call(kernel, name='probs', grid=(tokens // tile,), in_specs=[pl...  22.6 us
    all_to_all x1, waiting for transfers between devices, on_device(): recv = lax.all_to_all(send, 'seq', split_axis=0, concat_axis=0, tiled=True)  17.8 us
    all_to_all x1, starting transfers between devices, on_device(): recv = lax.all_to_all(send, 'seq', split_axis=0, concat_axis=0, tiled=True)  16.9 us
    pallas_call x1, Pallas kernels, weigh_values(): pl.pallas_call(kernel, name='weigh', grid=(tokens // tile,), in_specs=[pl...  14.4 us
    all_to_all x1, starting transfers between devices, on_device(): lax.all_to_all(values, 'seq', split_axis=0, concat_axis=0, tiled=True)  6.64 us
  transfers between devices with their start and end apart: 3, of which 3 were waited for; matrix products, arithmetic and copies ran while one was open for 1% of the time, Pallas kernels for 7%

profile of v7, /device:TPU:1, one launch (start us, length us, event | category | flops | bytes accessed | tf_op | source)
XLA Modules:
  0.0 302.4 jit_solution(12539864516475833158)
XLA Ops:
  6.5 0.0 copy-start
  6.5 0.7 copy-done
  7.2 4.3 %pack.1 = bf16[32,320,128]{2,1,0:T(8,128)(2,1)} custom-call(s32[32]{0:T(128)S(1)} %copy-done, bf16[128,32,128]{2,1,0:T(8,128)(2,1)} %q_ref.1, bf16[128,32,128]{2,1,0:T(8,128)(2,1)} %k_ref.1, bf16[32,32,128]{2,1,0:T(8,128)(2,1)} %splat_ref.1), custom_call_target="tpu_custom_call" | custom-call | tf_op jit(solution)/shard_map/pack/pallas_call | solution.py:109
  11.5 0.0 copy-start.1
  11.5 0.0 copy-start.4
  11.5 0.0 copy-start.3
  11.5 0.0 copy-start.2
  11.6 16.9 %all-to-all-start = ((bf16[32,320,128]{2,1,0:T(8,128)(2,1)}), bf16[32,320,128]{2,1,0:T(8,128)(2,1)S(1)}, u32[]{:S(2)}, u32[]{:S(2)}) async-start(bf16[32,320,128]{2,1,0:T(8,128)(2,1)} %pack.1), calls=%async_computation | async-start | bytes 5242880 | tf_op jit(solution)/shard_map/all_to_all | solution.py:213
  28.5 0.0 all-gather.3.cloned.1.call-start
  28.5 0.0 copy-done.1
  28.5 0.0 copy-done.4
  28.5 0.0 copy-done.3
  28.6 0.0 copy-done.2
  28.6 0.6 fusion.1
  29.2 0.0 all-gather.3.cloned.1.call-update
  29.2 2.6 copy.14
  31.8 104.0 %all-gather.3.cloned.1.call-done = bf16[4352,128]{1,0:T(8,128)(2,1)} async-done(((bf16[136,128]{1,0:T(8,128)(2,1)}), bf16[4352,128]{1,0:T(8,128)(2,1)}) %all-gather.3.cloned.1.call-update) | async-done | bytes 1114128 | tf_op jit(solution)/shard_map/all_gather | solution.py:210
  135.9 17.8 %all-to-all-done.q_ref.k_ref.refs_0_.refs_1_.refs_2_.refs_3_ = bf16[32,320,128]{2,1,0:T(8,128)(2,1)S(1)} async-done(((bf16[32,320,128]{2,1,0:T(8,128)(2,1)}), bf16[32,320,128]{2,1,0:T(8,128)(2,1)S(1)}, u32[]{:S(2)}, u32[]{:S(2)}) %all-to-all-start) | async-done | bytes 2621472 | tf_op jit(solution)/shard_map/all_to_all | solution.py:213
  153.7 4.5 %mix.1 = bf16[32,128,128]{2,1,0:T(8,128)(2,1)} custom-call(s32[1]{0:T(128)} %bitcast.place_ref, bf16[32,320,128]{2,1,0:T(8,128)(2,1)S(1)} %all-to-all-done.q_ref.k_ref.refs_0_.refs_1_.refs_2_.refs_3_, bf16[32,320,128]{2,1,0:T(8,128)(2,1)S(1)} %all-to-all-done.q_ref.k_ref.refs_0_.refs_1_.refs_2_.refs_3_, ...), custom_call_target="tpu_custom_call" | custom-call | tf_op jit(solution)/shard_map/mix/pallas_call | solution.py:181
  158.2 6.6 %all-to-all-start.1 = ((bf16[32,128,128]{2,1,0:T(8,128)(2,1)}), bf16[32,128,128]{2,1,0:T(8,128)(2,1)}, u32[]{:S(2)}, u32[]{:S(2)}) async-start(bf16[32,128,128]{2,1,0:T(8,128)(2,1)} %mix.1), calls=%async_computation.1 | async-start | bytes 2097152 | tf_op jit(solution)/shard_map/all_to_all | solution.py:217
  164.8 22.6 %probs.1.p_ref = bf16[4096,4096]{1,0:T(8,128)(2,1)} custom-call(bf16[32,320,128]{2,1,0:T(8,128)(2,1)S(1)} %all-to-all-done.q_ref.k_ref.refs_0_.refs_1_.refs_2_.refs_3_, bf16[32,320,128]{2,1,0:T(8,128)(2,1)S(1)} %all-to-all-done.q_ref.k_ref.refs_0_.refs_1_.refs_2_.refs_3_), custom_call_target="tpu_custom_call" | custom-call | flops 4294967296 | bytes 33554432 | tf_op jit(solution)/shard_map/probs/pallas_call | solution.py:28
  187.4 33.2 %all-to-all-done.1.v_ref = bf16[32,128,128]{2,1,0:T(8,128)(2,1)} async-done(((bf16[32,128,128]{2,1,0:T(8,128)(2,1)}), bf16[32,128,128]{2,1,0:T(8,128)(2,1)}, u32[]{:S(2)}, u32[]{:S(2)}) %all-to-all-start.1) | async-done | bytes 1048608 | tf_op jit(solution)/shard_map/all_to_all | solution.py:217
  220.6 14.4 %weigh.1 = bf16[4096,128]{1,0:T(8,128)(2,1)S(1)} custom-call(bf16[4096,4096]{1,0:T(8,128)(2,1)} %probs.1.p_ref, bf16[32,128,128]{2,1,0:T(8,128)(2,1)} %all-to-all-done.1.v_ref), custom_call_target="tpu_custom_call" | custom-call | tf_op jit(solution)/shard_map/weigh/pallas_call | solution.py:57
  234.9 59.0 %all_to_all.15 = bf16[32,128,128]{2,1,0:T(8,128)(2,1)S(1)} all-to-all(bf16[32,128,128]{2,1,0:T(8,128)(2,1)S(1)} %bitcast.13), channel_id=1, replica_groups=mesh['dp'=16,'seq'=32] {'seq'}, dimensions={0} | all-to-all | bytes 2097152 | tf_op jit(solution)/shard_map/all_to_all | solution.py:221
  293.9 1.6 copy.12
  (3 shorter events, 0.0 us)
Async XLA Ops:
  6.5 0.7 copy-start
  11.5 17.0 %copy-start.1 = (s32[32]{0:T(128)S(1)}, s32[32]{0:T(128)}, u32[]{:S(2)}) copy-start(s32[32]{0:T(128)} %dest_ref.1) | copy-start | bytes 388
  11.5 17.0 %copy-start.4 = (s32[32]{0:T(128)S(1)}, s32[32]{0:T(128)}, u32[]{:S(2)}) copy-start(s32[32]{0:T(128)} %param.13) | copy-start | bytes 388
  11.5 17.0 %copy-start.3 = (bf16[32]{0:T(256)(128)(2,1)S(1)}, bf16[32]{0:T(256)(128)(2,1)}, u32[]{:S(2)}) copy-start(bf16[32]{0:T(256)(128)(2,1)} %param.14) | copy-start | bytes 196
  11.5 17.0 %copy-start.2 = (bf16[128,1,128]{2,0,1:T(8,128)(2,1)S(1)}, bf16[128,1,128]{2,0,1:T(8,128)(2,1)}, u32[]{:S(2)}) copy-start(bf16[128,1,128]{2,0,1:T(8,128)(2,1)} %param.15) | copy-start | bytes 98308
  11.6 142.1 %all-to-all-start = ((bf16[32,320,128]{2,1,0:T(8,128)(2,1)}), bf16[32,320,128]{2,1,0:T(8,128)(2,1)S(1)}, u32[]{:S(2)}, u32[]{:S(2)}) async-start(bf16[32,320,128]{2,1,0:T(8,128)(2,1)} %pack.1), calls=%async_computation | async-start | bytes 5242880 | tf_op jit(solution)/shard_map/all_to_all | solution.py:213
  28.5 107.4 %all-gather.3.cloned.1.call-start = ((), (), s32[]{:S(2)}) async-start(), calls=%async_computation.3 | async-start | bytes 1148928 | tf_op jit(solution)/shard_map/all_gather | solution.py:210
  158.2 62.4 %all-to-all-start.1 = ((bf16[32,128,128]{2,1,0:T(8,128)(2,1)}), bf16[32,128,128]{2,1,0:T(8,128)(2,1)}, u32[]{:S(2)}, u32[]{:S(2)}) async-start(bf16[32,128,128]{2,1,0:T(8,128)(2,1)} %mix.1), calls=%async_computation.1 | async-start | bytes 2097152 | tf_op jit(solution)/shard_map/all_to_all | solution.py:217
Sparse Core Ops, SparseCore 0:
  31.4 104.3 all-gather.2

commit v8 on v7

--- a/solution.py
+++ b/solution.py
@@ -44,27 +44,51 @@
     )(recv, recv)
 
 
-def weigh_values(probs, values, tile):
+def weigh_values(probs, values, tile, width):
     peers, rows, hd = values.shape
     tokens = peers * rows
-
-    def kernel(p_ref, v_ref, o_ref):
-        v = v_ref[...].reshape(tokens, hd)
-        o_ref[...] = jnp.dot(p_ref[...], v, preferred_element_type=jnp.float32).astype(
-            jnp.bfloat16
-        )
+    tiles, pieces = tokens // tile, tokens // width
+
+    def kernel(p_ref, v_ref, o_ref, buffer, sems):
+        def copy(at, piece):
+            return pltpu.make_async_copy(
+                p_ref.at[pl.ds(at * tile, tile), pl.ds(piece * width, width)],
+                buffer.at[at % 2, piece],
+                sems.at[at % 2, piece],
+            )
+
+        for at in range(2):
+            for piece in range(pieces):
+                copy(at, piece).start()
+        for at in range(tiles):
+            total = None
+            for piece in range(pieces):
+                copy(at, piece).wait()
+                v = v_ref[piece * (width // rows) : (piece + 1) * (width // rows)]
+                part = jnp.dot(
+                    buffer[at % 2, piece],
+                    v.reshape(width, hd),
+                    preferred_element_type=jnp.float32,
+                )
+                total = part if total is None else total + part
+                if at + 2 < tiles:
+                    copy(at + 2, piece).start()
+            o_ref[at * tile : (at + 1) * tile] = total.astype(jnp.bfloat16)
 
     return pl.pallas_call(
         kernel,
         name="weigh",
-        grid=(tokens // tile,),
         in_specs=[
-            pl.BlockSpec((tile, tokens), lambda i: (i, 0)),
-            pl.BlockSpec((peers, rows, hd), lambda i: (0, 0, 0)),
-        ],
-        out_specs=pl.BlockSpec((tile, hd), lambda i: (i, 0)),
+            pl.BlockSpec(memory_space=pltpu.HBM),
+            pl.BlockSpec(memory_space=pltpu.VMEM),
+        ],
+        out_specs=pl.BlockSpec(memory_space=pltpu.VMEM),
         out_shape=jax.ShapeDtypeStruct((tokens, hd), jnp.bfloat16),
-        compiler_params=pltpu.CompilerParams(vmem_limit_bytes=24 << 20),
+        scratch_shapes=[
+            pltpu.VMEM((2, pieces, tile, width), jnp.bfloat16),
+            pltpu.SemaphoreType.DMA((2, pieces)),
+        ],
+        compiler_params=pltpu.CompilerParams(vmem_limit_bytes=28 << 20),
     )(probs, values)
 
 
@@ -171,9 +195,11 @@
                         jnp.bfloat16
                     )
 
+        side_by_side = jnp.concatenate([w_ref[h] for h in range(group)], axis=1)
+        mix = jnp.dot(cond_ref[...], side_by_side, preferred_element_type=jnp.float32)
         for h in range(group):
-            mix = jnp.dot(cond_ref[...], w_ref[h], preferred_element_type=jnp.float32)
-            o_ref[h] = (v_ref[h].astype(jnp.float32) + mix).astype(jnp.bfloat16)
+            own_mix = mix[:, h * hd : (h + 1) * hd]
+            o_ref[h] = (v_ref[h].astype(jnp.float32) + own_mix).astype(jnp.bfloat16)
 
     def piece_spec(at):
         return pl.BlockSpec((peers, part, feats), lambda i, p: (0, first_row // part + at, 0))
@@ -216,7 +242,7 @@
     )
     values = lax.all_to_all(values, "seq", split_axis=0, concat_axis=0, tiled=True)
     probs = attention_probs(recv, tok_rows, 512, 128)
-    head_out = weigh_values(probs, values, 1024)
+    head_out = weigh_values(probs, values, 1024, 1024)
     head_out = head_out.reshape(peers, tok_rows, head_size)
     arrived = lax.all_to_all(head_out, "seq", split_axis=0, concat_axis=0, tiled=True)
     return arrived.transpose(1, 0, 2)

time: 303 us -> 311 us (1.026)
  Pallas kernels: 45.8 us -> 53.8 us
    pallas_call x1, Pallas kernels: 14.4 us -> 22.4 us  [weigh_values(): pl.pallas_call(kernel, name='weigh', in_specs=[pl.BlockSpec(memory_space=...]
where the time goes in v8:
time: 311 us; the launch traced here: 310 us
  waiting for transfers between devices  155 us (50%)
  blocking collectives  59 us (19%)
  Pallas kernels  53.8 us (17%)
  starting transfers between devices  23.6 us (8%)
  between operations  13.5 us (4%)
  local copies, waits for them, and re-layouts  4.92 us (2%)
    all_gather x1, waiting for transfers between devices, on_device(): lax.all_gather(jnp.concatenate([cond_weight[:, 0], info]), 'seq', axis=0)  104 us
    all_to_all x1, blocking collectives, on_device(): lax.all_to_all(head_out, 'seq', split_axis=0, concat_axis=0, tiled=True)  59 us
    all_to_all x1, waiting for transfers between devices, on_device(): lax.all_to_all(values, 'seq', split_axis=0, concat_axis=0, tiled=True)  33.2 us
    pallas_call x1, Pallas kernels, attention_probs(): pl.pallas_call(kernel, name='probs', grid=(tokens // tile,), in_specs=[pl...  22.6 us
    pallas_call x1, Pallas kernels, weigh_values(): pl.pallas_call(kernel, name='weigh', in_specs=[pl.BlockSpec(memory_space=...  22.4 us
    all_to_all x1, waiting for transfers between devices, on_device(): recv = lax.all_to_all(send, 'seq', split_axis=0, concat_axis=0, tiled=True)  17.8 us
    all_to_all x1, starting transfers between devices, on_device(): recv = lax.all_to_all(send, 'seq', split_axis=0, concat_axis=0, tiled=True)  16.9 us
    all_to_all x1, starting transfers between devices, on_device(): lax.all_to_all(values, 'seq', split_axis=0, concat_axis=0, tiled=True)  6.65 us
  transfers between devices with their start and end apart: 3, of which 3 were waited for; matrix products, arithmetic and copies ran while one was open for 1% of the time, Pallas kernels for 7%

profile of v8, /device:TPU:1, one launch (start us, length us, event | category | flops | bytes accessed | tf_op | source)
XLA Modules:
  0.0 310.5 jit_solution(7637902490416703714)
XLA Ops:
  6.5 0.0 copy-start
  6.5 0.7 copy-done
  7.2 4.3 %pack.1 = bf16[32,320,128]{2,1,0:T(8,128)(2,1)} custom-call(s32[32]{0:T(128)S(1)} %copy-done, bf16[128,32,128]{2,1,0:T(8,128)(2,1)} %q_ref.1, bf16[128,32,128]{2,1,0:T(8,128)(2,1)} %k_ref.1, bf16[32,32,128]{2,1,0:T(8,128)(2,1)} %splat_ref.1), custom_call_target="tpu_custom_call" | custom-call | tf_op jit(solution)/shard_map/pack/pallas_call | solution.py:133
  11.5 0.0 copy-start.1
  11.5 0.0 copy-start.4
  11.5 0.0 copy-start.3
  11.5 0.0 copy-start.2
  11.6 16.9 %all-to-all-start = ((bf16[32,320,128]{2,1,0:T(8,128)(2,1)}), bf16[32,320,128]{2,1,0:T(8,128)(2,1)S(1)}, u32[]{:S(2)}, u32[]{:S(2)}) async-start(bf16[32,320,128]{2,1,0:T(8,128)(2,1)} %pack.1), calls=%async_computation | async-start | bytes 5242880 | tf_op jit(solution)/shard_map/all_to_all | solution.py:239
  28.5 0.0 all-gather.3.cloned.1.call-start
  28.5 0.0 copy-done.1
  28.5 0.0 copy-done.4
  28.5 0.0 copy-done.3
  28.6 0.0 copy-done.2
  28.6 0.6 fusion.1
  29.2 0.0 all-gather.3.cloned.1.call-update
  29.2 2.6 copy.14
  31.8 104.0 %all-gather.3.cloned.1.call-done = bf16[4352,128]{1,0:T(8,128)(2,1)} async-done(((bf16[136,128]{1,0:T(8,128)(2,1)}), bf16[4352,128]{1,0:T(8,128)(2,1)}) %all-gather.3.cloned.1.call-update) | async-done | bytes 1114128 | tf_op jit(solution)/shard_map/all_gather | solution.py:236
  135.9 17.8 %all-to-all-done.q_ref.k_ref.refs_0_.refs_1_.refs_2_.refs_3_ = bf16[32,320,128]{2,1,0:T(8,128)(2,1)S(1)} async-done(((bf16[32,320,128]{2,1,0:T(8,128)(2,1)}), bf16[32,320,128]{2,1,0:T(8,128)(2,1)S(1)}, u32[]{:S(2)}, u32[]{:S(2)}) %all-to-all-start) | async-done | bytes 2621472 | tf_op jit(solution)/shard_map/all_to_all | solution.py:239
  153.7 4.5 %mix.1 = bf16[32,128,128]{2,1,0:T(8,128)(2,1)} custom-call(s32[1]{0:T(128)} %bitcast.place_ref, bf16[32,320,128]{2,1,0:T(8,128)(2,1)S(1)} %all-to-all-done.q_ref.k_ref.refs_0_.refs_1_.refs_2_.refs_3_, bf16[32,320,128]{2,1,0:T(8,128)(2,1)S(1)} %all-to-all-done.q_ref.k_ref.refs_0_.refs_1_.refs_2_.refs_3_, ...), custom_call_target="tpu_custom_call" | custom-call | tf_op jit(solution)/shard_map/mix/pallas_call | solution.py:207
  158.2 6.7 %all-to-all-start.1 = ((bf16[32,128,128]{2,1,0:T(8,128)(2,1)}), bf16[32,128,128]{2,1,0:T(8,128)(2,1)}, u32[]{:S(2)}, u32[]{:S(2)}) async-start(bf16[32,128,128]{2,1,0:T(8,128)(2,1)} %mix.1), calls=%async_computation.1 | async-start | bytes 2097152 | tf_op jit(solution)/shard_map/all_to_all | solution.py:243
  164.8 22.6 %probs.1.p_ref = bf16[4096,4096]{1,0:T(8,128)(2,1)} custom-call(bf16[32,320,128]{2,1,0:T(8,128)(2,1)S(1)} %all-to-all-done.q_ref.k_ref.refs_0_.refs_1_.refs_2_.refs_3_, bf16[32,320,128]{2,1,0:T(8,128)(2,1)S(1)} %all-to-all-done.q_ref.k_ref.refs_0_.refs_1_.refs_2_.refs_3_), custom_call_target="tpu_custom_call" | custom-call | flops 4294967296 | bytes 33554432 | tf_op jit(solution)/shard_map/probs/pallas_call | solution.py:28
  187.4 33.2 %all-to-all-done.1.v_ref = bf16[32,128,128]{2,1,0:T(8,128)(2,1)} async-done(((bf16[32,128,128]{2,1,0:T(8,128)(2,1)}), bf16[32,128,128]{2,1,0:T(8,128)(2,1)}, u32[]{:S(2)}, u32[]{:S(2)}) %all-to-all-start.1) | async-done | bytes 1048608 | tf_op jit(solution)/shard_map/all_to_all | solution.py:243
  220.6 22.4 %weigh.1 = bf16[4096,128]{1,0:T(8,128)(2,1)S(1)} custom-call(bf16[4096,4096]{1,0:T(8,128)(2,1)} %probs.1.p_ref, bf16[32,128,128]{2,1,0:T(8,128)(2,1)} %all-to-all-done.1.v_ref), custom_call_target="tpu_custom_call" | custom-call | tf_op jit(solution)/shard_map/weigh/pallas_call | solution.py:78
  243.0 59.0 %all_to_all.15 = bf16[32,128,128]{2,1,0:T(8,128)(2,1)S(1)} all-to-all(bf16[32,128,128]{2,1,0:T(8,128)(2,1)S(1)} %bitcast.13), channel_id=1, replica_groups=mesh['dp'=16,'seq'=32] {'seq'}, dimensions={0} | all-to-all | bytes 2097152 | tf_op jit(solution)/shard_map/all_to_all | solution.py:247
  302.0 1.6 copy.12
  (3 shorter events, 0.0 us)
Async XLA Ops:
  6.5 0.7 copy-start
  11.5 17.0 %copy-start.1 = (s32[32]{0:T(128)S(1)}, s32[32]{0:T(128)}, u32[]{:S(2)}) copy-start(s32[32]{0:T(128)} %dest_ref.1) | copy-start | bytes 388
  11.5 17.0 %copy-start.4 = (s32[32]{0:T(128)S(1)}, s32[32]{0:T(128)}, u32[]{:S(2)}) copy-start(s32[32]{0:T(128)} %param.13) | copy-start | bytes 388
  11.5 17.0 %copy-start.3 = (bf16[32]{0:T(256)(128)(2,1)S(1)}, bf16[32]{0:T(256)(128)(2,1)}, u32[]{:S(2)}) copy-start(bf16[32]{0:T(256)(128)(2,1)} %param.14) | copy-start | bytes 196
  11.5 17.0 %copy-start.2 = (bf16[128,1,128]{2,0,1:T(8,128)(2,1)S(1)}, bf16[128,1,128]{2,0,1:T(8,128)(2,1)}, u32[]{:S(2)}) copy-start(bf16[128,1,128]{2,0,1:T(8,128)(2,1)} %param.15) | copy-start | bytes 98308
  11.6 142.1 %all-to-all-start = ((bf16[32,320,128]{2,1,0:T(8,128)(2,1)}), bf16[32,320,128]{2,1,0:T(8,128)(2,1)S(1)}, u32[]{:S(2)}, u32[]{:S(2)}) async-start(bf16[32,320,128]{2,1,0:T(8,128)(2,1)} %pack.1), calls=%async_computation | async-start | bytes 5242880 | tf_op jit(solution)/shard_map/all_to_all | solution.py:239
  28.5 107.4 %all-gather.3.cloned.1.call-start = ((), (), s32[]{:S(2)}) async-start(), calls=%async_computation.3 | async-start | bytes 1148928 | tf_op jit(solution)/shard_map/all_gather | solution.py:236
  158.2 62.4 %all-to-all-start.1 = ((bf16[32,128,128]{2,1,0:T(8,128)(2,1)}), bf16[32,128,128]{2,1,0:T(8,128)(2,1)}, u32[]{:S(2)}, u32[]{:S(2)}) async-start(bf16[32,128,128]{2,1,0:T(8,128)(2,1)} %mix.1), calls=%async_computation.1 | async-start | bytes 2097152 | tf_op jit(solution)/shard_map/all_to_all | solution.py:243
Sparse Core Ops, SparseCore 0:
  31.4 104.3 all-gather.2

commit v9 on v7

--- a/solution.py
+++ b/solution.py
@@ -123,79 +123,95 @@
     )(splat_dest, *map(in_hbm, (queries, keys, splats)))
 
 
+def slot_weights(info, own_blocks):
+    peers, _, lanes = info.shape
+    place = lax.axis_index("seq").astype(jnp.int32)[None]
+
+    def kernel(place_ref, info_ref, scale_ref, denom_ref):
+        rows = info_ref[...].astype(jnp.float32)
+        dest, sub, weight = rows[:, 0], rows[:, 1], rows[:, 2]
+        mine = (dest == place_ref[0].astype(jnp.float32)).astype(jnp.float32)
+        before = lax.broadcasted_iota(jnp.int32, (lanes, lanes), 0)
+        before = (before < lax.broadcasted_iota(jnp.int32, (lanes, lanes), 1)).astype(jnp.float32)
+        rank = jnp.dot(mine, before, preferred_element_type=jnp.float32)
+        for b in range(own_blocks):
+            total = jnp.zeros((1, lanes), jnp.float32)
+            for slot in range(SLOTS):
+                chosen = (mine > 0) & (rank == slot) & (sub == b)
+                column = jnp.sum(jnp.where(chosen, weight, 0.0), axis=1, keepdims=True)
+                scale = jnp.broadcast_to(column, (peers, lanes))
+                scale_ref[slot * own_blocks + b] = scale
+                total += jnp.sum(scale, axis=0, keepdims=True)
+            denom_ref[b] = jnp.broadcast_to(jnp.maximum(total, 1.0), (8, lanes))
+
+    return pl.pallas_call(
+        kernel,
+        name="slot_weights",
+        in_specs=[
+            pl.BlockSpec(memory_space=pltpu.SMEM),
+            pl.BlockSpec(memory_space=pltpu.VMEM),
+        ],
+        out_specs=[pl.BlockSpec(memory_space=pltpu.VMEM)] * 2,
+        out_shape=[
+            pltpu.HBM((SLOTS * own_blocks, peers, lanes), jnp.float32),
+            pltpu.HBM((own_blocks, 8, lanes), jnp.float32),
+        ],
+    )(place, info)
+
+
 def mix_values(recv, first_row, gathered, values, own_blocks, blk_rows):
     heads, rows, hd = values.shape
     peers, _, feats = recv.shape
-    group = 8
+    group = 16
     part = 16
     parts = SLOTS * blk_rows // part
-    place = lax.axis_index("seq").astype(jnp.int32)[None]
-
-    def slot_weights(info, own):
-        dest, sub, weight = info[:, 0], info[:, 1], info[:, 2]
-        mine = (dest == own).astype(jnp.float32)
-        lanes = dest.shape[1]
-        before = lax.broadcasted_iota(jnp.int32, (lanes, lanes), 0)
-        before = (before < lax.broadcasted_iota(jnp.int32, (lanes, lanes), 1)).astype(jnp.float32)
-        rank = jnp.dot(mine, before, preferred_element_type=jnp.float32)
-        columns = []
-        for slot in range(SLOTS):
-            chosen = jnp.where((mine > 0) & (rank == slot), weight, 0.0)
-            columns.append(
-                [
-                    jnp.sum(jnp.where(sub == b, chosen, 0.0), axis=1, keepdims=True)
-                    for b in range(own_blocks)
-                ]
-            )
-        return columns
-
-    def kernel(place_ref, *refs):
-        data_refs, info_ref = refs[:parts], refs[parts]
-        w_ref, v_ref, o_ref, cond_ref = refs[parts + 1 :]
+    scales, denoms = slot_weights(gathered[:, feats:], own_blocks)
+
+    def kernel(*refs):
+        data_refs = refs[:parts]
+        scale_ref, denom_ref, w_ref, v_ref, o_ref, cond_ref = refs[parts:]
 
         @pl.when(pl.program_id(0) == 0)
         def _():
-            own = place_ref[0].astype(jnp.float32)
-            columns = slot_weights(info_ref[...].astype(jnp.float32), own)
-            for b in range(own_blocks):
-                weight = sum(jnp.sum(columns[slot][b], axis=0, keepdims=True) for slot in range(SLOTS))
-                denom = jnp.maximum(weight, 1.0)
-                for piece in range(0, blk_rows, part):
-                    total = jnp.zeros((part, feats), jnp.float32)
-                    for slot in range(SLOTS):
-                        data_ref = data_refs[(slot * blk_rows + piece) // part]
-                        scale = jnp.broadcast_to(columns[slot][b], (peers, feats))
-                        data = data_ref[...].astype(jnp.float32) * scale[:, None]
-                        total += jnp.sum(data, axis=0)
-                    cond_ref[pl.ds(b * blk_rows + piece, part)] = (total / denom).astype(
-                        jnp.bfloat16
-                    )
-
+            for piece in range(0, blk_rows, part):
+                total = [jnp.zeros((part, feats), jnp.float32) for _ in range(own_blocks)]
+                for slot in range(SLOTS):
+                    data_ref = data_refs[(slot * blk_rows + piece) // part]
+                    for src in range(peers):
+                        data = data_ref[src].astype(jnp.float32)
+                        for b in range(own_blocks):
+                            scale = scale_ref[slot * own_blocks + b, pl.ds(src, 1)]
+                            total[b] += data * scale
+                for b in range(own_blocks):
+                    cond_ref[pl.ds(b * blk_rows + piece, part)] = (
+                        total[b] / denom_ref[b, :1]
+                    ).astype(jnp.bfloat16)
+
+        side_by_side = jnp.concatenate([w_ref[h] for h in range(group)], axis=1)
+        mix = jnp.dot(cond_ref[...], side_by_side, preferred_element_type=jnp.float32)
         for h in range(group):
-            mix = jnp.dot(cond_ref[...], w_ref[h], preferred_element_type=jnp.float32)
-            o_ref[h] = (v_ref[h].astype(jnp.float32) + mix).astype(jnp.bfloat16)
+            own_mix = mix[:, h * hd : (h + 1) * hd]
+            o_ref[h] = (v_ref[h].astype(jnp.float32) + own_mix).astype(jnp.bfloat16)
 
     def piece_spec(at):
-        return pl.BlockSpec((peers, part, feats), lambda i, p: (0, first_row // part + at, 0))
+        return pl.BlockSpec((peers, part, feats), lambda i: (0, first_row // part + at, 0))
 
     return pl.pallas_call(
         kernel,
         name="mix",
-        grid_spec=pltpu.PrefetchScalarGridSpec(
-            num_scalar_prefetch=1,
-            grid=(heads // group,),
-            in_specs=[
-                *[piece_spec(at) for at in range(parts)],
-                pl.BlockSpec((peers, INFO_ROWS, feats), lambda i, p: (0, feats // INFO_ROWS, 0)),
-                pl.BlockSpec((group, feats, hd), lambda i, p: (i, 0, 0)),
-                pl.BlockSpec((group, rows, hd), lambda i, p: (i, 0, 0)),
-            ],
-            out_specs=pl.BlockSpec((group, rows, hd), lambda i, p: (i, 0, 0)),
-            scratch_shapes=[pltpu.VMEM((rows, feats), jnp.bfloat16)],
-        ),
+        grid=(heads // group,),
+        in_specs=[
+            *[piece_spec(at) for at in range(parts)],
+            pl.BlockSpec((SLOTS * own_blocks, peers, feats), lambda i: (0, 0, 0)),
+            pl.BlockSpec((own_blocks, 8, feats), lambda i: (0, 0, 0)),
+            pl.BlockSpec((group, feats, hd), lambda i: (i, 0, 0)),
+            pl.BlockSpec((group, rows, hd), lambda i: (i, 0, 0)),
+        ],
+        out_specs=pl.BlockSpec((group, rows, hd), lambda i: (i, 0, 0)),
         out_shape=pltpu.HBM((heads, rows, hd), jnp.bfloat16),
-        compiler_params=pltpu.CompilerParams(vmem_limit_bytes=24 << 20),
-    )(place, *[recv] * parts, *[in_hbm(gathered)] * 2, in_hbm(values))
+        scratch_shapes=[pltpu.VMEM((rows, feats), jnp.bfloat16)],
+        compiler_params=pltpu.CompilerParams(vmem_limit_bytes=24 << 20),
+    )(*[recv] * parts, *map(in_hbm, (scales, denoms, gathered, values)))
 
 
 def on_device(

time: 303 us -> 302 us (level)
    all_to_all x1, waiting for transfers between devices: 17.8 us -> 14.6 us  [on_device(): recv = lax.all_to_all(send, 'seq', split_axis=0, concat_axis=0, tiled=True)]
  transfers between devices with their start and end apart: 3 -> 3, of which waited for: 3 -> 3; matrix products, arithmetic and copies ran while one was open for 1% -> 2% of each run, Pallas kernels for 7% -> 8%
where the time goes in v9:
time: 302 us; the launch traced here: 301 us
  waiting for transfers between devices  152 us (50%)
  blocking collectives  59 us (20%)
  Pallas kernels  46.1 us (15%)
  starting transfers between devices  23.6 us (8%)
  between operations  13.5 us (4%)
  local copies, waits for them, and re-layouts  6.4 us (2%)
    all_gather x1, waiting for transfers between devices, on_device(): lax.all_gather(jnp.concatenate([cond_weight[:, 0], info]), 'seq', axis=0)  104 us
    all_to_all x1, blocking collectives, on_device(): lax.all_to_all(head_out, 'seq', split_axis=0, concat_axis=0, tiled=True)  59 us
    all_to_all x1, waiting for transfers between devices, on_device(): lax.all_to_all(values, 'seq', split_axis=0, concat_axis=0, tiled=True)  33.2 us
    pallas_call x1, Pallas kernels, attention_probs(): pl.pallas_call(kernel, name='probs', grid=(tokens // tile,), in_specs=[pl...  22.6 us
    all_to_all x1, starting transfers between devices, on_device(): recv = lax.all_to_all(send, 'seq', split_axis=0, concat_axis=0, tiled=True)  16.9 us
    all_to_all x1, waiting for transfers between devices, on_device(): recv = lax.all_to_all(send, 'seq', split_axis=0, concat_axis=0, tiled=True)  14.6 us
    pallas_call x1, Pallas kernels, weigh_values(): pl.pallas_call(kernel, name='weigh', grid=(tokens // tile,), in_specs=[pl...  14.4 us
    all_to_all x1, starting transfers between devices, on_device(): lax.all_to_all(values, 'seq', split_axis=0, concat_axis=0, tiled=True)  6.64 us
  transfers between devices with their start and end apart: 3, of which 3 were waited for; matrix products, arithmetic and copies ran while one was open for 2% of the time, Pallas kernels for 8%

profile of v9, /device:TPU:1, one launch (start us, length us, event | category | flops | bytes accessed | tf_op | source)
XLA Modules:
  0.0 301.0 jit_solution(3743444061674180770)
XLA Ops:
  6.5 0.0 copy-start
  6.5 0.7 copy-done
  7.2 4.3 %pack.1 = bf16[32,320,128]{2,1,0:T(8,128)(2,1)} custom-call(s32[32]{0:T(128)S(1)} %copy-done, bf16[128,32,128]{2,1,0:T(8,128)(2,1)} %q_ref.1, bf16[128,32,128]{2,1,0:T(8,128)(2,1)} %k_ref.1, bf16[32,32,128]{2,1,0:T(8,128)(2,1)} %splat_ref.1), custom_call_target="tpu_custom_call" | custom-call | tf_op jit(solution)/shard_map/pack/pallas_call | solution.py:109
  11.5 0.0 copy-start.1
  11.5 0.0 copy-start.4
  11.5 0.0 copy-start.3
  11.6 0.0 copy-start.2
  11.6 16.9 %all-to-all-start = ((bf16[32,320,128]{2,1,0:T(8,128)(2,1)}), bf16[32,320,128]{2,1,0:T(8,128)(2,1)S(1)}, u32[]{:S(2)}, u32[]{:S(2)}) async-start(bf16[32,320,128]{2,1,0:T(8,128)(2,1)} %pack.1), calls=%async_computation | async-start | bytes 5242880 | tf_op jit(solution)/shard_map/all_to_all | solution.py:229
  28.5 0.0 all-gather.3.cloned.1.call-start
  28.5 0.0 copy-done.1
  28.5 0.0 copy-done.4
  28.6 0.0 copy-done.3
  28.6 0.0 copy-done.2
  28.6 0.6 fusion.1
  29.2 0.0 all-gather.3.cloned.1.call-update
  29.2 2.6 copy.14
  31.8 104.0 %all-gather.3.cloned.1.call-done = bf16[4352,128]{1,0:T(8,128)(2,1)} async-done(((bf16[136,128]{1,0:T(8,128)(2,1)}), bf16[4352,128]{1,0:T(8,128)(2,1)}) %all-gather.3.cloned.1.call-update) | async-done | bytes 1114128 | tf_op jit(solution)/shard_map/all_gather | solution.py:226
  135.9 1.5 slice.4.info_ref
  137.4 1.8 slot_weights.1
  139.1 14.6 %all-to-all-done.q_ref.k_ref.refs_0_.refs_1_.refs_2_.refs_3_ = bf16[32,320,128]{2,1,0:T(8,128)(2,1)S(1)} async-done(((bf16[32,320,128]{2,1,0:T(8,128)(2,1)}), bf16[32,320,128]{2,1,0:T(8,128)(2,1)S(1)}, u32[]{:S(2)}, u32[]{:S(2)}) %all-to-all-start) | async-done | bytes 2621472 | tf_op jit(solution)/shard_map/all_to_all | solution.py:229
  153.7 3.0 %mix.1 = bf16[32,128,128]{2,1,0:T(8,128)(2,1)} custom-call(bf16[32,320,128]{2,1,0:T(8,128)(2,1)S(1)} %all-to-all-done.q_ref.k_ref.refs_0_.refs_1_.refs_2_.refs_3_, bf16[32,320,128]{2,1,0:T(8,128)(2,1)S(1)} %all-to-all-done.q_ref.k_ref.refs_0_.refs_1_.refs_2_.refs_3_, bf16[32,320,128]{2,1,0:T(8,128)(2,1)S(1)} %all-to-all-done.q_ref.k_ref.refs_0_.refs_1_.refs_2_.refs_3_, ...), custom_call_target="tpu_custom_call" | custom-call | tf_op jit(solution)/shard_map/mix/pallas_call | solution.py:199
  156.7 6.6 %all-to-all-start.1 = ((bf16[32,128,128]{2,1,0:T(8,128)(2,1)}), bf16[32,128,128]{2,1,0:T(8,128)(2,1)}, u32[]{:S(2)}, u32[]{:S(2)}) async-start(bf16[32,128,128]{2,1,0:T(8,128)(2,1)} %mix.1), calls=%async_computation.1 | async-start | bytes 2097152 | tf_op jit(solution)/shard_map/all_to_all | solution.py:233
  163.4 22.6 %probs.1.p_ref = bf16[4096,4096]{1,0:T(8,128)(2,1)} custom-call(bf16[32,320,128]{2,1,0:T(8,128)(2,1)S(1)} %all-to-all-done.q_ref.k_ref.refs_0_.refs_1_.refs_2_.refs_3_, bf16[32,320,128]{2,1,0:T(8,128)(2,1)S(1)} %all-to-all-done.q_ref.k_ref.refs_0_.refs_1_.refs_2_.refs_3_), custom_call_target="tpu_custom_call" | custom-call | flops 4294967296 | bytes 33554432 | tf_op jit(solution)/shard_map/probs/pallas_call | solution.py:28
  186.0 33.2 %all-to-all-done.1.v_ref = bf16[32,128,128]{2,1,0:T(8,128)(2,1)} async-done(((bf16[32,128,128]{2,1,0:T(8,128)(2,1)}), bf16[32,128,128]{2,1,0:T(8,128)(2,1)}, u32[]{:S(2)}, u32[]{:S(2)}) %all-to-all-start.1) | async-done | bytes 1048608 | tf_op jit(solution)/shard_map/all_to_all | solution.py:233
  219.1 14.4 %weigh.1 = bf16[4096,128]{1,0:T(8,128)(2,1)S(1)} custom-call(bf16[4096,4096]{1,0:T(8,128)(2,1)} %probs.1.p_ref, bf16[32,128,128]{2,1,0:T(8,128)(2,1)} %all-to-all-done.1.v_ref), custom_call_target="tpu_custom_call" | custom-call | tf_op jit(solution)/shard_map/weigh/pallas_call | solution.py:57
  233.5 59.0 %all_to_all.15 = bf16[32,128,128]{2,1,0:T(8,128)(2,1)S(1)} all-to-all(bf16[32,128,128]{2,1,0:T(8,128)(2,1)S(1)} %bitcast.13), channel_id=1, replica_groups=mesh['dp'=16,'seq'=32] {'seq'}, dimensions={0} | all-to-all | bytes 2097152 | tf_op jit(solution)/shard_map/all_to_all | solution.py:237
  292.5 1.6 copy.12
  (3 shorter events, 0.0 us)
Async XLA Ops:
  6.5 0.7 copy-start
  11.5 17.0 %copy-start.1 = (s32[32]{0:T(128)S(1)}, s32[32]{0:T(128)}, u32[]{:S(2)}) copy-start(s32[32]{0:T(128)} %dest_ref.1) | copy-start | bytes 388
  11.5 17.0 %copy-start.4 = (s32[32]{0:T(128)S(1)}, s32[32]{0:T(128)}, u32[]{:S(2)}) copy-start(s32[32]{0:T(128)} %param.13) | copy-start | bytes 388
  11.5 17.0 %copy-start.3 = (bf16[32]{0:T(256)(128)(2,1)S(1)}, bf16[32]{0:T(256)(128)(2,1)}, u32[]{:S(2)}) copy-start(bf16[32]{0:T(256)(128)(2,1)} %param.14) | copy-start | bytes 196
  11.6 17.0 %copy-start.2 = (bf16[128,1,128]{2,0,1:T(8,128)(2,1)S(1)}, bf16[128,1,128]{2,0,1:T(8,128)(2,1)}, u32[]{:S(2)}) copy-start(bf16[128,1,128]{2,0,1:T(8,128)(2,1)} %param.15) | copy-start | bytes 98308
  11.6 142.1 %all-to-all-start = ((bf16[32,320,128]{2,1,0:T(8,128)(2,1)}), bf16[32,320,128]{2,1,0:T(8,128)(2,1)S(1)}, u32[]{:S(2)}, u32[]{:S(2)}) async-start(bf16[32,320,128]{2,1,0:T(8,128)(2,1)} %pack.1), calls=%async_computation | async-start | bytes 5242880 | tf_op jit(solution)/shard_map/all_to_all | solution.py:229
  28.5 107.4 %all-gather.3.cloned.1.call-start = ((), (), s32[]{:S(2)}) async-start(), calls=%async_computation.3 | async-start | bytes 1148928 | tf_op jit(solution)/shard_map/all_gather | solution.py:226
  156.7 62.4 %all-to-all-start.1 = ((bf16[32,128,128]{2,1,0:T(8,128)(2,1)}), bf16[32,128,128]{2,1,0:T(8,128)(2,1)}, u32[]{:S(2)}, u32[]{:S(2)}) async-start(bf16[32,128,128]{2,1,0:T(8,128)(2,1)} %mix.1), calls=%async_computation.1 | async-start | bytes 2097152 | tf_op jit(solution)/shard_map/all_to_all | solution.py:233
Sparse Core Ops, SparseCore 0:
  31.4 104.3 all-gather.2

commit v10 on v9

--- a/solution.py
+++ b/solution.py
@@ -120,7 +120,7 @@
         out_shape=pltpu.HBM((heads, out_rows, hd), jnp.bfloat16),
         scratch_shapes=[pltpu.SMEM((heads * SLOTS,), jnp.int32)],
         compiler_params=pltpu.CompilerParams(vmem_limit_bytes=24 << 20),
-    )(splat_dest, *map(in_hbm, (queries, keys, splats)))
+    )(*map(in_hbm, (splat_dest, queries, keys, splats)))
 
 
 def slot_weights(info, own_blocks):

time: 302 us -> 301 us (level)
  no operation moved by 1% of the time
where the time goes in v10:
time: 301 us; the launch traced here: 300 us
  waiting for transfers between devices  152 us (50%)
  blocking collectives  59 us (20%)
  Pallas kernels  46.1 us (15%)
  starting transfers between devices  23.6 us (8%)
  between operations  13.5 us (4%)
  local copies, waits for them, and re-layouts  5.73 us (2%)
    all_gather x1, waiting for transfers between devices, on_device(): lax.all_gather(jnp.concatenate([cond_weight[:, 0], info]), 'seq', axis=0)  104 us
    all_to_all x1, blocking collectives, on_device(): lax.all_to_all(head_out, 'seq', split_axis=0, concat_axis=0, tiled=True)  59 us
    all_to_all x1, waiting for transfers between devices, on_device(): lax.all_to_all(values, 'seq', split_axis=0, concat_axis=0, tiled=True)  33.2 us
    pallas_call x1, Pallas kernels, attention_probs(): pl.pallas_call(kernel, name='probs', grid=(tokens // tile,), in_specs=[pl...  22.6 us
    all_to_all x1, starting transfers between devices, on_device(): recv = lax.all_to_all(send, 'seq', split_axis=0, concat_axis=0, tiled=True)  16.9 us
    all_to_all x1, waiting for transfers between devices, on_device(): recv = lax.all_to_all(send, 'seq', split_axis=0, concat_axis=0, tiled=True)  14.6 us
    pallas_call x1, Pallas kernels, weigh_values(): pl.pallas_call(kernel, name='weigh', grid=(tokens // tile,), in_specs=[pl...  14.4 us
    all_to_all x1, starting transfers between devices, on_device(): lax.all_to_all(values, 'seq', split_axis=0, concat_axis=0, tiled=True)  6.64 us
  transfers between devices with their start and end apart: 3, of which 3 were waited for; matrix products, arithmetic and copies ran while one was open for 2% of the time, Pallas kernels for 8%

profile of v10, /device:TPU:1, one launch (start us, length us, event | category | flops | bytes accessed | tf_op | source)
XLA Modules:
  0.0 300.3 jit_solution(9931777829451258103)
XLA Ops:
  6.5 4.3 %pack.1 = bf16[32,320,128]{2,1,0:T(8,128)(2,1)} custom-call(s32[32]{0:T(128)} %dest_ref.1, bf16[128,32,128]{2,1,0:T(8,128)(2,1)} %q_ref.1, bf16[128,32,128]{2,1,0:T(8,128)(2,1)} %k_ref.1, bf16[32,32,128]{2,1,0:T(8,128)(2,1)} %splat_ref.1), custom_call_target="tpu_custom_call" | custom-call | tf_op jit(solution)/shard_map/pack/pallas_call | solution.py:109
  10.9 0.0 copy-start.1
  10.9 0.0 copy-start.3
  10.9 0.0 copy-start.2
  10.9 0.0 copy-start
  10.9 16.9 %all-to-all-start = ((bf16[32,320,128]{2,1,0:T(8,128)(2,1)}), bf16[32,320,128]{2,1,0:T(8,128)(2,1)S(1)}, u32[]{:S(2)}, u32[]{:S(2)}) async-start(bf16[32,320,128]{2,1,0:T(8,128)(2,1)} %pack.1), calls=%async_computation | async-start | bytes 5242880 | tf_op jit(solution)/shard_map/all_to_all | solution.py:229
  27.8 0.0 all-gather.3.cloned.1.call-start
  27.8 0.0 copy-done.1
  27.9 0.0 copy-done.3
  27.9 0.0 copy-done.2
  27.9 0.0 copy-done
  27.9 0.6 fusion.1
  28.5 0.0 all-gather.3.cloned.1.call-update
  28.6 2.6 copy.14
  31.2 104.0 %all-gather.3.cloned.1.call-done = bf16[4352,128]{1,0:T(8,128)(2,1)} async-done(((bf16[136,128]{1,0:T(8,128)(2,1)}), bf16[4352,128]{1,0:T(8,128)(2,1)}) %all-gather.3.cloned.1.call-update) | async-done | bytes 1114128 | tf_op jit(solution)/shard_map/all_gather | solution.py:226
  135.2 1.5 slice.4.info_ref
  136.7 1.7 slot_weights.1
  138.4 14.6 %all-to-all-done.q_ref.k_ref.refs_0_.refs_1_.refs_2_.refs_3_ = bf16[32,320,128]{2,1,0:T(8,128)(2,1)S(1)} async-done(((bf16[32,320,128]{2,1,0:T(8,128)(2,1)}), bf16[32,320,128]{2,1,0:T(8,128)(2,1)S(1)}, u32[]{:S(2)}, u32[]{:S(2)}) %all-to-all-start) | async-done | bytes 2621472 | tf_op jit(solution)/shard_map/all_to_all | solution.py:229
  153.0 3.0 %mix.1 = bf16[32,128,128]{2,1,0:T(8,128)(2,1)} custom-call(bf16[32,320,128]{2,1,0:T(8,128)(2,1)S(1)} %all-to-all-done.q_ref.k_ref.refs_0_.refs_1_.refs_2_.refs_3_, bf16[32,320,128]{2,1,0:T(8,128)(2,1)S(1)} %all-to-all-done.q_ref.k_ref.refs_0_.refs_1_.refs_2_.refs_3_, bf16[32,320,128]{2,1,0:T(8,128)(2,1)S(1)} %all-to-all-done.q_ref.k_ref.refs_0_.refs_1_.refs_2_.refs_3_, ...), custom_call_target="tpu_custom_call" | custom-call | tf_op jit(solution)/shard_map/mix/pallas_call | solution.py:199
  156.0 6.6 %all-to-all-start.1 = ((bf16[32,128,128]{2,1,0:T(8,128)(2,1)}), bf16[32,128,128]{2,1,0:T(8,128)(2,1)}, u32[]{:S(2)}, u32[]{:S(2)}) async-start(bf16[32,128,128]{2,1,0:T(8,128)(2,1)} %mix.1), calls=%async_computation.1 | async-start | bytes 2097152 | tf_op jit(solution)/shard_map/all_to_all | solution.py:233
  162.7 22.6 %probs.1.p_ref = bf16[4096,4096]{1,0:T(8,128)(2,1)} custom-call(bf16[32,320,128]{2,1,0:T(8,128)(2,1)S(1)} %all-to-all-done.q_ref.k_ref.refs_0_.refs_1_.refs_2_.refs_3_, bf16[32,320,128]{2,1,0:T(8,128)(2,1)S(1)} %all-to-all-done.q_ref.k_ref.refs_0_.refs_1_.refs_2_.refs_3_), custom_call_target="tpu_custom_call" | custom-call | flops 4294967296 | bytes 33554432 | tf_op jit(solution)/shard_map/probs/pallas_call | solution.py:28
  185.3 33.2 %all-to-all-done.1.v_ref = bf16[32,128,128]{2,1,0:T(8,128)(2,1)} async-done(((bf16[32,128,128]{2,1,0:T(8,128)(2,1)}), bf16[32,128,128]{2,1,0:T(8,128)(2,1)}, u32[]{:S(2)}, u32[]{:S(2)}) %all-to-all-start.1) | async-done | bytes 1048608 | tf_op jit(solution)/shard_map/all_to_all | solution.py:233
  218.4 14.4 %weigh.1 = bf16[4096,128]{1,0:T(8,128)(2,1)S(1)} custom-call(bf16[4096,4096]{1,0:T(8,128)(2,1)} %probs.1.p_ref, bf16[32,128,128]{2,1,0:T(8,128)(2,1)} %all-to-all-done.1.v_ref), custom_call_target="tpu_custom_call" | custom-call | tf_op jit(solution)/shard_map/weigh/pallas_call | solution.py:57
  232.8 59.0 %all_to_all.15 = bf16[32,128,128]{2,1,0:T(8,128)(2,1)S(1)} all-to-all(bf16[32,128,128]{2,1,0:T(8,128)(2,1)S(1)} %bitcast.13), channel_id=1, replica_groups=mesh['dp'=16,'seq'=32] {'seq'}, dimensions={0} | all-to-all | bytes 2097152 | tf_op jit(solution)/shard_map/all_to_all | solution.py:237
  291.8 1.6 copy.12
  (3 shorter events, 0.0 us)
Async XLA Ops:
  10.9 17.0 %copy-start.1 = (s32[32]{0:T(128)S(1)}, s32[32]{0:T(128)}, u32[]{:S(2)}) copy-start(s32[32]{0:T(128)} %dest_ref.1) | copy-start | bytes 388
  10.9 17.0 %copy-start.3 = (s32[32]{0:T(128)S(1)}, s32[32]{0:T(128)}, u32[]{:S(2)}) copy-start(s32[32]{0:T(128)} %param.13) | copy-start | bytes 388
  10.9 17.0 %copy-start.2 = (bf16[32]{0:T(256)(128)(2,1)S(1)}, bf16[32]{0:T(256)(128)(2,1)}, u32[]{:S(2)}) copy-start(bf16[32]{0:T(256)(128)(2,1)} %param.14) | copy-start | bytes 196
  10.9 17.0 %copy-start = (bf16[128,1,128]{2,0,1:T(8,128)(2,1)S(1)}, bf16[128,1,128]{2,0,1:T(8,128)(2,1)}, u32[]{:S(2)}) copy-start(bf16[128,1,128]{2,0,1:T(8,128)(2,1)} %param.15) | copy-start | bytes 98308
  10.9 142.1 %all-to-all-start = ((bf16[32,320,128]{2,1,0:T(8,128)(2,1)}), bf16[32,320,128]{2,1,0:T(8,128)(2,1)S(1)}, u32[]{:S(2)}, u32[]{:S(2)}) async-start(bf16[32,320,128]{2,1,0:T(8,128)(2,1)} %pack.1), calls=%async_computation | async-start | bytes 5242880 | tf_op jit(solution)/shard_map/all_to_all | solution.py:229
  27.8 107.4 %all-gather.3.cloned.1.call-start = ((), (), s32[]{:S(2)}) async-start(), calls=%async_computation.3 | async-start | bytes 1148928 | tf_op jit(solution)/shard_map/all_gather | solution.py:226
  156.0 62.4 %all-to-all-start.1 = ((bf16[32,128,128]{2,1,0:T(8,128)(2,1)}), bf16[32,128,128]{2,1,0:T(8,128)(2,1)}, u32[]{:S(2)}, u32[]{:S(2)}) async-start(bf16[32,128,128]{2,1,0:T(8,128)(2,1)} %mix.1), calls=%async_computation.1 | async-start | bytes 2097152 | tf_op jit(solution)/shard_map/all_to_all | solution.py:233
Sparse Core Ops, SparseCore 0:
  30.8 104.3 all-gather.2
